TPU v7x, 256 devices: a whole 4x4x8 slice. The times are simulated.
256 devices in a mesh: row: 2 (over y_hi), col: 4 (over x), frame: 32 (over z, y_lo, core).
Axes of the slice: x: 4, y: 4 (y_hi: 2, y_lo: 2; y = y_hi * 2 + y_lo), z: 8, core: 2. Of those that a mesh axis runs over, the one named last changes fastest.
Arguments:
- video: float32 [128, 576, 1024], P('frame', 'row', 'col'), may hold values from -60 to 60
- multiplier: float32 [128, 576, 1024], P('frame', 'row', 'col'), may hold values from -3 to 3
- foreground: float32 [128, 576, 1024], P('frame', 'row', 'col'), may hold values from -6 to 6
- basis: float32 [16, 576, 1024], P(None, 'row', 'col'), may hold values from -40 to 40
- coefficients: float32 [128, 16], P('frame'), may hold values from -10 to 10
Outputs:
- new_foreground: float32 [128, 576, 1024], P('frame', 'row', 'col')
- new_coefficients: float32 [128, 16], P('frame')
- new_basis: float32 [16, 576, 1024], P(None, ('row', 'frame'), 'col')
All inputs are finite; a program needn't handle non-finite values.
Results may differ from a plain program's by a relative error of at most 0.0003.
Values sent between devices are 32-bit elements; how exact they have to be, the bound alone decides.
No kernel may reach another device: no remote copies, remote signals or barrier semaphores. Data moves between devices by JAX's collectives and lax.ppermute only.
A program may use at most 128 MiB of HBM per device.

v0:
```python
import jax
import jax.numpy as jnp
from jax import lax
from jax.sharding import PartitionSpec as P

PASSES = 3


relax_rate = 0.8
smooth_weight = 0.5
smooth_floor = 0.25
shrink_level = 0.4
dual_scale = 0.8
ridge_share = 0.1


def with_halo(block, sides, width):
    for axis, dim in sides:
        count = lax.axis_size(axis)
        forward = [(i, i + 1) for i in range(count - 1)]
        backward = [(target, source) for source, target in forward]
        low = lax.ppermute(
            lax.slice_in_dim(block, block.shape[dim] - width, None, axis=dim), axis, forward
        )
        high = lax.ppermute(lax.slice_in_dim(block, 0, width, axis=dim), axis, backward)
        block = jnp.concatenate([low, block, high], axis=dim)
    return block


def from_everyone(value, axis):
    peers = lax.axis_size(axis)
    return lax.all_to_all(
        jnp.broadcast_to(value[None], (peers, *value.shape)), axis, 0, 0, tiled=True
    )


def over_copies(value, axis):
    return from_everyone(value, axis).sum(axis=0)


def in_one(arrays, axis):
    line, at, done = (jnp.concatenate([a.reshape(-1) for a in arrays]), 0, [])
    running = over_copies(line, axis)
    for a in arrays:
        done.append(running[at : at + a.size].reshape(a.shape))
        at += a.size
    return tuple(done)


def forward_cells(padded, direction, shape):
    starts = [0, 0, 0]
    starts[direction] = 1
    limits = [starts[axis_dim] + shape[axis_dim] for axis_dim in range(3)]
    return lax.slice(padded, starts, limits)


def descend(padded, source, anchor, extent):
    shape = tuple((int(length) - 1 for length in padded.shape))
    here_cells = padded[:-1, :-1, :-1]
    slopes = []
    for direction in range(3):
        ahead_cells = forward_cells(padded, direction, shape)
        places = anchor[direction] + jnp.arange(shape[direction], dtype=jnp.int32)
        inside = (places >= 0) & (places < extent[direction] - 1)
        layout = [1, 1, 1]
        layout[direction] = shape[direction]
        inside = inside.reshape(layout)
        slopes.append(jnp.where(inside, ahead_cells - here_cells, jnp.zeros_like(here_cells)))
    weight = lax.rsqrt(
        smooth_floor + slopes[0] * slopes[0] + slopes[1] * slopes[1] + slopes[2] * slopes[2]
    )
    fluxes = [slope_part * weight for slope_part in slopes]
    spread = (
        fluxes[0][1:, 1:, 1:]
        - fluxes[0][:-1, 1:, 1:]
        + (fluxes[1][1:, 1:, 1:] - fluxes[1][1:, :-1, 1:])
        + (fluxes[2][1:, 1:, 1:] - fluxes[2][1:, 1:, :-1])
    )
    center = padded[1:-1, 1:-1, 1:-1]
    return center + relax_rate * (source - center + smooth_weight * spread)


def solve_definite(matrix, right_side):
    factor_lower = jnp.linalg.cholesky(matrix)
    half_solved = lax.linalg.triangular_solve(factor_lower, right_side, left_side=True, lower=True)
    return lax.linalg.triangular_solve(
        factor_lower, half_solved, left_side=True, lower=True, transpose_a=True
    )


def local(video, multiplier, foreground, basis, coefficients):
    highest = lax.Precision.HIGHEST
    frames_here, rows_here, cols_here = video.shape
    rank_size = basis.shape[0]
    frame_count = lax.axis_size("frame")
    row_count = lax.axis_size("row")
    col_count = lax.axis_size("col")
    extent = (frames_here * frame_count, rows_here * row_count, cols_here * col_count)
    frame_slot = lax.axis_index("frame")
    corner = (
        frame_slot * frames_here,
        lax.axis_index("row") * rows_here,
        lax.axis_index("col") * cols_here,
    )
    pixels = rows_here * cols_here
    flat_basis = basis.reshape(rank_size, pixels)
    background = jnp.dot(coefficients, flat_basis, precision=highest).reshape(video.shape)
    target = video - background + dual_scale * multiplier
    current = foreground
    for sweep in range(PASSES):
        padded = with_halo(current, (("row", 1), ("col", 2), ("frame", 0)), 1)
        current = descend(padded, target, tuple((start_cell - 1 for start_cell in corner)), extent)
    shrunk = current - jnp.clip(current, -shrink_level, shrink_level)
    residual_target = video + dual_scale * multiplier - shrunk
    flat_target = residual_target.reshape(frames_here, pixels)
    gram_part = jnp.dot(flat_basis, flat_basis.T, precision=highest)
    cross_part = jnp.dot(flat_basis, flat_target.T, precision=highest)
    gram_sum, cross_sum = in_one((gram_part, cross_part), ("row", "col"))
    identity_matrix = jnp.eye(rank_size, dtype=gram_sum.dtype)
    pixel_ridge = ridge_share * pixels * row_count * col_count
    coeff_rows = solve_definite(
        gram_sum + pixel_ridge * identity_matrix, cross_sum + pixel_ridge * coefficients.T
    )
    total_part = jnp.dot(coeff_rows, flat_target, precision=highest).reshape(
        rank_size, rows_here, cols_here
    )
    frame_gram_part = jnp.dot(coeff_rows, coeff_rows.T, precision=highest)
    owned_rows = rows_here // frame_count
    owned_sums = lax.psum_scatter(total_part, "frame", scatter_dimension=1, tiled=True)
    frame_gram = over_copies(frame_gram_part, "frame")
    old_owned = lax.dynamic_slice_in_dim(basis, frame_slot * owned_rows, owned_rows, 1)
    frame_ridge = ridge_share * frames_here * frame_count
    right_side = (owned_sums + frame_ridge * old_owned).reshape(rank_size, owned_rows * cols_here)
    new_basis = solve_definite(frame_gram + frame_ridge * identity_matrix, right_side)
    return (shrunk, coeff_rows.T, new_basis.reshape(rank_size, owned_rows, cols_here))


def solution(mesh):
    placed = (
        P("frame", "row", "col"),
        P("frame", "row", "col"),
        P("frame", "row", "col"),
        P(None, "row", "col"),
        P("frame", None),
    )
    return jax.shard_map(
        local,
        mesh=mesh,
        in_specs=placed,
        out_specs=(P("frame", "row", "col"), P("frame", None), P(None, ("row", "frame"), "col")),
        check_vma=False,
    )
```

profile of v0, /device:TPU:2, one launch (start us, length us, event | category | flops | bytes accessed | tf_op | source)
XLA Modules:
  0.0 356.5 jit_solution(8225191443156521703)
XLA Ops:
  8.0 5.1 %collective-permute-start = (f32[4,1,256]{2,0,1:T(4,128)S(1)}, f32[4,1,256]{2,0,1:T(4,128)S(1)}, u32[]{:S(2)}, u32[]{:S(2)}) collective-permute-start(f32[4,1,256]{2,0,1:T(4,128)S(1)} %copy.235), channel_id=1, source_target_pairs={{0,128},{1,129},{2,130},{3,131},{4,132},{5,133},{6,134},{7,135},{8... | collective-permute-start | bytes 12296 | tf_op jit(solution)/shard_map/ppermute | solution.py:22
  16.5 3.6 %collective-permute-done.1 = f32[4,1,256]{2,0,1:T(4,128)S(1)} collective-permute-done((f32[4,1,256]{2,0,1:T(4,128)S(1)}, f32[4,1,256]{2,0,1:T(4,128)S(1)}, u32[]{:S(2)}, u32[]{:S(2)}) %collective-permute-start.1) | collective-permute-done | bytes 4128 | tf_op jit(solution)/shard_map/ppermute | solution.py:25
  20.8 3.4 collective-permute-start.2
  30.4 3.2 pad_maximum_fusion.27
  39.6 4.6 %fusion.78 = (f32[5,289,257]{2,0,1:T(8,128)}, f32[5,289,257]{2,0,1:T(8,128)S(1)}) fusion(f32[5,290,258]{2,0,1:T(8,128)S(1)} %maximum_maximum_fusion, f32[1,290,258]{2,0,1:T(1,128)S(1)} %collective-permute-done.4, f32[4,290,1]{2,0,1:T(4,128)S(1)} %copy.165, f32[4,290,256]{2,0,1:T(4,128)S(1)} %constant_dynamic-update-slice_fusion, ...), kind=kLoop, calls=%fused_computation.147 | loop fusion | flops 5941840 | bytes 8924251 | tf_op jit(solution)/shard_map/mul | solution.py:72
  46.5 13.0 %fusion.37 = (f32[4,288,256]{2,0,1:T(4,128)S(1)}, f32[4,288,256]{2,0,1:T(4,128)}) fusion(f32[5,289,257]{2,0,1:T(8,128)S(1)} %get-tuple-element.33, f32[5,289,257]{2,0,1:T(8,128)S(1)} %get-tuple-element.32, f32[5,289,257]{2,0,1:T(8,128)} %get-tuple-element.26, f32[4,288,256]{2,1,0:T(8,128)S(1)} %copy-done.7, f32[4,288,256]{2,1,0:T(8,128)S(1)} %copy-done, ...), kind=kOutput, calls=%fused_computation.68 | convolution fusion | flops 60456960 | bytes 17694976 | tf_op jit(solution)/shard_map/dot_general | solution.py:107
  63.9 5.7 %collective-permute-done.7 = f32[4,1,256]{2,0,1:T(4,128)S(1)} collective-permute-done((f32[4,1,256]{2,0,1:T(4,128)S(1)}, f32[4,1,256]{2,0,1:T(4,128)S(1)}, u32[]{:S(2)}, u32[]{:S(2)}) %collective-permute-start.7) | collective-permute-done | bytes 4128 | tf_op jit(solution)/shard_map/ppermute | solution.py:25
  81.1 5.3 %pad_maximum_fusion.24 = (f32[1,290,258]{2,0,1:T(1,128)S(1)}, f32[1,290,258]{2,0,1:T(1,128)S(1)}) fusion(f32[4,290,1]{2,0,1:T(4,128)S(1)} %copy.170, f32[4,290,1]{2,0,1:T(4,128)S(1)} %copy.169, f32[4,1,256]{2,0,1:T(4,128)S(1)} %collective-permute-done.7, f32[4,288,256]{2,0,1:T(4,128)S(1)} %get-tuple-element.52, f32[4,1,256]{2,0,1:T(4,128)S(1)} %collective-permute-done.6), kind=kLoop, calls=%fused_computation.90 | loop fusion | flops 598560 | bytes 1795680 | tf_op jit(solution)/shard_map/slice | solution.py:25
  86.4 5.5 %collective-permute-start.11 = (f32[1,290,258]{2,0,1:T(1,128)S(1)}, f32[1,290,258]{2,0,1:T(1,128)S(1)}, u32[]{:S(2)}, u32[]{:S(2)}) collective-permute-start(f32[1,290,258]{2,0,1:T(1,128)S(1)} %get-tuple-element.37), channel_id=1, source_target_pairs={{0,1},{1,2},{2,3},{3,4},{4,5},{5,6},{6,7},{7,8},{8,9},{9,10},{10,1... | collective-permute-start | bytes 897848 | tf_op jit(solution)/shard_map/ppermute | solution.py:22
  97.2 4.5 %fusion.79 = (f32[5,289,257]{2,0,1:T(8,128)S(1)}, f32[5,289,257]{2,0,1:T(8,128)S(1)}) fusion(f32[5,290,258]{2,0,1:T(8,128)S(1)} %maximum_maximum_fusion.1, f32[1,290,258]{2,0,1:T(1,128)S(1)} %collective-permute-done.10, f32[4,290,1]{2,0,1:T(4,128)S(1)} %copy.170, f32[4,1,256]{2,0,1:T(4,128)S(1)} %collective-permute-done.7, ...), kind=kLoop, calls=%fused_computation.148 | loop fusion | flops 6684570 | bytes 8924251 | tf_op jit(solution)/shard_map/mul | solution.py:72
  103.9 3.3 fusion.31
  110.8 5.7 %collective-permute-done.13 = f32[4,1,256]{2,0,1:T(4,128)S(1)} collective-permute-done((f32[4,1,256]{2,0,1:T(4,128)S(1)}, f32[4,1,256]{2,0,1:T(4,128)S(1)}, u32[]{:S(2)}, u32[]{:S(2)}) %collective-permute-start.13) | collective-permute-done | bytes 4128 | tf_op jit(solution)/shard_map/ppermute | solution.py:25
  121.5 3.9 %collective-permute-start.15 = (f32[4,290,1]{1,0,2:T(4,128)S(1)}, f32[4,290,1]{1,0,2:T(4,128)S(1)}, u32[]{:S(2)}, u32[]{:S(2)}) collective-permute-start(f32[4,290,1]{1,0,2:T(4,128)S(1)} %copy.172), channel_id=1, source_target_pairs={{32,0},{64,32},{96,64},{33,1},{65,33},{97,65},{34,2},{66,34},{98,6... | collective-permute-start | bytes 13928 | tf_op jit(solution)/shard_map/ppermute | solution.py:25
  128.2 7.5 %pad_maximum_fusion.19 = (f32[1,290,258]{2,0,1:T(1,128)}, f32[1,290,258]{2,0,1:T(1,128)}) fusion(f32[4,290,1]{2,0,1:T(4,128)} %copy.174, f32[4,290,1]{2,0,1:T(4,128)S(1)} %copy.173, f32[4,1,256]{2,0,1:T(4,128)S(1)} %collective-permute-done.13, f32[4,288,256]{2,0,1:T(4,128)S(1)} %fusion.31, f32[4,1,256]{2,0,1:T(4,128)S(1)} %collective-permute-done.12), kind=kLoop, calls=%fused_computation.85 | loop fusion | flops 598560 | bytes 1795680 | tf_op jit(solution)/shard_map/slice | solution.py:25
  135.6 5.8 %collective-permute-start.17 = (f32[1,290,258]{2,0,1:T(1,128)}, f32[1,290,258]{2,0,1:T(1,128)S(1)}, u32[]{:S(2)}, u32[]{:S(2)}) collective-permute-start(f32[1,290,258]{2,0,1:T(1,128)} %get-tuple-element.35), channel_id=1, source_target_pairs={{0,1},{1,2},{2,3},{3,4},{4,5},{5,6},{6,7},{7,8},{8,9},{9,10},{10,1... | collective-permute-start | bytes 897848 | tf_op jit(solution)/shard_map/ppermute | solution.py:22
  143.2 14.2 %convolution_bitcast_fusion = f32[16,16]{1,0:T(8,128)S(1)} fusion(f32[16,288,256]{2,1,0:T(8,128)} %param.9), kind=kOutput, calls=%fused_computation.76 | convolution fusion | flops 226492416 | bytes 4719616 | tf_op jit(solution)/shard_map/dot_general | solution.py:116
  160.2 5.8 %fusion.80 = (f32[5,289,257]{2,0,1:T(8,128)S(1)}, f32[5,289,257]{2,0,1:T(8,128)S(1)}) fusion(f32[5,290,258]{2,0,1:T(8,128)S(1)} %maximum_maximum_fusion.2, f32[1,290,258]{2,0,1:T(1,128)} %collective-permute-done.16, f32[4,290,1]{2,0,1:T(4,128)S(1)} %copy-done.6, f32[4,1,256]{2,0,1:T(4,128)S(1)} %collective-permute-done.13, f32[4,288,256]{2,0,1:T(4,128)S(1)} %fusion.31, ...), kind=kLoop, calls=%fused_computation.149 | loop fusion | flops 6684570 | bytes 8924251 | tf_op jit(solution)/shard_map/mul | solution.py:72
  168.3 3.4 clamp_subtract_fusion
  171.8 9.6 %convolution_bitcast_fusion.1 = f32[16,4]{0,1:T(4,128)S(1)} fusion(f32[16,288,256]{2,1,0:T(8,128)S(1)} %bitcast.90, f32[4,288,256]{2,0,1:T(4,128)S(1)} %clamp_subtract_fusion, f32[4,288,256]{2,1,0:T(8,128)S(1)} %copy-done.2, f32[4,288,256]{2,1,0:T(8,128)S(1)} %copy-done), kind=kOutput, calls=%fused_computation.77 | convolution fusion | flops 57507840 | bytes 8257792 | tf_op jit(solution)/shard_map/dot_general | solution.py:117
  181.6 10.6 %all_to_all.11 = f32[8,1,320]{2,1,0:T(1,128)S(1)} all-to-all(f32[8,1,320]{2,1,0:T(1,128)S(1)} %broadcast_in_dim.58), channel_id=1, replica_groups=mesh['row'=2,'col'=4,'frame'=32] {'row','col'}, dimensions={0} | all-to-all | bytes 20480 | tf_op jit(solution)/shard_map/all_to_all | solution.py:32
  204.0 6.6 %fusion.39 = f32[16,288,256]{2,0,1:T(8,128)} fusion(f32[16,4]{0,1:T(4,128)S(1)} %fusion.56, f32[4,288,256]{2,0,1:T(4,128)S(1)} %clamp_subtract_fusion, f32[4,288,256]{2,1,0:T(8,128)S(1)} %copy-done.3, f32[4,288,256]{2,1,0:T(8,128)S(1)} %copy-done), kind=kOutput, calls=%fused_computation.72 | convolution fusion | flops 57507840 | bytes 8257792 | tf_op jit(solution)/shard_map/dot_general | solution.py:124
  211.6 21.7 %all-to-all-start.1 = ((f32[32,1,256]{2,1,0:T(1,128)}), f32[32,1,256]{2,1,0:T(1,128)S(1)}, u32[]{:S(2)}, u32[]{:S(2)}) async-start(f32[32,1,256]{2,1,0:T(1,128)} %reshape.115), calls=%async_computation.1 | async-start | bytes 65536 | tf_op jit(solution)/shard_map/all_to_all | solution.py:32
  233.3 7.3 %copy.175 = f32[16,288,256]{2,0,1:T(8,128)} copy(f32[16,288,256]{2,1,0:T(8,128)} %param.9) | data formatting | bytes 9437184 | tf_op args[3]
  247.5 99.7 %reduce-scatter.2.cloned.1.call-done = f32[16,9,256]{2,0,1:T(8,128)} async-done(((f32[16,288,256]{2,0,1:T(8,128)}), f32[16,9,256]{2,0,1:T(8,128)}) %reduce-scatter.2.cloned.1.call-update) | async-done | bytes 147472 | tf_op jit(solution)/shard_map/reduce_scatter | solution.py:129
  (154 shorter events, 82.3 us)
Async XLA Ops:
  7.2 340.0 %reduce-scatter.2.cloned.1.call-start = ((), (), s32[]{:S(2)}) async-start(), calls=%async_computation.3 | async-start | bytes 4866048 | tf_op jit(solution)/shard_map/reduce_scatter | solution.py:129
  8.0 6.4 %collective-permute-start = (f32[4,1,256]{2,0,1:T(4,128)S(1)}, f32[4,1,256]{2,0,1:T(4,128)S(1)}, u32[]{:S(2)}, u32[]{:S(2)}) collective-permute-start(f32[4,1,256]{2,0,1:T(4,128)S(1)} %copy.235), channel_id=1, source_target_pairs={{0,128},{1,129},{2,130},{3,131},{4,132},{5,133},{6,134},{7,135},{8... | collective-permute-start | bytes 12296 | tf_op jit(solution)/shard_map/ppermute | solution.py:22
  13.1 7.0 %collective-permute-start.1 = (f32[4,1,256]{2,0,1:T(4,128)S(1)}, f32[4,1,256]{2,0,1:T(4,128)S(1)}, u32[]{:S(2)}, u32[]{:S(2)}) collective-permute-start(f32[4,1,256]{2,0,1:T(4,128)S(1)} %copy.236), channel_id=1, source_target_pairs={{128,0},{129,1},{130,2},{131,3},{132,4},{133,5},{134,6},{135,7},{1... | collective-permute-start | bytes 12296 | tf_op jit(solution)/shard_map/ppermute | solution.py:25
  20.8 6.2 %collective-permute-start.2 = (f32[4,290,1]{1,0,2:T(4,128)S(1)}, f32[4,290,1]{1,0,2:T(4,128)S(1)}, u32[]{:S(2)}, u32[]{:S(2)}) collective-permute-start(f32[4,290,1]{1,0,2:T(4,128)S(1)} %copy.162), channel_id=1, source_target_pairs={{0,32},{32,64},{64,96},{1,33},{33,65},{65,97},{2,34},{34,66},{66,9... | collective-permute-start | bytes 13928 | tf_op jit(solution)/shard_map/ppermute | solution.py:22
  24.5 5.5 %collective-permute-start.3 = (f32[4,290,1]{1,0,2:T(4,128)S(1)}, f32[4,290,1]{1,0,2:T(4,128)S(1)}, u32[]{:S(2)}, u32[]{:S(2)}) collective-permute-start(f32[4,290,1]{1,0,2:T(4,128)S(1)} %copy.163), channel_id=1, source_target_pairs={{32,0},{64,32},{96,64},{33,1},{65,33},{97,65},{34,2},{66,34},{98,6... | collective-permute-start | bytes 13928 | tf_op jit(solution)/shard_map/ppermute | solution.py:25
  33.6 2.9 collective-permute-start.5
  35.0 4.6 %collective-permute-start.4 = (f32[1,290,258]{2,0,1:T(1,128)S(1)}, f32[1,290,258]{2,0,1:T(1,128)S(1)}, u32[]{:S(2)}, u32[]{:S(2)}) collective-permute-start(f32[1,290,258]{2,0,1:T(1,128)S(1)} %get-tuple-element.38), channel_id=1, source_target_pairs={{1,0},{2,1},{3,2},{4,3},{5,4},{6,5},{7,6},{8,7},{9,8},{10,9},{11,1... | collective-permute-start | bytes 897848 | tf_op jit(solution)/shard_map/ppermute | solution.py:25
  59.5 4.4 %collective-permute-start.6 = (f32[4,1,256]{2,0,1:T(4,128)S(1)}, f32[4,1,256]{2,0,1:T(4,128)S(1)}, u32[]{:S(2)}, u32[]{:S(2)}) collective-permute-start(f32[4,1,256]{2,0,1:T(4,128)S(1)} %get-tuple-element.48), channel_id=1, source_target_pairs={{0,128},{1,129},{2,130},{3,131},{4,132},{5,133},{6,134},{7,135},{8... | collective-permute-start | bytes 12296 | tf_op jit(solution)/shard_map/ppermute | solution.py:22
  62.6 7.0 %collective-permute-start.7 = (f32[4,1,256]{2,0,1:T(4,128)S(1)}, f32[4,1,256]{2,0,1:T(4,128)S(1)}, u32[]{:S(2)}, u32[]{:S(2)}) collective-permute-start(f32[4,1,256]{2,0,1:T(4,128)S(1)} %get-tuple-element.49), channel_id=1, source_target_pairs={{128,0},{129,1},{130,2},{131,3},{132,4},{133,5},{134,6},{135,7},{1... | collective-permute-start | bytes 12296 | tf_op jit(solution)/shard_map/ppermute | solution.py:25
  71.1 6.3 %collective-permute-start.8 = (f32[4,290,1]{1,0,2:T(4,128)}, f32[4,290,1]{1,0,2:T(4,128)S(1)}, u32[]{:S(2)}, u32[]{:S(2)}) collective-permute-start(f32[4,290,1]{1,0,2:T(4,128)} %copy.167), channel_id=1, source_target_pairs={{0,32},{32,64},{64,96},{1,33},{33,65},{65,97},{2,34},{34,66},{66,9... | collective-permute-start | bytes 13928 | tf_op jit(solution)/shard_map/ppermute | solution.py:22
  74.5 5.6 %collective-permute-start.9 = (f32[4,290,1]{1,0,2:T(4,128)S(1)}, f32[4,290,1]{1,0,2:T(4,128)}, u32[]{:S(2)}, u32[]{:S(2)}) collective-permute-start(f32[4,290,1]{1,0,2:T(4,128)S(1)} %copy.168), channel_id=1, source_target_pairs={{32,0},{64,32},{96,64},{33,1},{65,33},{97,65},{34,2},{66,34},{98,6... | collective-permute-start | bytes 13928 | tf_op jit(solution)/shard_map/ppermute | solution.py:25
  86.4 10.8 %copy-start.10 = (pred[289]{0:T(512)(128)(4,1)S(1)}, pred[289]{0:T(512)(128)(4,1)}, u32[]{:S(2)}) copy-start(pred[289]{0:T(512)(128)(4,1)} %copy-done.9) | copy-start | bytes 871
  86.4 10.8 %copy-start.13 = (pred[257]{0:T(512)(128)(4,1)S(1)}, pred[257]{0:T(512)(128)(4,1)}, u32[]{:S(2)}) copy-start(pred[257]{0:T(512)(128)(4,1)} %copy-done.12) | copy-start | bytes 775
  86.4 6.9 %collective-permute-start.11 = (f32[1,290,258]{2,0,1:T(1,128)S(1)}, f32[1,290,258]{2,0,1:T(1,128)S(1)}, u32[]{:S(2)}, u32[]{:S(2)}) collective-permute-start(f32[1,290,258]{2,0,1:T(1,128)S(1)} %get-tuple-element.37), channel_id=1, source_target_pairs={{0,1},{1,2},{2,3},{3,4},{4,5},{5,6},{6,7},{7,8},{8,9},{9,10},{10,1... | collective-permute-start | bytes 897848 | tf_op jit(solution)/shard_map/ppermute | solution.py:22
  92.0 5.3 %collective-permute-start.10 = (f32[1,290,258]{2,0,1:T(1,128)S(1)}, f32[1,290,258]{2,0,1:T(1,128)S(1)}, u32[]{:S(2)}, u32[]{:S(2)}) collective-permute-start(f32[1,290,258]{2,0,1:T(1,128)S(1)} %get-tuple-element.36), channel_id=1, source_target_pairs={{1,0},{2,1},{3,2},{4,3},{5,4},{6,5},{7,6},{8,7},{9,8},{10,9},{11,1... | collective-permute-start | bytes 897848 | tf_op jit(solution)/shard_map/ppermute | solution.py:25
  107.2 3.6 %collective-permute-start.12 = (f32[4,1,256]{2,0,1:T(4,128)S(1)}, f32[4,1,256]{2,0,1:T(4,128)S(1)}, u32[]{:S(2)}, u32[]{:S(2)}) collective-permute-start(f32[4,1,256]{2,0,1:T(4,128)S(1)} %get-tuple-element.46), channel_id=1, source_target_pairs={{0,128},{1,129},{2,130},{3,131},{4,132},{5,133},{6,134},{7,135},{8... | collective-permute-start | bytes 12296 | tf_op jit(solution)/shard_map/ppermute | solution.py:22
  109.5 7.0 %collective-permute-start.13 = (f32[4,1,256]{2,0,1:T(4,128)S(1)}, f32[4,1,256]{2,0,1:T(4,128)S(1)}, u32[]{:S(2)}, u32[]{:S(2)}) collective-permute-start(f32[4,1,256]{2,0,1:T(4,128)S(1)} %get-tuple-element.47), channel_id=1, source_target_pairs={{128,0},{129,1},{130,2},{131,3},{132,4},{133,5},{134,6},{135,7},{1... | collective-permute-start | bytes 12296 | tf_op jit(solution)/shard_map/ppermute | solution.py:25
  119.3 6.1 %collective-permute-start.14 = (f32[4,290,1]{1,0,2:T(4,128)S(1)}, f32[4,290,1]{1,0,2:T(4,128)S(1)}, u32[]{:S(2)}, u32[]{:S(2)}) collective-permute-start(f32[4,290,1]{1,0,2:T(4,128)S(1)} %copy.171), channel_id=1, source_target_pairs={{0,32},{32,64},{64,96},{1,33},{33,65},{65,97},{2,34},{34,66},{66,9... | collective-permute-start | bytes 13928 | tf_op jit(solution)/shard_map/ppermute | solution.py:22
  121.5 5.5 %collective-permute-start.15 = (f32[4,290,1]{1,0,2:T(4,128)S(1)}, f32[4,290,1]{1,0,2:T(4,128)S(1)}, u32[]{:S(2)}, u32[]{:S(2)}) collective-permute-start(f32[4,290,1]{1,0,2:T(4,128)S(1)} %copy.172), channel_id=1, source_target_pairs={{32,0},{64,32},{96,64},{33,1},{65,33},{97,65},{34,2},{66,34},{98,6... | collective-permute-start | bytes 13928 | tf_op jit(solution)/shard_map/ppermute | solution.py:25
  135.6 21.8 %collective-permute-start.17 = (f32[1,290,258]{2,0,1:T(1,128)}, f32[1,290,258]{2,0,1:T(1,128)S(1)}, u32[]{:S(2)}, u32[]{:S(2)}) collective-permute-start(f32[1,290,258]{2,0,1:T(1,128)} %get-tuple-element.35), channel_id=1, source_target_pairs={{0,1},{1,2},{2,3},{3,4},{4,5},{5,6},{6,7},{7,8},{8,9},{9,10},{10,1... | collective-permute-start | bytes 897848 | tf_op jit(solution)/shard_map/ppermute | solution.py:22
  141.5 18.7 %collective-permute-start.16 = (f32[1,290,258]{2,0,1:T(1,128)}, f32[1,290,258]{2,0,1:T(1,128)}, u32[]{:S(2)}, u32[]{:S(2)}) collective-permute-start(f32[1,290,258]{2,0,1:T(1,128)} %get-tuple-element.34), channel_id=1, source_target_pairs={{1,0},{2,1},{3,2},{4,3},{5,4},{6,5},{7,6},{8,7},{9,8},{10,9},{11,1... | collective-permute-start | bytes 897848 | tf_op jit(solution)/shard_map/ppermute | solution.py:25
  160.2 11.5 %slice-start.2 = ((s8[4718592]{0:T(1024)(128)(4,1)}), s8[4194304]{0:T(1024)(128)(4,1)S(1)}, s32[]{:S(2)}) async-start(s8[4718592]{0:T(1024)(128)(4,1)} %bitcast.89), calls=%async_computation.6 | async-start | bytes 8388608
  171.8 32.2 %copy-start.3 = (f32[4,288,256]{2,1,0:T(8,128)S(1)}, f32[4,288,256]{2,1,0:T(8,128)}, u32[]{:S(2)}) copy-start(f32[4,288,256]{2,1,0:T(8,128)} %param.6) | copy-start | bytes 3538948
  211.6 30.3 %all-to-all-start.1 = ((f32[32,1,256]{2,1,0:T(1,128)}), f32[32,1,256]{2,1,0:T(1,128)S(1)}, u32[]{:S(2)}, u32[]{:S(2)}) async-start(f32[32,1,256]{2,1,0:T(1,128)} %reshape.115), calls=%async_computation.1 | async-start | bytes 65536 | tf_op jit(solution)/shard_map/all_to_all | solution.py:32
  (19 other events, 86.3 us)
Sparse Core Ops, SparseCore 0:
  210.7 136.4 reduce-scatter.1
where the time goes:
time: 362 us; the launch traced here: 357 us
  waiting for transfers between devices  125 us (35%)
  starting transfers between devices  70.9 us (20%)
  other arithmetic  61.7 us (17%)
  matrix products  46.7 us (13%)
  local copies, waits for them, and re-layouts  26.5 us (7%)
  between operations  15 us (4%)
  blocking collectives  10.6 us (3%)
    reduce_scatter x1, waiting for transfers between devices, local(): lax.psum_scatter(total_part, 'frame', scatter_dimension=1, tiled=True)  99.7 us
    ppermute x9, starting transfers between devices, with_halo(): lax.ppermute(lax.slice_in_dim(block, block.shape[dim] - width, None, axis...  31.5 us
    ppermute x9, waiting for transfers between devices, with_halo(): lax.ppermute(lax.slice_in_dim(block, 0, width, axis=dim), axis, backward)  25.2 us
    all_to_all x1, starting transfers between devices, from_everyone(): lax.all_to_all(jnp.broadcast_to(value[None], (peers, *value.shape)), axis...  21.7 us
    mul x6, other arithmetic, descend(): fluxes = [slope_part * weight for slope_part in slopes]  21.4 us
    ppermute x9, starting transfers between devices, with_halo(): lax.ppermute(lax.slice_in_dim(block, 0, width, axis=dim), axis, backward)  17.6 us
    slice x3, other arithmetic, with_halo(): lax.slice_in_dim(block, 0, width, axis=dim)  16 us
    dot_general x1, matrix products, local(): gram_part = jnp.dot(flat_basis, flat_basis.T, precision=highest)  14.2 us
  transfers between devices with their start and end apart: 20, of which 10 were waited for; matrix products, arithmetic and copies ran while one was open for 11% of the time, Pallas kernels for 0%

commit v1 on v0

--- a/solution.py
+++ b/solution.py
@@ -1,6 +1,10 @@
+import functools
+
 import jax
 import jax.numpy as jnp
 from jax import lax
+from jax.experimental import pallas as pl
+from jax.experimental.pallas import tpu as pltpu
 from jax.sharding import PartitionSpec as P
 
 PASSES = 3
@@ -25,26 +29,6 @@
         high = lax.ppermute(lax.slice_in_dim(block, 0, width, axis=dim), axis, backward)
         block = jnp.concatenate([low, block, high], axis=dim)
     return block
-
-
-def from_everyone(value, axis):
-    peers = lax.axis_size(axis)
-    return lax.all_to_all(
-        jnp.broadcast_to(value[None], (peers, *value.shape)), axis, 0, 0, tiled=True
-    )
-
-
-def over_copies(value, axis):
-    return from_everyone(value, axis).sum(axis=0)
-
-
-def in_one(arrays, axis):
-    line, at, done = (jnp.concatenate([a.reshape(-1) for a in arrays]), 0, [])
-    running = over_copies(line, axis)
-    for a in arrays:
-        done.append(running[at : at + a.size].reshape(a.shape))
-        at += a.size
-    return tuple(done)
 
 
 def forward_cells(padded, direction, shape):
@@ -80,12 +64,94 @@
     return center + relax_rate * (source - center + smooth_weight * spread)
 
 
-def solve_definite(matrix, right_side):
-    factor_lower = jnp.linalg.cholesky(matrix)
-    half_solved = lax.linalg.triangular_solve(factor_lower, right_side, left_side=True, lower=True)
-    return lax.linalg.triangular_solve(
-        factor_lower, half_solved, left_side=True, lower=True, transpose_a=True
-    )
+HIGHEST = lax.Precision.HIGHEST
+
+
+def iota(shape, dim):
+    return lax.broadcasted_iota(jnp.int32, shape, dim)
+
+
+def dot(a, b):
+    return jnp.dot(a, b, precision=HIGHEST, preferred_element_type=jnp.float32)
+
+
+def eliminated(matrix):
+    n = matrix.shape[0]
+    wide = (n, 128)
+    lanes, rows = iota(wide, 1), iota(wide, 0)
+    work = jnp.concatenate([matrix, jnp.zeros((n, 128 - n), jnp.float32)], axis=1)
+    work = work + jnp.where(lanes == rows + n, 1.0, 0.0)
+    for k in range(n):
+        column = jnp.broadcast_to(work[:, k : k + 1], wide)
+        pivot = jnp.broadcast_to(work[k : k + 1, :], wide)
+        scaled = pivot / jnp.broadcast_to(column[k : k + 1, :], wide)
+        work = jnp.where(rows == k, scaled, work - column * scaled)
+    return work[:, n : 2 * n]
+
+
+def spread_ranks(rank, width):
+    return jnp.where(iota((width, rank), 0) % rank == iota((width, rank), 1), 1.0, 0.0)
+
+
+def inverse_kernel(ridge, gram_ref, out_ref):
+    rank = gram_ref.shape[0]
+    eye = jnp.where(iota((rank, rank), 0) == iota((rank, rank), 1), ridge, 0.0)
+    inverse = eliminated(gram_ref[...] + eye)
+    out_ref[...] = spread_blocks(inverse, out_ref.shape[0], 4)
+
+
+def spread_blocks(block, width, count):
+    rank = block.shape[0]
+    pick = spread_ranks(rank, width)
+    full = dot(dot(pick, block), pick.T)
+    a, b = iota((width, width), 0) // rank, iota((width, width), 1) // rank
+    return jnp.where((a == b) & (a < count), full, 0.0)
+
+
+def final_kernel(ridge, rank, slot_ref, got_ref, cross_ref, inverse_ref, old_ref, basis_ref, coeff_ref, coeff_all, stage):
+    slots = got_ref.shape[0]
+    rows_owned = old_ref.shape[0]
+    cross = cross_ref[0]
+    for peer in range(1, cross_ref.shape[0]):
+        cross = cross + cross_ref[peer]
+    coeff = dot(cross, inverse_ref[...])
+    coeff_all[...] = coeff
+    mine = coeff_all[pl.ds(slot_ref[0], 1), :]
+    for f in range(4):
+        coeff_ref[f : f + 1, :] = mine[:, f * rank : (f + 1) * rank]
+    width = 128
+    coeff_t = coeff.T
+    full = dot(coeff_t, coeff)
+    a, b = iota((width, width), 0) // rank, iota((width, width), 1) // rank
+    pick = spread_ranks(rank, width)
+    gram = dot(dot(pick.T, jnp.where(a == b, full, 0.0)), pick)
+    eye = jnp.where(iota((rank, rank), 0) == iota((rank, rank), 1), ridge, 0.0)
+    inverse = eliminated(gram + eye)
+    lines = 8 * slots
+    repeat = jnp.where(iota((slots, lines), 0) == iota((slots, lines), 1) // 8, 1.0, 0.0)
+    wide = dot(coeff_t, repeat)
+    wide = jnp.where(
+        iota((width, lines), 0) // rank == iota((width, lines), 1) % 4, wide, 0.0
+    )
+    twice = spread_ranks(rank, 2 * rank)
+    mix = dot(dot(twice, inverse), pick.T)
+    factor = jnp.where(
+        iota((2 * rank, lines), 0) // rank == (iota((2 * rank, lines), 1) // 4) % 2, dot(mix, wide), 0.0
+    )
+    old_factor = ridge * spread_blocks(inverse, 2 * rank, 2)
+    for i in range(rows_owned):
+        block = got_ref[:, 8 * i : 8 * (i + 1), :].reshape(lines, 128)
+        stage[i] = dot(factor, block) + dot(old_factor, old_ref[i])
+    flat = stage.reshape(rows_owned * 2 * rank, 128)
+    for half in range(2):
+        for r in range(rank):
+            basis_ref[r, :, half * 128 : (half + 1) * 128] = flat[
+                pl.ds(half * rank + r, rows_owned, stride=2 * rank), :
+            ]
+
+
+def vmem(count):
+    return [pl.BlockSpec(memory_space=pltpu.VMEM)] * count
 
 
 def local(video, multiplier, foreground, basis, coefficients):
@@ -106,33 +172,57 @@
     flat_basis = basis.reshape(rank_size, pixels)
     background = jnp.dot(coefficients, flat_basis, precision=highest).reshape(video.shape)
     target = video - background + dual_scale * multiplier
+    blocks = row_count * col_count
+    pixel_ridge = ridge_share * pixels * blocks
+    gram_sum = lax.psum(jnp.dot(flat_basis, flat_basis.T, precision=highest), ("row", "col"))
+    inverse = pl.pallas_call(
+        functools.partial(inverse_kernel, pixel_ridge),
+        out_shape=jax.ShapeDtypeStruct((128, 128), jnp.float32),
+        in_specs=vmem(1),
+        out_specs=vmem(1)[0],
+        name="inverse",
+    )(gram_sum)
     current = foreground
     for sweep in range(PASSES):
         padded = with_halo(current, (("row", 1), ("col", 2), ("frame", 0)), 1)
         current = descend(padded, target, tuple((start_cell - 1 for start_cell in corner)), extent)
+        if sweep == 1:
+            current, inverse = lax.optimization_barrier((current, inverse))
     shrunk = current - jnp.clip(current, -shrink_level, shrink_level)
     residual_target = video + dual_scale * multiplier - shrunk
     flat_target = residual_target.reshape(frames_here, pixels)
-    gram_part = jnp.dot(flat_basis, flat_basis.T, precision=highest)
-    cross_part = jnp.dot(flat_basis, flat_target.T, precision=highest)
-    gram_sum, cross_sum = in_one((gram_part, cross_part), ("row", "col"))
-    identity_matrix = jnp.eye(rank_size, dtype=gram_sum.dtype)
-    pixel_ridge = ridge_share * pixels * row_count * col_count
-    coeff_rows = solve_definite(
-        gram_sum + pixel_ridge * identity_matrix, cross_sum + pixel_ridge * coefficients.T
-    )
-    total_part = jnp.dot(coeff_rows, flat_target, precision=highest).reshape(
-        rank_size, rows_here, cols_here
-    )
-    frame_gram_part = jnp.dot(coeff_rows, coeff_rows.T, precision=highest)
+    cross_part = jnp.dot(flat_target, flat_basis.T, precision=highest)
+    cross_part = cross_part + (pixel_ridge / blocks) * coefficients
     owned_rows = rows_here // frame_count
-    owned_sums = lax.psum_scatter(total_part, "frame", scatter_dimension=1, tiled=True)
-    frame_gram = over_copies(frame_gram_part, "frame")
+    chunks = residual_target.reshape(frames_here, frame_count, owned_rows, 2, 128)
+    chunks = chunks.transpose(1, 2, 3, 0, 4).reshape(frame_count, owned_rows * 8, 128)
+    extra = jnp.pad(cross_part.reshape(1, 1, -1), ((0, 0), (0, 7), (0, 64)))
+    extra = jnp.broadcast_to(extra, (frame_count, 8, 128))
+    sent = jnp.concatenate([chunks, extra], axis=1)
+    got = lax.all_to_all(sent, "frame", 0, 0, tiled=True)
+    cross_all = got[:, owned_rows * 8, :]
+    cross_all = lax.all_to_all(
+        jnp.broadcast_to(cross_all[None], (blocks, *cross_all.shape)), ("row", "col"), 0, 0, tiled=True
+    )
     old_owned = lax.dynamic_slice_in_dim(basis, frame_slot * owned_rows, owned_rows, 1)
+    old_owned = old_owned.reshape(rank_size, owned_rows, 2, 128).transpose(1, 2, 0, 3)
+    old_owned = old_owned.reshape(owned_rows, 2 * rank_size, 128)
     frame_ridge = ridge_share * frames_here * frame_count
-    right_side = (owned_sums + frame_ridge * old_owned).reshape(rank_size, owned_rows * cols_here)
-    new_basis = solve_definite(frame_gram + frame_ridge * identity_matrix, right_side)
-    return (shrunk, coeff_rows.T, new_basis.reshape(rank_size, owned_rows, cols_here))
+    new_basis, new_coeff = pl.pallas_call(
+        functools.partial(final_kernel, frame_ridge, rank_size),
+        out_shape=(
+            jax.ShapeDtypeStruct((rank_size, owned_rows, cols_here), jnp.float32),
+            jax.ShapeDtypeStruct((frames_here, rank_size), jnp.float32),
+        ),
+        in_specs=[pl.BlockSpec(memory_space=pltpu.SMEM)] + vmem(4),
+        out_specs=vmem(2),
+        scratch_shapes=[
+            pltpu.VMEM((frame_count, 128), jnp.float32),
+            pltpu.VMEM((owned_rows, 2 * rank_size, 128), jnp.float32),
+        ],
+        name="final",
+    )(frame_slot.reshape(1), got, cross_all, inverse, old_owned)
+    return shrunk, new_coeff, new_basis
 
 
 def solution(mesh):

time: 362 us -> 287 us (0.79)
  waiting for transfers between devices: 125 us -> 62.1 us
  between operations: 15 us -> 1.58 us
  other arithmetic: 61.7 us -> 50.4 us
  matrix products: 46.7 us -> 35.6 us
  blocking collectives: 10.6 us -> 20.9 us
  Pallas kernels: 0 us -> 9.93 us
  starting transfers between devices: 70.9 us -> 76.1 us
    reduce_scatter x1 -> x0, waiting for transfers between devices: 99.7 us -> none  [local(): lax.psum_scatter(total_part, 'frame', scatter_dimension=1, tiled=True)]
    all_to_all x1 -> x2, waiting for transfers between devices: 0.01 us -> 38 us  [the longest x1 34 us: local(): got = lax.all_to_all(sent, 'frame', 0, 0, tiled=True)]
    psum x0 -> x1, blocking collectives: none -> 20.9 us  [local(): lax.psum(jnp.dot(flat_basis, flat_basis.T, precision=highest), ('row', 'c...]
    all_to_all x1 -> x0, blocking collectives: 10.6 us -> none  [from_everyone(): lax.all_to_all(jnp.broadcast_to(value[None], (peers, *value.shape)), axis...]
    pallas_call x0 -> x2, Pallas kernels: none -> 9.93 us  [the longest x1 6.29 us: local(): pl.pallas_call(functools.partial(final_kernel, frame_ridge, rank_size), o...]
    another operation x10 -> x0, other arithmetic: 9.31 us -> none  [the longest x4 5.05 us: solve_definite(): lax.linalg.triangular_solve(factor_lower, half_solved, left_side=True, lo...]
    dot_general x4 -> x2, matrix products: 30.6 us -> 22.3 us  [the longest x1 14.8 us: local(): jnp.dot(flat_basis, flat_basis.T, precision=highest)]
    all_to_all x1 -> x2, starting transfers between devices: 21.7 us -> 29.2 us  [the longest x1 23.9 us: local(): got = lax.all_to_all(sent, 'frame', 0, 0, tiled=True)]
  transfers between devices with their start and end apart: 20 -> 20, of which waited for: 10 -> 9; matrix products, arithmetic and copies ran while one was open for 11% -> 11% of each run, Pallas kernels for 0% -> 1%
where the time goes in v1:
time: 287 us; the launch traced here: 281 us
  starting transfers between devices  76.1 us (27%)
  waiting for transfers between devices  62.1 us (22%)
  other arithmetic  50.4 us (18%)
  matrix products  35.6 us (12%)
  local copies, waits for them, and re-layouts  24.8 us (9%)
  blocking collectives  20.9 us (7%)
  Pallas kernels  9.93 us (3%)
    all_to_all x1, waiting for transfers between devices, local(): got = lax.all_to_all(sent, 'frame', 0, 0, tiled=True)  34 us
    ppermute x9, starting transfers between devices, with_halo(): lax.ppermute(lax.slice_in_dim(block, block.shape[dim] - width, None, axis...  27.5 us
    ppermute x9, waiting for transfers between devices, with_halo(): lax.ppermute(lax.slice_in_dim(block, 0, width, axis=dim), axis, backward)  24.1 us
    all_to_all x1, starting transfers between devices, local(): got = lax.all_to_all(sent, 'frame', 0, 0, tiled=True)  23.9 us
    psum x1, blocking collectives, local(): lax.psum(jnp.dot(flat_basis, flat_basis.T, precision=highest), ('row', 'c...  20.9 us
    mul x6, other arithmetic, descend(): fluxes = [slope_part * weight for slope_part in slopes]  20.3 us
    ppermute x9, starting transfers between devices, with_halo(): lax.ppermute(lax.slice_in_dim(block, 0, width, axis=dim), axis, backward)  19.4 us
    dot_general x1, matrix products, local(): jnp.dot(flat_basis, flat_basis.T, precision=highest)  14.8 us
  transfers between devices with their start and end apart: 20, of which 9 were waited for; matrix products, arithmetic and copies ran while one was open for 11% of the time, Pallas kernels for 1%

profile of v1, /device:TPU:2, one launch (start us, length us, event | category | flops | bytes accessed | tf_op | source)
XLA Modules:
  0.0 281.3 jit_solution(13777170669553900946)
XLA Ops:
  1.4 5.1 %collective-permute-start = (f32[4,1,256]{2,0,1:T(4,128)S(1)}, f32[4,1,256]{2,0,1:T(4,128)S(1)}, u32[]{:S(2)}, u32[]{:S(2)}) collective-permute-start(f32[4,1,256]{2,0,1:T(4,128)S(1)} %copy.99), channel_id=1, source_target_pairs={{0,128},{1,129},{2,130},{3,131},{4,132},{5,133},{6,134},{7,135},{8... | collective-permute-start | bytes 12296 | tf_op jit(solution)/shard_map/ppermute | solution.py:26
  10.0 3.6 %collective-permute-done.1 = f32[4,1,256]{2,0,1:T(4,128)S(1)} collective-permute-done((f32[4,1,256]{2,0,1:T(4,128)S(1)}, f32[4,1,256]{2,0,1:T(4,128)S(1)}, u32[]{:S(2)}, u32[]{:S(2)}) %collective-permute-start.1) | collective-permute-done | bytes 4128 | tf_op jit(solution)/shard_map/ppermute | solution.py:29
  14.2 3.4 %collective-permute-start.2 = (f32[4,290,1]{1,0,2:T(4,128)S(1)}, f32[4,290,1]{1,0,2:T(4,128)S(1)}, u32[]{:S(2)}, u32[]{:S(2)}) collective-permute-start(f32[4,290,1]{1,0,2:T(4,128)S(1)} %copy.46), channel_id=1, source_target_pairs={{0,32},{32,64},{64,96},{1,33},{33,65},{65,97},{2,34},{34,66},{66,9... | collective-permute-start | bytes 13928 | tf_op jit(solution)/shard_map/ppermute | solution.py:26
  33.0 4.6 %fusion.65 = (f32[5,289,257]{2,0,1:T(8,128)}, f32[5,289,257]{2,0,1:T(8,128)S(1)}) fusion(f32[5,290,258]{2,0,1:T(8,128)S(1)} %maximum_maximum_fusion, f32[1,290,258]{2,0,1:T(1,128)S(1)} %collective-permute-done.4, f32[4,290,1]{2,0,1:T(4,128)S(1)} %copy.49, f32[4,290,256]{2,0,1:T(4,128)S(1)} %constant_dynamic-update-slice_fusion, f32[4,290,1]{2,0,1:T(4,128)S(1)} %copy.48, ...), kind=kLoop, calls=%fused_computation.114 | loop fusion | flops 5941840 | bytes 8924251 | tf_op jit(solution)/shard_map/mul | solution.py:56
  39.9 13.3 %fusion.41 = (f32[4,288,256]{2,0,1:T(4,128)S(1)}, f32[4,288,256]{2,0,1:T(4,128)S(1)}) fusion(f32[5,289,257]{2,0,1:T(8,128)S(1)} %get-tuple-element.33, f32[5,289,257]{2,0,1:T(8,128)S(1)} %get-tuple-element.32, f32[5,289,257]{2,0,1:T(8,128)} %get-tuple-element.26, f32[4,288,256]{2,1,0:T(8,128)S(1)} %copy-done.3, f32[4,288,256]{2,1,0:T(8,128)} %param.6, ...), kind=kOutput, calls=%fused_computation.70 | convolution fusion | flops 60456960 | bytes 17694976 | tf_op jit(solution)/shard_map/dot_general | solution.py:173
  57.6 5.7 %collective-permute-done.7 = f32[4,1,256]{2,0,1:T(4,128)S(1)} collective-permute-done((f32[4,1,256]{2,0,1:T(4,128)S(1)}, f32[4,1,256]{2,0,1:T(4,128)S(1)}, u32[]{:S(2)}, u32[]{:S(2)}) %collective-permute-start.7) | collective-permute-done | bytes 4128 | tf_op jit(solution)/shard_map/ppermute | solution.py:29
  77.4 6.0 %pad_maximum_fusion.20 = (f32[1,290,258]{2,0,1:T(1,128)}, f32[1,290,258]{2,0,1:T(1,128)}) fusion(f32[4,290,1]{2,0,1:T(4,128)S(1)} %copy.54, f32[4,290,1]{2,0,1:T(4,128)S(1)} %copy.53, f32[4,1,256]{2,0,1:T(4,128)S(1)} %collective-permute-done.7, f32[4,288,256]{2,0,1:T(4,128)S(1)} %get-tuple-element.52, f32[4,1,256]{2,0,1:T(4,128)S(1)} %collective-permute-done.6), kind=kLoop, calls=%fused_computation.89 | loop fusion | flops 598560 | bytes 1795680 | tf_op jit(solution)/shard_map/slice | solution.py:29
  83.4 6.3 %collective-permute-start.11 = (f32[1,290,258]{2,0,1:T(1,128)}, f32[1,290,258]{2,0,1:T(1,128)}, u32[]{:S(2)}, u32[]{:S(2)}) collective-permute-start(f32[1,290,258]{2,0,1:T(1,128)} %get-tuple-element.37), channel_id=1, source_target_pairs={{0,1},{1,2},{2,3},{3,4},{4,5},{5,6},{6,7},{7,8},{8,9},{9,10},{10,1... | collective-permute-start | bytes 897848 | tf_op jit(solution)/shard_map/ppermute | solution.py:26
  90.9 14.8 %fusion.43 = f32[16,16]{1,0:T(8,128)} fusion(f32[16,288,256]{2,1,0:T(8,128)} %param.8), kind=kOutput, calls=%fused_computation.76 | convolution fusion | flops 226492416 | bytes 4719616 | tf_op jit(solution)/shard_map/dot_general | solution.py:177
  105.8 20.9 %psum.7.gram_ref = f32[16,16]{1,0:T(8,128)} all-reduce(f32[16,16]{1,0:T(8,128)} %fusion.43), channel_id=1, replica_groups=mesh['row'=2,'col'=4,'frame'=32] {'row','col'}, use_global_device_ids=true, to_apply=%region_0.0 | all-reduce | flops 256 | bytes 2048 | tf_op jit(solution)/shard_map/psum | solution.py:177
  126.6 3.6 %inverse.1.inverse_ref = f32[128,128]{1,0:T(8,128)} custom-call(f32[16,16]{1,0:T(8,128)} %psum.7.gram_ref), custom_call_target="tpu_custom_call" | custom-call | tf_op jit(solution)/shard_map/inverse/pallas_call | solution.py:178
  132.9 5.5 %fusion.67 = (f32[5,289,257]{2,0,1:T(8,128)S(1)}, f32[5,289,257]{2,0,1:T(8,128)S(1)}) fusion(f32[5,290,258]{2,0,1:T(8,128)S(1)} %maximum_maximum_fusion.1, f32[1,290,258]{2,0,1:T(1,128)} %collective-permute-done.10, f32[4,290,1]{2,0,1:T(4,128)S(1)} %copy.54, f32[4,1,256]{2,0,1:T(4,128)S(1)} %collective-permute-done.7, ...), kind=kLoop, calls=%fused_computation.116 | loop fusion | flops 6684570 | bytes 8924251 | tf_op jit(solution)/shard_map/mul | solution.py:56
  140.6 3.3 %fusion.35 = f32[4,288,256]{2,0,1:T(4,128)S(1)} fusion(f32[4,288,256]{2,0,1:T(4,128)S(1)} %get-tuple-element.52, f32[5,289,257]{2,0,1:T(8,128)S(1)} %get-tuple-element.31, f32[5,289,257]{2,0,1:T(8,128)S(1)} %get-tuple-element.30, f32[5,289,257]{2,0,1:T(8,128)S(1)} %get-tuple-element.24, f32[4,288,256]{2,0,1:T(4,128)S(1)} %get-tuple-element.53), kind=kLoop, calls=%fused_computation.61 | loop fusion | flops 2949120 | bytes 10616832 | tf_op jit(solution)/shard_map/add | solution.py:64
  147.5 5.4 %collective-permute-done.13 = f32[4,1,256]{2,0,1:T(4,128)S(1)} collective-permute-done((f32[4,1,256]{2,0,1:T(4,128)S(1)}, f32[4,1,256]{2,0,1:T(4,128)S(1)}, u32[]{:S(2)}, u32[]{:S(2)}) %collective-permute-start.13) | collective-permute-done | bytes 4128 | tf_op jit(solution)/shard_map/ppermute | solution.py:29
  159.4 5.5 %collective-permute-start.15 = (f32[4,290,1]{1,0,2:T(4,128)}, f32[4,290,1]{1,0,2:T(4,128)}, u32[]{:S(2)}, u32[]{:S(2)}) collective-permute-start(f32[4,290,1]{1,0,2:T(4,128)} %copy.58), channel_id=1, source_target_pairs={{32,0},{64,32},{96,64},{33,1},{65,33},{97,65},{34,2},{66,34},{98,6... | collective-permute-start | bytes 13928 | tf_op jit(solution)/shard_map/ppermute | solution.py:29
  168.6 4.9 %pad_maximum_fusion.15 = (f32[1,290,258]{2,0,1:T(1,128)S(1)}, f32[1,290,258]{2,0,1:T(1,128)S(1)}) fusion(f32[4,290,1]{2,0,1:T(4,128)} %copy.60, f32[4,290,256]{2,0,1:T(4,128)S(1)} %constant_dynamic-update-slice_fusion.3, f32[4,290,1]{2,0,1:T(4,128)} %copy.59), kind=kLoop, calls=%fused_computation.84 | loop fusion | flops 299280 | bytes 1795680 | tf_op jit(solution)/shard_map/slice | solution.py:29
  181.2 3.7 %fusion.66 = (f32[5,289,257]{2,0,1:T(8,128)S(1)}, f32[5,289,257]{2,0,1:T(8,128)S(1)}) fusion(f32[5,290,258]{2,0,1:T(8,128)S(1)} %maximum_maximum_fusion.2, f32[1,290,258]{2,0,1:T(1,128)S(1)} %collective-permute-done.16, f32[4,290,1]{2,0,1:T(4,128)S(1)} %copy-done.1, f32[4,290,256]{2,0,1:T(4,128)S(1)} %constant_dynamic-update-slice_fusion.3, ...), kind=kLoop, calls=%fused_computation.115 | loop fusion | flops 5941840 | bytes 8924251 | tf_op jit(solution)/shard_map/mul | solution.py:56
  187.1 5.5 %add_subtract_fusion = (f32[4,288,256]{2,0,1:T(4,128)S(1)}, f32[4,288,256]{2,0,1:T(4,128)}) fusion(f32[4,288,256]{2,1,0:T(8,128)S(1)} %copy-done.4, f32[4,288,256]{2,1,0:T(8,128)S(1)} %copy-done.5, f32[4,288,256]{2,0,1:T(4,128)S(1)} %fusion.35, f32[5,289,257]{2,0,1:T(8,128)S(1)} %get-tuple-element.29, f32[5,289,257]{2,0,1:T(8,128)S(1)} %get-tuple-element.28, ...), kind=kLoop, calls=%fused_computation.75 | loop fusion | flops 4423680 | bytes 14155776 | tf_op jit(solution)/shard_map/sub | solution.py:192
  192.7 7.5 %fusion.49 = f32[4,16]{1,0:T(4,128)S(1)} fusion(f32[4,288,256]{2,0,1:T(4,128)S(1)} %get-tuple-element.20, f32[16,288,256]{2,1,0:T(8,128)S(1)} %bitcast.45, f32[4,16]{1,0:T(4,128)S(1)} %copy-done.15), kind=kOutput, calls=%fused_computation.78 | convolution fusion | flops 56623232 | bytes 5898752 | tf_op jit(solution)/shard_map/dot_general | solution.py:194
  201.5 23.9 %all-to-all-start = ((f32[32,80,128]{2,1,0:T(8,128)}), f32[32,80,128]{2,1,0:T(8,128)S(1)}, u32[]{:S(2)}, u32[]{:S(2)}) async-start(f32[32,80,128]{2,1,0:T(8,128)} %pad_maximum_fusion.11), calls=%async_computation | async-start | bytes 2621440 | tf_op jit(solution)/shard_map/all_to_all | solution.py:202
  225.3 34.0 %all-to-all-done.got_ref = f32[32,80,128]{2,1,0:T(8,128)S(1)} async-done(((f32[32,80,128]{2,1,0:T(8,128)}), f32[32,80,128]{2,1,0:T(8,128)S(1)}, u32[]{:S(2)}, u32[]{:S(2)}) %all-to-all-start) | async-done | bytes 1310752 | tf_op jit(solution)/shard_map/all_to_all | solution.py:202
  260.1 5.4 %all-to-all-start.1 = ((f32[8,32,128]{2,1,0:T(8,128)}), f32[8,32,128]{2,1,0:T(8,128)S(1)}, u32[]{:S(2)}, u32[]{:S(2)}) async-start(f32[8,32,128]{2,1,0:T(8,128)} %broadcast_in_dim.62), calls=%async_computation.1 | async-start | bytes 262144 | tf_op jit(solution)/shard_map/all_to_all | solution.py:204
  268.5 3.9 %all-to-all-done.1.cross_ref = f32[8,32,128]{2,1,0:T(8,128)S(1)} async-done(((f32[8,32,128]{2,1,0:T(8,128)}), f32[8,32,128]{2,1,0:T(8,128)S(1)}, u32[]{:S(2)}, u32[]{:S(2)}) %all-to-all-start.1) | async-done | bytes 131104 | tf_op jit(solution)/shard_map/all_to_all | solution.py:204
  273.1 6.3 %final.1 = (f32[16,9,256]{2,1,0:T(8,128)}, f32[4,16]{1,0:T(4,128)}) custom-call(s32[1]{0:T(128)} %bitcast.3.slot_ref, f32[32,80,128]{2,1,0:T(8,128)} %copy-done.2, f32[8,32,128]{2,1,0:T(8,128)} %copy-done.7, f32[128,128]{1,0:T(8,128)} %inverse.1.inverse_ref, f32[9,32,128]{2,1,0:T(8,128)} %bitcast.47), custom_call_target="tpu_custom_call" | custom-call | tf_op jit(solution)/shard_map/final/pallas_call | solution.py:211
  (125 shorter events, 77.7 us)
Async XLA Ops:
  1.4 6.4 %collective-permute-start = (f32[4,1,256]{2,0,1:T(4,128)S(1)}, f32[4,1,256]{2,0,1:T(4,128)S(1)}, u32[]{:S(2)}, u32[]{:S(2)}) collective-permute-start(f32[4,1,256]{2,0,1:T(4,128)S(1)} %copy.99), channel_id=1, source_target_pairs={{0,128},{1,129},{2,130},{3,131},{4,132},{5,133},{6,134},{7,135},{8... | collective-permute-start | bytes 12296 | tf_op jit(solution)/shard_map/ppermute | solution.py:26
  6.5 7.0 %collective-permute-start.1 = (f32[4,1,256]{2,0,1:T(4,128)S(1)}, f32[4,1,256]{2,0,1:T(4,128)S(1)}, u32[]{:S(2)}, u32[]{:S(2)}) collective-permute-start(f32[4,1,256]{2,0,1:T(4,128)S(1)} %copy.100), channel_id=1, source_target_pairs={{128,0},{129,1},{130,2},{131,3},{132,4},{133,5},{134,6},{135,7},{1... | collective-permute-start | bytes 12296 | tf_op jit(solution)/shard_map/ppermute | solution.py:29
  14.2 6.2 %collective-permute-start.2 = (f32[4,290,1]{1,0,2:T(4,128)S(1)}, f32[4,290,1]{1,0,2:T(4,128)S(1)}, u32[]{:S(2)}, u32[]{:S(2)}) collective-permute-start(f32[4,290,1]{1,0,2:T(4,128)S(1)} %copy.46), channel_id=1, source_target_pairs={{0,32},{32,64},{64,96},{1,33},{33,65},{65,97},{2,34},{34,66},{66,9... | collective-permute-start | bytes 13928 | tf_op jit(solution)/shard_map/ppermute | solution.py:26
  17.9 5.5 %collective-permute-start.3 = (f32[4,290,1]{1,0,2:T(4,128)S(1)}, f32[4,290,1]{1,0,2:T(4,128)S(1)}, u32[]{:S(2)}, u32[]{:S(2)}) collective-permute-start(f32[4,290,1]{1,0,2:T(4,128)S(1)} %copy.47), channel_id=1, source_target_pairs={{32,0},{64,32},{96,64},{33,1},{65,33},{97,65},{34,2},{66,34},{98,6... | collective-permute-start | bytes 13928 | tf_op jit(solution)/shard_map/ppermute | solution.py:29
  27.0 3.0 %collective-permute-start.5 = (f32[1,290,258]{2,0,1:T(1,128)S(1)}, f32[1,290,258]{2,0,1:T(1,128)S(1)}, u32[]{:S(2)}, u32[]{:S(2)}) collective-permute-start(f32[1,290,258]{2,0,1:T(1,128)S(1)} %get-tuple-element.39), channel_id=1, source_target_pairs={{0,1},{1,2},{2,3},{3,4},{4,5},{5,6},{6,7},{7,8},{8,9},{9,10},{10,1... | collective-permute-start | bytes 897848 | tf_op jit(solution)/shard_map/ppermute | solution.py:26
  28.4 9.2 %copy-start.8 = (pred[289]{0:T(512)(128)(4,1)}, pred[289]{0:T(512)(128)(4,1)S(1)}, u32[]{:S(2)}) copy-start(pred[289]{0:T(512)(128)(4,1)S(1)} %fusion.63) | copy-start | bytes 871
  28.4 4.6 %collective-permute-start.4 = (f32[1,290,258]{2,0,1:T(1,128)S(1)}, f32[1,290,258]{2,0,1:T(1,128)S(1)}, u32[]{:S(2)}, u32[]{:S(2)}) collective-permute-start(f32[1,290,258]{2,0,1:T(1,128)S(1)} %get-tuple-element.38), channel_id=1, source_target_pairs={{1,0},{2,1},{3,2},{4,3},{5,4},{6,5},{7,6},{8,7},{9,8},{10,9},{11,1... | collective-permute-start | bytes 897848 | tf_op jit(solution)/shard_map/ppermute | solution.py:29
  53.2 4.4 %collective-permute-start.6 = (f32[4,1,256]{2,0,1:T(4,128)S(1)}, f32[4,1,256]{2,0,1:T(4,128)S(1)}, u32[]{:S(2)}, u32[]{:S(2)}) collective-permute-start(f32[4,1,256]{2,0,1:T(4,128)S(1)} %get-tuple-element.48), channel_id=1, source_target_pairs={{0,128},{1,129},{2,130},{3,131},{4,132},{5,133},{6,134},{7,135},{8... | collective-permute-start | bytes 12296 | tf_op jit(solution)/shard_map/ppermute | solution.py:26
  56.3 7.0 %collective-permute-start.7 = (f32[4,1,256]{2,0,1:T(4,128)S(1)}, f32[4,1,256]{2,0,1:T(4,128)S(1)}, u32[]{:S(2)}, u32[]{:S(2)}) collective-permute-start(f32[4,1,256]{2,0,1:T(4,128)S(1)} %get-tuple-element.49), channel_id=1, source_target_pairs={{128,0},{129,1},{130,2},{131,3},{132,4},{133,5},{134,6},{135,7},{1... | collective-permute-start | bytes 12296 | tf_op jit(solution)/shard_map/ppermute | solution.py:29
  66.3 7.7 %collective-permute-start.8 = (f32[4,290,1]{1,0,2:T(4,128)S(1)}, f32[4,290,1]{1,0,2:T(4,128)S(1)}, u32[]{:S(2)}, u32[]{:S(2)}) collective-permute-start(f32[4,290,1]{1,0,2:T(4,128)S(1)} %copy.51), channel_id=1, source_target_pairs={{0,32},{32,64},{64,96},{1,33},{33,65},{65,97},{2,34},{34,66},{66,9... | collective-permute-start | bytes 13928 | tf_op jit(solution)/shard_map/ppermute | solution.py:26
  70.8 5.6 %collective-permute-start.9 = (f32[4,290,1]{1,0,2:T(4,128)S(1)}, f32[4,290,1]{1,0,2:T(4,128)}, u32[]{:S(2)}, u32[]{:S(2)}) collective-permute-start(f32[4,290,1]{1,0,2:T(4,128)S(1)} %copy.52), channel_id=1, source_target_pairs={{32,0},{64,32},{96,64},{33,1},{65,33},{97,65},{34,2},{66,34},{98,6... | collective-permute-start | bytes 13928 | tf_op jit(solution)/shard_map/ppermute | solution.py:29
  83.4 46.9 %collective-permute-start.11 = (f32[1,290,258]{2,0,1:T(1,128)}, f32[1,290,258]{2,0,1:T(1,128)}, u32[]{:S(2)}, u32[]{:S(2)}) collective-permute-start(f32[1,290,258]{2,0,1:T(1,128)} %get-tuple-element.37), channel_id=1, source_target_pairs={{0,1},{1,2},{2,3},{3,4},{4,5},{5,6},{6,7},{7,8},{8,9},{9,10},{10,1... | collective-permute-start | bytes 897848 | tf_op jit(solution)/shard_map/ppermute | solution.py:26
  89.7 43.2 %collective-permute-start.10 = (f32[1,290,258]{2,0,1:T(1,128)}, f32[1,290,258]{2,0,1:T(1,128)}, u32[]{:S(2)}, u32[]{:S(2)}) collective-permute-start(f32[1,290,258]{2,0,1:T(1,128)} %get-tuple-element.36), channel_id=1, source_target_pairs={{1,0},{2,1},{3,2},{4,3},{5,4},{6,5},{7,6},{8,7},{9,8},{10,9},{11,1... | collective-permute-start | bytes 897848 | tf_op jit(solution)/shard_map/ppermute | solution.py:29
  143.9 3.3 %collective-permute-start.12 = (f32[4,1,256]{2,0,1:T(4,128)S(1)}, f32[4,1,256]{2,0,1:T(4,128)S(1)}, u32[]{:S(2)}, u32[]{:S(2)}) collective-permute-start(f32[4,1,256]{2,0,1:T(4,128)S(1)} %get-tuple-element.47), channel_id=1, source_target_pairs={{0,128},{1,129},{2,130},{3,131},{4,132},{5,133},{6,134},{7,135},{8... | collective-permute-start | bytes 12296 | tf_op jit(solution)/shard_map/ppermute | solution.py:26
  145.8 7.0 %collective-permute-start.13 = (f32[4,1,256]{2,0,1:T(4,128)S(1)}, f32[4,1,256]{2,0,1:T(4,128)S(1)}, u32[]{:S(2)}, u32[]{:S(2)}) collective-permute-start(f32[4,1,256]{2,0,1:T(4,128)S(1)} %get-tuple-element.46), channel_id=1, source_target_pairs={{128,0},{129,1},{130,2},{131,3},{132,4},{133,5},{134,6},{135,7},{1... | collective-permute-start | bytes 12296 | tf_op jit(solution)/shard_map/ppermute | solution.py:29
  155.6 9.4 %collective-permute-start.14 = (f32[4,290,1]{1,0,2:T(4,128)S(1)}, f32[4,290,1]{1,0,2:T(4,128)}, u32[]{:S(2)}, u32[]{:S(2)}) collective-permute-start(f32[4,290,1]{1,0,2:T(4,128)S(1)} %copy.57), channel_id=1, source_target_pairs={{0,32},{32,64},{64,96},{1,33},{33,65},{65,97},{2,34},{34,66},{66,9... | collective-permute-start | bytes 13928 | tf_op jit(solution)/shard_map/ppermute | solution.py:26
  159.4 7.3 %collective-permute-start.15 = (f32[4,290,1]{1,0,2:T(4,128)}, f32[4,290,1]{1,0,2:T(4,128)}, u32[]{:S(2)}, u32[]{:S(2)}) collective-permute-start(f32[4,290,1]{1,0,2:T(4,128)} %copy.58), channel_id=1, source_target_pairs={{32,0},{64,32},{96,64},{33,1},{65,33},{97,65},{34,2},{66,34},{98,6... | collective-permute-start | bytes 13928 | tf_op jit(solution)/shard_map/ppermute | solution.py:29
  173.5 2.8 %collective-permute-start.17 = (f32[1,290,258]{2,0,1:T(1,128)S(1)}, f32[1,290,258]{2,0,1:T(1,128)S(1)}, u32[]{:S(2)}, u32[]{:S(2)}) collective-permute-start(f32[1,290,258]{2,0,1:T(1,128)S(1)} %get-tuple-element.35), channel_id=1, source_target_pairs={{0,1},{1,2},{2,3},{3,4},{4,5},{5,6},{6,7},{7,8},{8,9},{9,10},{10,1... | collective-permute-start | bytes 897848 | tf_op jit(solution)/shard_map/ppermute | solution.py:26
  174.8 6.3 %collective-permute-start.16 = (f32[1,290,258]{2,0,1:T(1,128)S(1)}, f32[1,290,258]{2,0,1:T(1,128)S(1)}, u32[]{:S(2)}, u32[]{:S(2)}) collective-permute-start(f32[1,290,258]{2,0,1:T(1,128)S(1)} %get-tuple-element.34), channel_id=1, source_target_pairs={{1,0},{2,1},{3,2},{4,3},{5,4},{6,5},{7,6},{8,7},{9,8},{10,9},{11,1... | collective-permute-start | bytes 897848 | tf_op jit(solution)/shard_map/ppermute | solution.py:29
  181.2 11.5 %slice-start.2 = ((s8[4718592]{0:T(1024)(128)(4,1)}), s8[4194304]{0:T(1024)(128)(4,1)S(1)}, s32[]{:S(2)}) async-start(s8[4718592]{0:T(1024)(128)(4,1)} %bitcast.44), calls=%async_computation.4 | async-start | bytes 8388608
  200.2 67.1 %copy-start.6 = (f32[4,288,256]{2,0,1:T(4,128)S(1)}, f32[4,288,256]{2,0,1:T(4,128)}, u32[]{:S(2)}) copy-start(f32[4,288,256]{2,0,1:T(4,128)} %get-tuple-element.21) | copy-start | bytes 3538948
  201.5 57.9 %all-to-all-start = ((f32[32,80,128]{2,1,0:T(8,128)}), f32[32,80,128]{2,1,0:T(8,128)S(1)}, u32[]{:S(2)}, u32[]{:S(2)}) async-start(f32[32,80,128]{2,1,0:T(8,128)} %pad_maximum_fusion.11), calls=%async_computation | async-start | bytes 2621440 | tf_op jit(solution)/shard_map/all_to_all | solution.py:202
  259.4 13.1 %copy-start.2 = (f32[32,80,128]{2,1,0:T(8,128)}, f32[32,80,128]{2,1,0:T(8,128)S(1)}, u32[]{:S(2)}) copy-start(f32[32,80,128]{2,1,0:T(8,128)S(1)} %all-to-all-done.got_ref) | copy-start | bytes 3932164
  260.1 12.3 %all-to-all-start.1 = ((f32[8,32,128]{2,1,0:T(8,128)}), f32[8,32,128]{2,1,0:T(8,128)S(1)}, u32[]{:S(2)}, u32[]{:S(2)}) async-start(f32[8,32,128]{2,1,0:T(8,128)} %broadcast_in_dim.62), calls=%async_computation.1 | async-start | bytes 262144 | tf_op jit(solution)/shard_map/all_to_all | solution.py:204
  (19 other events, 95.2 us)

commit v2 on v1

v2 whole, which is shorter than its diff:
```python
import functools

import jax
import jax.numpy as jnp
from jax import lax
from jax.experimental import pallas as pl
from jax.experimental.pallas import tpu as pltpu
from jax.sharding import PartitionSpec as P

PASSES = 3


relax_rate = 0.8
smooth_weight = 0.5
smooth_floor = 0.25
shrink_level = 0.4
dual_scale = 0.8
ridge_share = 0.1


HIGHEST = lax.Precision.HIGHEST


def iota(shape, dim):
    return lax.broadcasted_iota(jnp.int32, shape, dim)


def dot(a, b):
    return jnp.dot(a, b, precision=HIGHEST, preferred_element_type=jnp.float32)


def eliminated(matrix):
    n = matrix.shape[0]
    wide = (n, 128)
    lanes, rows = iota(wide, 1), iota(wide, 0)
    work = jnp.concatenate([matrix, jnp.zeros((n, 128 - n), jnp.float32)], axis=1)
    work = work + jnp.where(lanes == rows + n, 1.0, 0.0)
    for k in range(n):
        column = jnp.broadcast_to(work[:, k : k + 1], wide)
        pivot = jnp.broadcast_to(work[k : k + 1, :], wide)
        scaled = pivot / jnp.broadcast_to(column[k : k + 1, :], wide)
        work = jnp.where(rows == k, scaled, work - column * scaled)
    return work[:, n : 2 * n]


def spread_ranks(rank, width):
    return jnp.where(iota((width, rank), 0) % rank == iota((width, rank), 1), 1.0, 0.0)


def spread_blocks(block, width, count):
    rank = block.shape[0]
    pick = spread_ranks(rank, width)
    full = dot(dot(pick, block), pick.T)
    a, b = iota((width, width), 0) // rank, iota((width, width), 1) // rank
    return jnp.where((a == b) & (a < count), full, 0.0)


def final_kernel(pixel_ridge, ridge, slot_ref, got_ref, parts_ref, old_ref, basis_ref, coeff_ref, coeff_all):
    slots = got_ref.shape[0]
    rows_owned = old_ref.shape[0]
    rank = basis_ref.shape[1]
    total = parts_ref[0]
    for peer in range(1, parts_ref.shape[0]):
        total = total + parts_ref[peer]
    eye = jnp.where(iota((rank, rank), 0) == iota((rank, rank), 1), 1.0, 0.0)
    inverse = eliminated(total[slots:, 0:rank] + pixel_ridge * eye)
    coeff = dot(total[0:slots], spread_blocks(inverse, 128, 4))
    coeff_all[...] = coeff
    mine = coeff_all[pl.ds(slot_ref[0], 1), :]
    for f in range(4):
        coeff_ref[f : f + 1, :] = mine[:, f * rank : (f + 1) * rank]
    width = 128
    coeff_t = coeff.T
    full = dot(coeff_t, coeff)
    a, b = iota((width, width), 0) // rank, iota((width, width), 1) // rank
    pick = spread_ranks(rank, width)
    gram = dot(dot(pick.T, jnp.where(a == b, full, 0.0)), pick)
    inverse = eliminated(gram + ridge * eye)
    lines = 8 * slots
    repeat = jnp.where(iota((slots, lines), 0) == iota((slots, lines), 1) // 8, 1.0, 0.0)
    wide = dot(coeff_t, repeat)
    wide = jnp.where(
        iota((width, lines), 0) // rank == iota((width, lines), 1) % 4, wide, 0.0
    )
    twice = spread_ranks(rank, 2 * rank)
    mix = dot(dot(twice, inverse), pick.T)
    factor = jnp.where(
        iota((2 * rank, lines), 0) // rank == (iota((2 * rank, lines), 1) // 4) % 2, dot(mix, wide), 0.0
    )
    old_factor = ridge * spread_blocks(inverse, 2 * rank, 2)
    for i in range(rows_owned):
        block = got_ref[:, 8 * i : 8 * (i + 1), :].reshape(lines, 128)
        rows = dot(factor, block) + dot(old_factor, old_ref[i])
        for half in range(2):
            basis_ref[i, :, half * 128 : (half + 1) * 128] = rows[half * rank : (half + 1) * rank]


HALO = 3
GROUP = 12
TOP = 8
FLOOR, SMOOTH, RELAX = smooth_floor, smooth_weight, relax_rate


def lane_of(rows):
    return iota((rows, 128), 1)


def in_lanes(lanes, first, count):
    first = first % 128
    if first + count <= 128:
        return (lanes >= first) & (lanes < first + count)
    return (lanes >= first) | (lanes < first + count - 128)


def goal_rows(coeff, video, multiplier, basis, at):
    frames, rank = video.shape[0], basis.shape[0]
    sums = [None] * frames
    for r in range(rank):
        image = basis[r, at, :]
        for f in range(frames):
            term = coeff[f, r] * image
            sums[f] = term if r == 0 else sums[f] + term
    return [video[f, at, :] - sums[f] + dual_scale * multiplier[f, at, :] for f in range(frames)]


def edge_kernel(place, coeff, video, multiplier, basis, current, edge, *scratch):
    buffers, sems = scratch[:-1], scratch[-1]
    frames, rows, _ = video.shape
    at = pl.ds(pl.multiple_of((1 - place[0]) * (rows - 8), 8), 8)
    near = [
        pltpu.make_async_copy(ref.at[:, at, :], buf, sems.at[k])
        for k, (ref, buf) in enumerate(zip((video, multiplier, basis, current), buffers))
    ]
    for c in near:
        c.start()
    for c in near:
        c.wait()
    video, multiplier, basis, current = buffers
    edge[0] = current[...]
    for f, value in enumerate(goal_rows(coeff, video, multiplier, basis, slice(0, 8))):
        edge[1, f] = value


def target_kernel(
    coeff, video_in, multiplier_in, basis_in, current, up, down, video, multiplier, basis, low, high, sems
):
    frames, rows, _ = video.shape
    pieces, chunk = sems.shape[1], 16
    piece = rows // pieces
    waits = []
    for p in range(pieces):
        at = pl.ds(p * piece, piece)
        for k, (ref, buf) in enumerate(((basis_in, basis), (video_in, video), (multiplier_in, multiplier))):
            c = pltpu.make_async_copy(ref.at[:, at, :], buf.at[:, at, :], sems.at[k, p])
            c.start()
            waits.append(c)
    outs = [
        pltpu.make_async_copy(current.at[pl.ds(frames - HALO, HALO)], up.at[pl.ds(0, HALO)], sems.at[5, 0]),
        pltpu.make_async_copy(current.at[pl.ds(0, HALO)], down.at[pl.ds(0, HALO)], sems.at[5, 1]),
    ]
    for c in outs:
        c.start()
    for p in range(pieces):
        for c in waits[3 * p : 3 * p + 3]:
            c.wait()

        def body(c, carry):
            at = pl.ds(pl.multiple_of(p * piece + c * chunk, chunk), chunk)
            goals = goal_rows(coeff, video, multiplier, basis, at)
            for f in range(frames):
                (low if f < 2 else high)[f % 2, at, :] = goals[f]
            return carry

        lax.fori_loop(0, piece // chunk, body, 0)
        at = pl.ds(p * piece, piece)
        for k, (buf, ref) in enumerate(((low, down), (high, up))):
            c = pltpu.make_async_copy(buf.at[:, at, :], ref.at[pl.ds(HALO, 2), at, :], sems.at[3 + k, p])
            c.start()
            outs.append(c)
    for c in outs:
        c.wait()


def strips_kernel(current, up, down, edge, right, left):
    frames, rows, _ = current.shape
    sources = [(current, f, HALO * GROUP + GROUP * f, 0, f) for f in range(frames)]
    sources += [
        (down if f < 2 else up, HALO + f % 2, HALO * GROUP + GROUP * (f + frames), 1, f) for f in range(frames)
    ]

    def gather(out_at, count, pick):
        lanes = lane_of(count)
        a = jnp.zeros((count, 128), jnp.float32)
        b = a
        for ref, index, base, kind, f in sources:
            first, last = pick(ref, index, kind, f)
            both = jnp.where(lanes < 64, first, last)
            here = in_lanes(lanes, base, GROUP)
            a = jnp.where(here, pltpu.roll(both, (base + 3) % 128, 1), a)
            b = jnp.where(here, pltpu.roll(both, (base + 8) % 128, 1), b)
        right[out_at, :] = a
        left[out_at, :] = b

    def body(c, carry):
        at = pl.ds(pl.multiple_of(c * 32, 32), 32)
        out_at = pl.ds(pl.multiple_of(c * 32 + TOP, 8), 32)
        gather(out_at, 32, lambda ref, i, kind, f: (ref[i, at, 0:128], ref[i, at, 128:256]))
        return carry

    lax.fori_loop(0, rows // 32, body, 0)
    for out_at in (pl.ds(0, 8), pl.ds(rows + TOP, 8)):
        gather(out_at, 8, lambda ref, i, kind, f: (edge[kind, f, :, 0:128], edge[kind, f, :, 128:256]))


def ring_kernel(right, left, from_left, from_right, edge, out):
    rows = right.shape[0]
    lanes = lane_of(rows)
    k = (lanes + 128 - HALO * GROUP) % 128 % GROUP
    out[0:rows, :] = jnp.where(
        k <= 2,
        from_left[...],
        jnp.where(k <= 5, right[...], jnp.where(k <= 7, left[...], from_right[...])),
    )
    flat = edge.reshape(edge.shape[0] * edge.shape[1] * 8, 256)
    for half in range(2):
        at = rows + half * flat.shape[0]
        out[at : at + flat.shape[0], :] = flat[:, half * 128 : (half + 1) * 128]


def sweep_kernel(
    ridge_part,
    slot_count,
    col_count,
    place,
    current,
    before,
    after,
    up,
    down,
    ring,
    ring_before,
    ring_after,
    video,
    multiplier,
    basis,
    coeff,
    shrunk_out,
    sent,
    s_a,
    s_b,
    goal,
    strip_a,
    strip_b,
    strip_goal,
    strip_flux,
    flux_f,
    own_video,
    own_multiplier,
    own_basis,
    residual,
    out,
    sums,
    sems,
):
    frames, rows, _ = current.shape
    all_rows = rows + 2 * TOP
    rank = basis.shape[0]
    row, col, slot = place[0], place[1], place[2]
    copies = []

    def copy(src, dst):
        c = pltpu.make_async_copy(src, dst, sems.at[len(copies)])
        c.start()
        copies.append(c)
        return c

    own_at = pl.ds(TOP, rows)
    strip_chunks = [(c, min(80, all_rows - c)) for c in range(0, all_rows, 80)]
    first = []
    for half in range(2):
        at = pl.ds(half * 128, 128)
        for src, at_frame, count in ((before, 0, HALO), (current, HALO, frames), (after, HALO + frames, HALO)):
            first.append(copy(src.at[pl.ds(0, count), :, at], s_a.at[pl.ds(at_frame, count), half, own_at, :]))
        for src, at_frame in ((before, 0), (down, 2), (up, 4), (after, 6)):
            first.append(copy(src.at[pl.ds(HALO, 2), :, at], goal.at[pl.ds(at_frame, 2), half, own_at, :]))
    later = [copy(video, own_video), copy(multiplier, own_multiplier), copy(basis, own_basis)]

    for c, count in strip_chunks:
        at = slice(c, c + count)
        lanes = lane_of(count)
        mine, prev, nxt = ring[at, :], ring_before[at, :], ring_after[at, :]
        strip_a[at, :] = jnp.where(
            lanes < 36, pltpu.roll(prev, 80, 1), jnp.where(lanes < 84, mine, pltpu.roll(nxt, 48, 1))
        )
        strip_goal[at, :] = jnp.where(
            lanes < 36, pltpu.roll(prev, 32, 1), jnp.where(lanes < 84, pltpu.roll(mine, 80, 1), nxt)
        )
    zero8 = jnp.zeros((8, 128), jnp.float32)
    for buf in (strip_a, strip_b):
        buf[pl.ds(all_rows, 8), :] = zero8
    for half in range(2):
        for g in range(2 * HALO + frames):
            if g < HALO:
                src, f = ring_before, g + 1
            elif g < HALO + frames:
                src, f = ring, g - HALO
            else:
                src, f = ring_after, g - HALO - frames
            base = all_rows + half * 64
            tile = src[base + 8 * f : base + 8 * f + 8, :]
            s_a[g, half, 0:TOP, :] = tile
            s_a[g, half, pl.ds(TOP + rows, 8), :] = tile
            s_a[g, half, pl.ds(all_rows, 8), :] = zero8
            s_b[g, half, pl.ds(all_rows, 8), :] = zero8
            if 1 <= g <= 2 * HALO + frames - 2:
                tile = src[base + 32 + 8 * f : base + 32 + 8 * f + 8, :]
                goal[g - 1, half, 0:TOP, :] = tile
                goal[g - 1, half, pl.ds(TOP + rows, 8), :] = tile

    def first_row_last(value, count):
        return value[count - 1 : count, :]

    def down_one(value, carry, count):
        moved = pltpu.roll(value, 1, 0)
        return jnp.where(iota((count, 128), 0) == 0, jnp.broadcast_to(carry, (count, 128)), moved)

    def strip_sweep(old, new, flux_at):
        for c, count in strip_chunks:
            lanes = lane_of(count)
            k = lanes % GROUP
            s = old[c : c + count, :]
            s = jnp.where((slot == 0) & in_lanes(lanes, 24, 12), pltpu.roll(s, 116, 1), s)
            s = jnp.where((slot == slots_end) & in_lanes(lanes, 84, 12), pltpu.roll(s, 12, 1), s)
            s = jnp.where((col == 0) & (k == 2), pltpu.roll(s, 127, 1), s)
            s = jnp.where((col == cols_end) & (k == 8), pltpu.roll(s, 1, 1), s)
            old[c : c + count, :] = s

        @pl.when(row == 0)
        def _():
            old[TOP - 1 : TOP, :] = old[TOP : TOP + 1, :]

        @pl.when(row == 1)
        def _():
            old[TOP + rows : TOP + rows + 1, :] = old[TOP + rows - 1 : TOP + rows, :]

        carry = jnp.zeros((1, 128), jnp.float32)
        for c, count in strip_chunks:
            s = old[c : c + count, :]
            pf = pltpu.roll(s, 116, 1) - s
            pr = old[c + 1 : c + 1 + count, :] - s
            pc = pltpu.roll(s, 127, 1) - s
            weight = lax.rsqrt(FLOOR + pf * pf + pr * pr + pc * pc)
            ff, fr, fc = pf * weight, pr * weight, pc * weight
            strip_flux[flux_at, c : c + count, :] = fc
            spread = (
                (ff - pltpu.roll(ff, 12, 1)) + (fr - down_one(fr, carry, count)) + (fc - pltpu.roll(fc, 1, 1))
            )
            carry = first_row_last(fr, count)
            new[c : c + count, :] = s + RELAX * (strip_goal[c : c + count, :] - s + SMOOTH * spread)

    slots_end, cols_end = slot_count - 1, col_count - 1
    strip_sweep(strip_a, strip_b, 0)

    for c in first:
        c.wait()

    chunks = [(c, min(32, all_rows - c)) for c in range(0, all_rows, 32)]

    def edges(old):
        @pl.when(slot == 0)
        def _():
            old[HALO - 1] = old[HALO]

        @pl.when(slot == slots_end)
        def _():
            old[HALO + frames] = old[HALO + frames - 1]

        @pl.when(row == 0)
        def _():
            for g in range(2 * HALO + frames):
                for half in range(2):
                    old[g, half, TOP - 1 : TOP, :] = old[g, half, TOP : TOP + 1, :]

        @pl.when(row == 1)
        def _():
            end = TOP + rows
            for g in range(2 * HALO + frames):
                for half in range(2):
                    old[g, half, end : end + 1, :] = old[g, half, end - 1 : end, :]

    last_keep = jnp.where((lane_of(8)[0:1] == 127) & (col == cols_end), 0.0, 1.0)

    def main_sweep(old, new, strip, flux_at, g_first, g_count):
        edges(old)

        def body(i, carry0):
            g = g_first + i
            turn_ahead = (119 + 12 * 128 - 12 * g) % 128
            turn_flux = (128 * 12 - 2 - 12 * g) % 128
            goal_at = jnp.maximum(g - 1, 0)
            carry = [jnp.zeros((1, 128), jnp.float32)] * 2
            for c, count in chunks:
                lanes = lane_of(count)
                at = pl.ds(c, count)
                next_at = pl.ds(c + 1, count)
                s = [old[g, half, at, :] for half in range(2)]
                turned = [pltpu.roll(x, 127, 1) for x in s]
                outside = pltpu.roll(strip[at, :], turn_ahead, 1)
                ahead = [
                    jnp.where(lanes == 127, turned[1], turned[0]),
                    jnp.where(lanes == 127, outside, turned[1]),
                ]
                fc, fr, ff = [], [], []
                for half in range(2):
                    x = s[half]
                    pf = old[g + 1, half, at, :] - x
                    pr = old[g, half, next_at, :] - x
                    pc = ahead[half] - x
                    if half == 1:
                        pc = pc * last_keep
                    weight = lax.rsqrt(FLOOR + pf * pf + pr * pr + pc * pc)
                    ff.append(pf * weight)
                    fr.append(pr * weight)
                    fc.append(pc * weight)
                outside = pltpu.roll(strip_flux[flux_at, at, :], turn_flux, 1)
                turned = [pltpu.roll(x, 1, 1) for x in fc]
                behind = [
                    jnp.where(lanes == 0, outside, turned[0]),
                    jnp.where(lanes == 0, turned[0], turned[1]),
                ]
                for half in range(2):
                    x = s[half]
                    spread = (
                        (ff[half] - flux_f[half, at, :])
                        + (fr[half] - down_one(fr[half], carry[half], count))
                        + (fc[half] - behind[half])
                    )
                    flux_f[half, at, :] = ff[half]
                    new[g, half, at, :] = x + RELAX * (goal[goal_at, half, at, :] - x + SMOOTH * spread)
                carry = [first_row_last(x, count) for x in fr]
            return carry0

        lax.fori_loop(0, g_count, body, 0)

    main_sweep(s_a, s_b, strip_a, 0, 0, 9)
    strip_sweep(strip_b, strip_a, 1)
    main_sweep(s_b, s_a, strip_b, 1, 1, 7)
    strip_sweep(strip_a, strip_b, 2)
    main_sweep(s_a, s_b, strip_a, 2, 2, 5)

    for c in later:
        c.wait()
    sums[...] = jnp.zeros_like(sums)

    def finish(c, carry):
        chunk = 16
        at = pl.ds(pl.multiple_of(c * chunk, chunk), chunk)
        in_at = pl.ds(pl.multiple_of(c * chunk + TOP, 8), chunk)
        parts = []
        for f in range(frames):
            for half in range(2):
                cols = slice(half * 128, (half + 1) * 128)
                s = s_b[HALO + f, half, in_at, :]
                shrunk = s - jnp.clip(s, -shrink_level, shrink_level)
                out[f, at, cols] = shrunk
                r = own_video[f, at, cols] + dual_scale * own_multiplier[f, at, cols] - shrunk
                residual[half * frames + f, at, :] = r
                parts.append(r)
        for r in range(rank):
            images = [own_basis[r, at, half * 128 : (half + 1) * 128] for half in range(2)]
            for f in range(frames):
                term = images[0] * parts[2 * f] + images[1] * parts[2 * f + 1]
                sums[f * rank + r] += term[0:8] + term[8:16]
        return carry

    lax.fori_loop(0, rows // 16, finish, 0)
    done = copy(out, shrunk_out)
    lines = jnp.sum(sums[...], axis=1)
    total = lax.dot_general(
        jnp.ones((8, 128), jnp.float32),
        lines,
        (((1,), (1,)), ((), ())),
        precision=HIGHEST,
        preferred_element_type=jnp.float32,
    )
    cross = jnp.concatenate([total + ridge_part * coeff[...], jnp.zeros((8, 64), jnp.float32)], axis=1)
    chunk_rows = sent.shape[1]
    owned = rows // slot_count
    flat = sent.reshape(sent.shape[0] * chunk_rows, 128)

    def pack(j, carry):
        for f in range(frames):
            for half in range(2):
                flat[pl.ds(j * chunk_rows + half * frames + f, owned, stride=8), :] = residual[
                    half * frames + f, pl.ds(j * owned, owned), :
                ]
        sent[j, pl.ds(owned * 8, 8), :] = cross
        return carry

    lax.fori_loop(0, slot_count, pack, 0)
    done.wait()


def gram_kernel(slot, basis, out, old, sums, window):
    rank, rows, _ = basis.shape
    sums[...] = jnp.zeros_like(sums)

    def body(c, carry):
        at = pl.ds(pl.multiple_of(c * 8, 8), 8)
        images = [[basis[r, at, half * 128 : (half + 1) * 128] for half in range(2)] for r in range(rank)]
        for r in range(rank):
            for q in range(r, rank):
                sums[r * rank + q] += images[r][0] * images[q][0] + images[r][1] * images[q][1]
        return carry

    lax.fori_loop(0, rows // 8, body, 0)
    owned = old.shape[0]
    start = pl.multiple_of(slot[0] * owned // 8 * 8, 8)
    shift = slot[0] * owned - start
    flat = old.reshape(owned * 2 * rank, 128)
    for half in range(2):
        for r in range(rank):
            window[half * rank + r] = basis[r, pl.ds(start, 16), half * 128 : (half + 1) * 128]
            flat[pl.ds(half * rank + r, owned, stride=2 * rank), :] = window[half * rank + r, pl.ds(shift, owned), :]
    ones = jnp.ones((128, 128), jnp.float32)
    for r in range(rank):
        lines = jnp.concatenate(
            [jnp.sum(sums[min(r, q) * rank + max(r, q)], axis=0, keepdims=True) for q in range(rank)], axis=0
        )
        totals = dot(lines, ones)
        picked = jnp.where(iota((rank, 128), 0) == iota((rank, 128), 1), totals, 0.0)
        out[r : r + 1, :] = jnp.sum(picked, axis=0, keepdims=True)


def vmem(count):
    return [pl.BlockSpec(memory_space=pltpu.VMEM)] * count


def smem():
    return pl.BlockSpec(memory_space=pltpu.SMEM)


def anywhere(count):
    return [pl.BlockSpec(memory_space=pltpu.HBM)] * count


def floats(*shape):
    return jax.ShapeDtypeStruct(shape, jnp.float32)


LARGE = pltpu.CompilerParams(vmem_limit_bytes=48 * 1024 * 1024)


def local(video, multiplier, foreground, basis, coefficients):
    frames, rows, cols = video.shape
    rank = basis.shape[0]
    frame_count = lax.axis_size("frame")
    row_count = lax.axis_size("row")
    col_count = lax.axis_size("col")
    blocks = row_count * col_count
    frame_slot = lax.axis_index("frame")
    place = jnp.stack([lax.axis_index("row"), lax.axis_index("col"), frame_slot])
    all_rows = rows + 2 * TOP
    to_next = [(i, i + 1) for i in range(frame_count - 1)]
    to_previous = [(b, a) for a, b in to_next]
    to_right = [(i, i + 1) for i in range(col_count - 1)]
    to_left = [(b, a) for a, b in to_right]

    edge = pl.pallas_call(
        edge_kernel,
        out_shape=floats(2, frames, 8, cols),
        in_specs=[smem(), smem()] + anywhere(4),
        out_specs=vmem(1)[0],
        scratch_shapes=[pltpu.VMEM((n, 8, cols), jnp.float32) for n in (frames, frames, rank, frames)]
        + [pltpu.SemaphoreType.DMA((4,))],
        name="edge",
    )(place, coefficients, video, multiplier, basis, foreground)
    edge = lax.ppermute(edge, "row", [(0, 1), (1, 0)])
    up, down = pl.pallas_call(
        target_kernel,
        out_shape=(floats(HALO + 2, rows, cols), floats(HALO + 2, rows, cols)),
        in_specs=[smem()] + anywhere(4),
        out_specs=anywhere(2),
        scratch_shapes=[pltpu.VMEM(s, jnp.float32) for s in (video.shape, video.shape, basis.shape)]
        + [pltpu.VMEM((2, rows, cols), jnp.float32)] * 2
        + [pltpu.SemaphoreType.DMA((6, 6))],
        compiler_params=LARGE,
        name="target",
    )(coefficients, video, multiplier, basis, foreground)
    up, down, edge = lax.optimization_barrier((up, down, edge))
    before = lax.ppermute(up, "frame", to_next)
    after = lax.ppermute(down, "frame", to_previous)
    right, left = pl.pallas_call(
        strips_kernel,
        out_shape=(floats(all_rows, 128), floats(all_rows, 128)),
        in_specs=vmem(4),
        out_specs=vmem(2),
        compiler_params=LARGE,
        name="strips",
    )(foreground, up, down, edge)
    from_left = lax.ppermute(right, "col", to_right)
    from_right = lax.ppermute(left, "col", to_left)
    ring = pl.pallas_call(
        ring_kernel,
        out_shape=floats(all_rows + 128, 128),
        in_specs=vmem(5),
        out_specs=vmem(1)[0],
        compiler_params=LARGE,
        name="ring",
    )(right, left, from_left, from_right, edge)
    ring_before = lax.ppermute(ring, "frame", to_next)
    ring_after = lax.ppermute(ring, "frame", to_previous)

    pixel_ridge = ridge_share * rows * cols * blocks
    owned_rows = rows // frame_count
    main = (2 * HALO + frames, 2, all_rows + 8, 128)
    strip = (all_rows + 8, 128)
    scratch = [
        main,
        main,
        (2 * HALO + frames - 2, 2, all_rows, 128),
        strip,
        strip,
        (all_rows, 128),
        (3, all_rows, 128),
        (2, all_rows, 128),
        video.shape,
        video.shape,
        basis.shape,
        (2 * frames, rows, 128),
        video.shape,
        (frames * rank, 8, 128),
    ]
    shrunk, sent = pl.pallas_call(
        functools.partial(sweep_kernel, pixel_ridge / blocks, frame_count, col_count),
        out_shape=(floats(frames, rows, cols), floats(frame_count, owned_rows * 8 + 8, 128)),
        in_specs=[smem()] + anywhere(5) + vmem(3) + anywhere(3) + vmem(1),
        out_specs=anywhere(1) + vmem(1),
        scratch_shapes=[pltpu.VMEM(s, jnp.float32) for s in scratch] + [pltpu.SemaphoreType.DMA((18,))],
        compiler_params=LARGE,
        name="sweeps",
    )(
        place,
        foreground,
        before,
        after,
        up,
        down,
        ring,
        ring_before,
        ring_after,
        video,
        multiplier,
        basis,
        coefficients.reshape(1, frames * rank),
    )
    got = lax.all_to_all(sent, "frame", 0, 0, tiled=True)
    basis, _ = lax.optimization_barrier((basis, sent))
    gram, old_owned = pl.pallas_call(
        gram_kernel,
        out_shape=(floats(rank, 128), floats(owned_rows, 2 * rank, 128)),
        in_specs=[smem()] + vmem(1),
        out_specs=vmem(2),
        scratch_shapes=[
            pltpu.VMEM((rank * rank, 8, 128), jnp.float32),
            pltpu.VMEM((2 * rank, 16, 128), jnp.float32),
        ],
        compiler_params=LARGE,
        name="gram",
    )(frame_slot.reshape(1), basis)
    parts = jnp.concatenate([got[:, owned_rows * 8, :], gram], axis=0)
    parts = lax.all_to_all(jnp.broadcast_to(parts[None], (blocks, *parts.shape)), ("row", "col"), 0, 0, tiled=True)
    frame_ridge = ridge_share * frames * frame_count
    new_basis, new_coeff = pl.pallas_call(
        functools.partial(final_kernel, pixel_ridge, frame_ridge),
        out_shape=(floats(owned_rows, rank, cols), floats(frames, rank)),
        in_specs=[smem()] + vmem(3),
        out_specs=vmem(2),
        scratch_shapes=[pltpu.VMEM((frame_count, 128), jnp.float32)],
        compiler_params=LARGE,
        name="final",
    )(frame_slot.reshape(1), got, parts, old_owned)
    return shrunk, new_coeff, new_basis.transpose(1, 0, 2)


def solution(mesh):
    placed = (
        P("frame", "row", "col"),
        P("frame", "row", "col"),
        P("frame", "row", "col"),
        P(None, "row", "col"),
        P("frame", None),
    )
    return jax.shard_map(
        local,
        mesh=mesh,
        in_specs=placed,
        out_specs=(P("frame", "row", "col"), P("frame", None), P(None, ("row", "frame"), "col")),
        check_vma=False,
    )
```

time: 287 us -> 139 us (0.48); the launches traced: 281 us -> 138 us
  other arithmetic: 50.4 us -> 0.59 us
  matrix products: 35.6 us -> 0 us
  starting transfers between devices: 76.1 us -> 43.4 us
  Pallas kernels: 9.93 us -> 41.5 us
  waiting for transfers between devices: 62.1 us -> 34.8 us
  local copies, waits for them, and re-layouts: 24.8 us -> 4.9 us
  blocking collectives: 20.9 us -> 12.2 us
    dot_general x3 -> x0, matrix products: 35.6 us -> none  [the longest x1 14.8 us: local(): jnp.dot(flat_basis, flat_basis.T, precision=highest)]
    pallas_call x2 -> x7, Pallas kernels: 9.93 us -> 41.5 us  [the longest x1 19.4 us: local(): pl.pallas_call(functools.partial(sweep_kernel, pixel_ridge / blocks, fram...]
    ppermute x18 -> x7, starting transfers between devices: 46.9 us -> 18 us  [the longest x1 3.72 us: local(): ring_before = lax.ppermute(ring, 'frame', to_next)]
    psum x1 -> x0, blocking collectives: 20.9 us -> none  [local(): lax.psum(jnp.dot(flat_basis, flat_basis.T, precision=highest), ('row', 'c...]
    mul x6 -> x0, other arithmetic: 20.3 us -> none  [descend(): fluxes = [slope_part * weight for slope_part in slopes]]
    ppermute x18 -> x7, waiting for transfers between devices: 24.1 us -> 6.89 us  [the longest x1 3.44 us: local(): from_right = lax.ppermute(left, 'col', to_left)]
    slice x3 -> x0, other arithmetic: 14.1 us -> none  [with_halo(): lax.slice_in_dim(block, 0, width, axis=dim)]
    all_to_all x0 -> x1, blocking collectives: none -> 12.2 us  [local(): lax.all_to_all(jnp.broadcast_to(parts[None], (blocks, *parts.shape)), ('r...]
  transfers between devices with their start and end apart: 20 -> 8, of which waited for: 9 -> 4; matrix products, arithmetic and copies ran while one was open for 11% -> 0% of each run, Pallas kernels for 1% -> 9%
where the time goes in v2:
time: 139 us; the launch traced here: 138 us
  starting transfers between devices  43.4 us (31%)
  Pallas kernels  41.5 us (30%)
  waiting for transfers between devices  34.8 us (25%)
  blocking collectives  12.2 us (9%)
  local copies, waits for them, and re-layouts  4.9 us (4%)
    all_to_all x1, waiting for transfers between devices, local(): got = lax.all_to_all(sent, 'frame', 0, 0, tiled=True)  27.9 us
    all_to_all x1, starting transfers between devices, local(): got = lax.all_to_all(sent, 'frame', 0, 0, tiled=True)  25.4 us
    pallas_call x1, Pallas kernels, local(): pl.pallas_call(functools.partial(sweep_kernel, pixel_ridge / blocks, fram...  19.4 us
    all_to_all x1, blocking collectives, local(): lax.all_to_all(jnp.broadcast_to(parts[None], (blocks, *parts.shape)), ('r...  12.2 us
    pallas_call x1, Pallas kernels, local(): pl.pallas_call(functools.partial(final_kernel, pixel_ridge, frame_ridge),...  7.05 us
    pallas_call x1, Pallas kernels, local(): pl.pallas_call(target_kernel, out_shape=(floats(HALO + 2, rows, cols), fl...  5.16 us
    unnamed x16, local copies, waits for them, and re-layouts  4.79 us
    pallas_call x1, Pallas kernels, local(): pl.pallas_call(gram_kernel, out_shape=(floats(rank, 128), floats(owned_ro...  3.77 us
  transfers between devices with their start and end apart: 8, of which 4 were waited for; matrix products, arithmetic and copies ran while one was open for 0% of the time, Pallas kernels for 9%

profile of v2, /device:TPU:2, one launch (start us, length us, event | category | flops | bytes accessed | tf_op | source)
XLA Modules:
  0.0 138.2 jit_solution(12451959160908340966)
XLA Ops:
  0.6 0.6 pad_add_fusion.place
  1.2 2.7 %edge.1 = f32[2,4,8,256]{3,2,1,0:T(8,128)} custom-call(s32[3]{0:T(128)} %pad_add_fusion.place, f32[4,16]{1,0:T(4,128)} %coeff.3, f32[4,288,256]{2,1,0:T(8,128)} %video.3, f32[4,288,256]{2,1,0:T(8,128)} %multiplier.3, f32[16,288,256]{2,1,0:T(8,128)} %basis.4, f32[4,288,256]{2,1,0:T(8,128)} %current.7), custom_call_target="tpu_custom_call" | custom-call | tf_op jit(solution)/shard_map/edge/pallas_call | solution.py:569
  4.0 3.3 %collective-permute-start = (f32[2,4,8,256]{3,2,1,0:T(8,128)}, f32[2,4,8,256]{3,2,1,0:T(8,128)S(1)}, u32[]{:S(2)}, u32[]{:S(2)}) collective-permute-start(f32[2,4,8,256]{3,2,1,0:T(8,128)} %edge.1), channel_id=1, source_target_pairs={{0,128},{128,0},{1,129},{129,1},{2,130},{130,2},{3,131},{131,3},{4... | collective-permute-start | bytes 196616 | tf_op jit(solution)/shard_map/ppermute | solution.py:578
  7.3 5.2 %target.1 = (f32[5,288,256]{2,1,0:T(8,128)}, f32[5,288,256]{2,1,0:T(8,128)}) custom-call(f32[4,16]{1,0:T(4,128)S(1)} %copy-done.6, f32[4,288,256]{2,1,0:T(8,128)S(1)} %copy-done.2, f32[4,288,256]{2,1,0:T(8,128)S(1)} %copy-done.3, f32[16,288,256]{2,1,0:T(8,128)} %basis.4, f32[4,288,256]{2,1,0:T(8,128)S(1)} %copy-done.1), custom_call_target="tpu_custom_call" | custom-call | tf_op jit(solution)/shard_map/target/pallas_call | solution.py:579
  12.5 2.6 %collective-permute-start.1 = (f32[5,288,256]{2,1,0:T(8,128)}, f32[5,288,256]{2,1,0:T(8,128)}, u32[]{:S(2)}, u32[]{:S(2)}) collective-permute-start(f32[5,288,256]{2,1,0:T(8,128)} %get-tuple-element.19.up), channel_id=1, source_target_pairs={{0,1},{1,2},{2,3},{3,4},{4,5},{5,6},{6,7},{7,8},{8,9},{9,10},{10,1... | collective-permute-start | bytes 4423688 | tf_op jit(solution)/shard_map/ppermute | solution.py:591
  15.0 1.3 collective-permute-start.2
  16.3 1.4 copy-done.4
  17.7 2.7 %strips.1 = (f32[304,128]{1,0:T(8,128)S(1)}, f32[304,128]{1,0:T(8,128)S(1)}) custom-call(f32[4,288,256]{2,1,0:T(8,128)S(1)} %copy-done.1, f32[5,288,256]{2,1,0:T(8,128)} %get-tuple-element.19.up, f32[5,288,256]{2,1,0:T(8,128)S(1)} %copy-done.4, f32[2,4,8,256]{3,2,1,0:T(8,128)S(1)} %collective-permute-done.edge), custom_call_target="tpu_custom_call" | custom-call | tf_op jit(solution)/shard_map/strips/pallas_call | solution.py:593
  20.4 3.4 %collective-permute-start.3 = (f32[304,128]{1,0:T(8,128)S(1)}, f32[304,128]{1,0:T(8,128)S(1)}, u32[]{:S(2)}, u32[]{:S(2)}) collective-permute-start(f32[304,128]{1,0:T(8,128)S(1)} %get-tuple-element.22.right), channel_id=1, source_target_pairs={{0,32},{32,64},{64,96},{1,33},{33,65},{65,97},{2,34},{34,66},{66,9... | collective-permute-start | bytes 466952 | tf_op jit(solution)/shard_map/ppermute | solution.py:601
  23.8 2.4 %collective-permute-start.4 = (f32[304,128]{1,0:T(8,128)S(1)}, f32[304,128]{1,0:T(8,128)S(1)}, u32[]{:S(2)}, u32[]{:S(2)}) collective-permute-start(f32[304,128]{1,0:T(8,128)S(1)} %get-tuple-element.23.left), channel_id=1, source_target_pairs={{32,0},{64,32},{96,64},{33,1},{65,33},{97,65},{34,2},{66,34},{98,6... | collective-permute-start | bytes 466952 | tf_op jit(solution)/shard_map/ppermute | solution.py:602
  26.2 2.8 %collective-permute-done.3.from_left = f32[304,128]{1,0:T(8,128)S(1)} collective-permute-done((f32[304,128]{1,0:T(8,128)S(1)}, f32[304,128]{1,0:T(8,128)S(1)}, u32[]{:S(2)}, u32[]{:S(2)}) %collective-permute-start.3) | collective-permute-done | bytes 155680 | tf_op jit(solution)/shard_map/ppermute | solution.py:601
  29.0 3.4 %collective-permute-done.4.from_right = f32[304,128]{1,0:T(8,128)S(1)} collective-permute-done((f32[304,128]{1,0:T(8,128)S(1)}, f32[304,128]{1,0:T(8,128)S(1)}, u32[]{:S(2)}, u32[]{:S(2)}) %collective-permute-start.4) | collective-permute-done | bytes 155680 | tf_op jit(solution)/shard_map/ppermute | solution.py:602
  32.5 0.7 ring.1
  33.2 1.3 collective-permute-start.6
  34.5 3.7 %collective-permute-start.5 = (f32[432,128]{1,0:T(8,128)}, f32[432,128]{1,0:T(8,128)}, u32[]{:S(2)}, u32[]{:S(2)}) collective-permute-start(f32[432,128]{1,0:T(8,128)} %ring.1), channel_id=1, source_target_pairs={{0,1},{1,2},{2,3},{3,4},{4,5},{5,6},{6,7},{7,8},{8,9},{9,10},{10,1... | collective-permute-start | bytes 663560 | tf_op jit(solution)/shard_map/ppermute | solution.py:611
  38.3 0.7 collective-permute-done.5.ring_before
  39.0 19.4 %sweeps.1 = (f32[4,288,256]{2,1,0:T(8,128)}, f32[32,80,128]{2,1,0:T(8,128)S(1)}) custom-call(s32[3]{0:T(128)S(1)} %copy-done.7, f32[4,288,256]{2,1,0:T(8,128)S(1)} %copy-done.1, f32[5,288,256]{2,1,0:T(8,128)} %collective-permute-done.1.before, f32[5,288,256]{2,1,0:T(8,128)} %collective-permute-done.2.after, f32[5,288,256]{2,1,0:T(8,128)} %get-tuple-element.19.up, ...), custom_call_target="tpu_custom_call" | custom-call | tf_op jit(solution)/shard_map/sweeps/pallas_call | solution.py:634
  58.3 1.1 copy-done.5
  59.4 25.4 %all-to-all-start = ((f32[32,80,128]{2,1,0:T(8,128)}), f32[32,80,128]{2,1,0:T(8,128)S(1)}, u32[]{:S(2)}, u32[]{:S(2)}) async-start(f32[32,80,128]{2,1,0:T(8,128)} %copy-done.5), calls=%async_computation | async-start | bytes 2621440 | tf_op jit(solution)/shard_map/all_to_all | solution.py:657
  84.8 2.3 %copy-done = f32[16,288,256]{2,1,0:T(8,128)S(1)} copy-done((f32[16,288,256]{2,1,0:T(8,128)S(1)}, f32[16,288,256]{2,1,0:T(8,128)}, u32[]{:S(2)}) %copy-start) | copy-done | bytes 4718616
  87.2 3.8 %gram.1 = (f32[16,128]{1,0:T(8,128)S(1)}, f32[9,32,128]{2,1,0:T(8,128)S(1)}) custom-call(s32[1]{0:T(128)} %bitcast.2.slot.slot_ref, f32[16,288,256]{2,1,0:T(8,128)S(1)} %copy-done), custom_call_target="tpu_custom_call" | custom-call | tf_op jit(solution)/shard_map/gram/pallas_call | solution.py:659
  90.9 27.9 %all-to-all-done.got_ref = f32[32,80,128]{2,1,0:T(8,128)S(1)} async-done(((f32[32,80,128]{2,1,0:T(8,128)}), f32[32,80,128]{2,1,0:T(8,128)S(1)}, u32[]{:S(2)}, u32[]{:S(2)}) %all-to-all-start) | async-done | bytes 1310752 | tf_op jit(solution)/shard_map/all_to_all | solution.py:657
  118.9 12.2 %all_to_all.10.parts_ref = f32[8,48,128]{2,1,0:T(8,128)S(1)} all-to-all(f32[8,48,128]{2,1,0:T(8,128)S(1)} %broadcast_in_dim.2), channel_id=1, replica_groups=mesh['row'=2,'col'=4,'frame'=32] {'row','col'}, dimensions={0} | all-to-all | bytes 393216 | tf_op jit(solution)/shard_map/all_to_all | solution.py:672
  131.1 7.0 %final.1 = (f32[9,16,256]{2,1,0:T(8,128)}, f32[4,16]{1,0:T(4,128)}) custom-call(s32[1]{0:T(128)} %bitcast.2.slot.slot_ref, f32[32,80,128]{2,1,0:T(8,128)S(1)} %all-to-all-done.got_ref, f32[8,48,128]{2,1,0:T(8,128)S(1)} %all_to_all.10.parts_ref, f32[9,32,128]{2,1,0:T(8,128)S(1)} %get-tuple-element.28.old_ref), custom_call_target="tpu_custom_call" | custom-call | tf_op jit(solution)/shard_map/final/pallas_call | solution.py:674
  (21 shorter events, 0.2 us)
Async XLA Ops:
  1.2 6.0 %copy-start.1 = (f32[4,288,256]{2,1,0:T(8,128)S(1)}, f32[4,288,256]{2,1,0:T(8,128)}, u32[]{:S(2)}) copy-start(f32[4,288,256]{2,1,0:T(8,128)} %current.7) | copy-start | bytes 3538948
  1.2 6.0 %copy-start.2 = (f32[4,288,256]{2,1,0:T(8,128)S(1)}, f32[4,288,256]{2,1,0:T(8,128)}, u32[]{:S(2)}) copy-start(f32[4,288,256]{2,1,0:T(8,128)} %video.3) | copy-start | bytes 3538948
  1.2 6.0 %copy-start.3 = (f32[4,288,256]{2,1,0:T(8,128)S(1)}, f32[4,288,256]{2,1,0:T(8,128)}, u32[]{:S(2)}) copy-start(f32[4,288,256]{2,1,0:T(8,128)} %multiplier.3) | copy-start | bytes 3538948
  1.2 6.0 %copy-start.6 = (f32[4,16]{1,0:T(4,128)S(1)}, f32[4,16]{1,0:T(4,128)}, u32[]{:S(2)}) copy-start(f32[4,16]{1,0:T(4,128)} %coeff.3) | copy-start | bytes 772
  4.0 8.5 %collective-permute-start = (f32[2,4,8,256]{3,2,1,0:T(8,128)}, f32[2,4,8,256]{3,2,1,0:T(8,128)S(1)}, u32[]{:S(2)}, u32[]{:S(2)}) collective-permute-start(f32[2,4,8,256]{3,2,1,0:T(8,128)} %edge.1), channel_id=1, source_target_pairs={{0,128},{128,0},{1,129},{129,1},{2,130},{130,2},{3,131},{131,3},{4... | collective-permute-start | bytes 196616 | tf_op jit(solution)/shard_map/ppermute | solution.py:578
  12.4 26.5 %copy-start.7 = (s32[3]{0:T(128)S(1)}, s32[3]{0:T(128)}, u32[]{:S(2)}) copy-start(s32[3]{0:T(128)} %pad_add_fusion.place) | copy-start | bytes 40
  12.5 26.5 %collective-permute-start.1 = (f32[5,288,256]{2,1,0:T(8,128)}, f32[5,288,256]{2,1,0:T(8,128)}, u32[]{:S(2)}, u32[]{:S(2)}) collective-permute-start(f32[5,288,256]{2,1,0:T(8,128)} %get-tuple-element.19.up), channel_id=1, source_target_pairs={{0,1},{1,2},{2,3},{3,4},{4,5},{5,6},{6,7},{7,8},{8,9},{9,10},{10,1... | collective-permute-start | bytes 4423688 | tf_op jit(solution)/shard_map/ppermute | solution.py:591
  15.0 23.9 %collective-permute-start.2 = (f32[5,288,256]{2,1,0:T(8,128)}, f32[5,288,256]{2,1,0:T(8,128)}, u32[]{:S(2)}, u32[]{:S(2)}) collective-permute-start(f32[5,288,256]{2,1,0:T(8,128)} %get-tuple-element.20.down), channel_id=1, source_target_pairs={{1,0},{2,1},{3,2},{4,3},{5,4},{6,5},{7,6},{8,7},{9,8},{10,9},{11,1... | collective-permute-start | bytes 4423688 | tf_op jit(solution)/shard_map/ppermute | solution.py:592
  16.3 1.4 copy-start.4
  20.4 8.6 %collective-permute-start.3 = (f32[304,128]{1,0:T(8,128)S(1)}, f32[304,128]{1,0:T(8,128)S(1)}, u32[]{:S(2)}, u32[]{:S(2)}) collective-permute-start(f32[304,128]{1,0:T(8,128)S(1)} %get-tuple-element.22.right), channel_id=1, source_target_pairs={{0,32},{32,64},{64,96},{1,33},{33,65},{65,97},{2,34},{34,66},{66,9... | collective-permute-start | bytes 466952 | tf_op jit(solution)/shard_map/ppermute | solution.py:601
  23.8 8.7 %collective-permute-start.4 = (f32[304,128]{1,0:T(8,128)S(1)}, f32[304,128]{1,0:T(8,128)S(1)}, u32[]{:S(2)}, u32[]{:S(2)}) collective-permute-start(f32[304,128]{1,0:T(8,128)S(1)} %get-tuple-element.23.left), channel_id=1, source_target_pairs={{32,0},{64,32},{96,64},{33,1},{65,33},{97,65},{34,2},{66,34},{98,6... | collective-permute-start | bytes 466952 | tf_op jit(solution)/shard_map/ppermute | solution.py:602
  33.2 5.1 %collective-permute-start.6 = (f32[432,128]{1,0:T(8,128)}, f32[432,128]{1,0:T(8,128)}, u32[]{:S(2)}, u32[]{:S(2)}) collective-permute-start(f32[432,128]{1,0:T(8,128)} %ring.1), channel_id=1, source_target_pairs={{1,0},{2,1},{3,2},{4,3},{5,4},{6,5},{7,6},{8,7},{9,8},{10,9},{11,1... | collective-permute-start | bytes 663560 | tf_op jit(solution)/shard_map/ppermute | solution.py:612
  34.5 4.5 %collective-permute-start.5 = (f32[432,128]{1,0:T(8,128)}, f32[432,128]{1,0:T(8,128)}, u32[]{:S(2)}, u32[]{:S(2)}) collective-permute-start(f32[432,128]{1,0:T(8,128)} %ring.1), channel_id=1, source_target_pairs={{0,1},{1,2},{2,3},{3,4},{4,5},{5,6},{6,7},{7,8},{8,9},{9,10},{10,1... | collective-permute-start | bytes 663560 | tf_op jit(solution)/shard_map/ppermute | solution.py:611
  58.3 1.1 copy-start.5
  59.4 59.4 %all-to-all-start = ((f32[32,80,128]{2,1,0:T(8,128)}), f32[32,80,128]{2,1,0:T(8,128)S(1)}, u32[]{:S(2)}, u32[]{:S(2)}) async-start(f32[32,80,128]{2,1,0:T(8,128)} %copy-done.5), calls=%async_computation | async-start | bytes 2621440 | tf_op jit(solution)/shard_map/all_to_all | solution.py:657
  84.8 2.3 %copy-start = (f32[16,288,256]{2,1,0:T(8,128)S(1)}, f32[16,288,256]{2,1,0:T(8,128)}, u32[]{:S(2)}) copy-start(f32[16,288,256]{2,1,0:T(8,128)} %basis.4) | copy-start | bytes 14155780

commit v3 on v2

--- a/solution.py
+++ b/solution.py
@@ -35,11 +35,16 @@
     lanes, rows = iota(wide, 1), iota(wide, 0)
     work = jnp.concatenate([matrix, jnp.zeros((n, 128 - n), jnp.float32)], axis=1)
     work = work + jnp.where(lanes == rows + n, 1.0, 0.0)
-    for k in range(n):
-        column = jnp.broadcast_to(work[:, k : k + 1], wide)
-        pivot = jnp.broadcast_to(work[k : k + 1, :], wide)
-        scaled = pivot / jnp.broadcast_to(column[k : k + 1, :], wide)
-        work = jnp.where(rows == k, scaled, work - column * scaled)
+    for k in range(0, n, 2):
+        col0 = jnp.broadcast_to(work[:, k : k + 1], wide)
+        col1 = jnp.broadcast_to(work[:, k + 1 : k + 2], wide)
+        row0, row1 = work[k : k + 1, :], work[k + 1 : k + 2, :]
+        a, b, d = col0[k : k + 1, :], col1[k : k + 1, :], col1[k + 1 : k + 2, :]
+        scale = 1.0 / (a * d - b * b)
+        new0 = jnp.broadcast_to((d * row0 - b * row1) * scale, wide)
+        new1 = jnp.broadcast_to((a * row1 - b * row0) * scale, wide)
+        left = work - col0 * new0 - col1 * new1
+        work = jnp.where(rows == k, new0, jnp.where(rows == k + 1, new1, left))
     return work[:, n : 2 * n]
 
 
@@ -75,22 +80,24 @@
     a, b = iota((width, width), 0) // rank, iota((width, width), 1) // rank
     pick = spread_ranks(rank, width)
     gram = dot(dot(pick.T, jnp.where(a == b, full, 0.0)), pick)
-    inverse = eliminated(gram + ridge * eye)
     lines = 8 * slots
     repeat = jnp.where(iota((slots, lines), 0) == iota((slots, lines), 1) // 8, 1.0, 0.0)
     wide = dot(coeff_t, repeat)
-    wide = jnp.where(
-        iota((width, lines), 0) // rank == iota((width, lines), 1) % 4, wide, 0.0
+    wide = jnp.where(iota((width, lines), 0) // rank == iota((width, lines), 1) % 4, wide, 0.0)
+    narrow = wide[0:rank]
+    for f in range(1, 4):
+        narrow = narrow + wide[f * rank : (f + 1) * rank]
+    twice = jnp.concatenate([narrow, narrow], axis=0)
+    factor = jnp.where(
+        iota((2 * rank, lines), 0) // rank == (iota((2 * rank, lines), 1) // 4) % 2, twice, 0.0
     )
-    twice = spread_ranks(rank, 2 * rank)
-    mix = dot(dot(twice, inverse), pick.T)
-    factor = jnp.where(
-        iota((2 * rank, lines), 0) // rank == (iota((2 * rank, lines), 1) // 4) % 2, dot(mix, wide), 0.0
-    )
-    old_factor = ridge * spread_blocks(inverse, 2 * rank, 2)
+    sums = []
+    for i in range(0, rows_owned):
+        block = got_ref[:, 8 * i : 8 * (i + 1), :].reshape(lines, 128)
+        sums.append(dot(factor, block) + ridge * old_ref[i])
+    inverse = spread_blocks(eliminated(gram + ridge * eye), 2 * rank, 2)
     for i in range(rows_owned):
-        block = got_ref[:, 8 * i : 8 * (i + 1), :].reshape(lines, 128)
-        rows = dot(factor, block) + dot(old_factor, old_ref[i])
+        rows = dot(inverse, sums[i])
         for half in range(2):
             basis_ref[i, :, half * 128 : (half + 1) * 128] = rows[half * rank : (half + 1) * rank]
 
@@ -141,44 +148,28 @@
         edge[1, f] = value
 
 
-def target_kernel(
-    coeff, video_in, multiplier_in, basis_in, current, up, down, video, multiplier, basis, low, high, sems
-):
+def target_kernel(coeff, video, multiplier, basis_in, current, up, down, basis, sems):
     frames, rows, _ = video.shape
-    pieces, chunk = sems.shape[1], 16
+    pieces, chunk = sems.shape[0], 16
     piece = rows // pieces
     waits = []
     for p in range(pieces):
         at = pl.ds(p * piece, piece)
-        for k, (ref, buf) in enumerate(((basis_in, basis), (video_in, video), (multiplier_in, multiplier))):
-            c = pltpu.make_async_copy(ref.at[:, at, :], buf.at[:, at, :], sems.at[k, p])
-            c.start()
-            waits.append(c)
-    outs = [
-        pltpu.make_async_copy(current.at[pl.ds(frames - HALO, HALO)], up.at[pl.ds(0, HALO)], sems.at[5, 0]),
-        pltpu.make_async_copy(current.at[pl.ds(0, HALO)], down.at[pl.ds(0, HALO)], sems.at[5, 1]),
-    ]
-    for c in outs:
-        c.start()
+        waits.append(pltpu.make_async_copy(basis_in.at[:, at, :], basis.at[:, at, :], sems.at[p]))
+        waits[p].start()
+    for k in range(HALO):
+        up[k] = current[frames - HALO + k]
+        down[k] = current[k]
     for p in range(pieces):
-        for c in waits[3 * p : 3 * p + 3]:
-            c.wait()
+        waits[p].wait()
 
         def body(c, carry):
             at = pl.ds(pl.multiple_of(p * piece + c * chunk, chunk), chunk)
-            goals = goal_rows(coeff, video, multiplier, basis, at)
-            for f in range(frames):
-                (low if f < 2 else high)[f % 2, at, :] = goals[f]
+            for f, value in enumerate(goal_rows(coeff, video, multiplier, basis, at)):
+                (down if f < 2 else up)[HALO + f % 2, at, :] = value
             return carry
 
         lax.fori_loop(0, piece // chunk, body, 0)
-        at = pl.ds(p * piece, piece)
-        for k, (buf, ref) in enumerate(((low, down), (high, up))):
-            c = pltpu.make_async_copy(buf.at[:, at, :], ref.at[pl.ds(HALO, 2), at, :], sems.at[3 + k, p])
-            c.start()
-            outs.append(c)
-    for c in outs:
-        c.wait()
 
 
 def strips_kernel(current, up, down, edge, right, left):
@@ -212,19 +203,30 @@
         gather(out_at, 8, lambda ref, i, kind, f: (edge[kind, f, :, 0:128], edge[kind, f, :, 128:256]))
 
 
-def ring_kernel(right, left, from_left, from_right, edge, out):
+def ring_kernel(right, left, from_left, from_right, edge, ring, up, down):
     rows = right.shape[0]
     lanes = lane_of(rows)
     k = (lanes + 128 - HALO * GROUP) % 128 % GROUP
-    out[0:rows, :] = jnp.where(
+    mine = jnp.where(
         k <= 2,
         from_left[...],
         jnp.where(k <= 5, right[...], jnp.where(k <= 7, left[...], from_right[...])),
     )
+    ring[0:rows, :] = mine
     flat = edge.reshape(edge.shape[0] * edge.shape[1] * 8, 256)
-    for half in range(2):
-        at = rows + half * flat.shape[0]
-        out[at : at + flat.shape[0], :] = flat[:, half * 128 : (half + 1) * 128]
+    for side in range(2):
+        at = rows + side * flat.shape[0]
+        ring[at : at + flat.shape[0], :] = flat[:, side * 128 : (side + 1) * 128]
+    half = rows // 2
+    for out, turn, turn_goal, frame, goal_frame in ((up, 80, 56, 1, 2), (down, 92, 80, 0, 0)):
+        part = jnp.where(lanes < 36, pltpu.roll(mine, turn, 1), pltpu.roll(mine, turn_goal, 1))
+        out[0:half, :] = jnp.where(lanes[0:half] < 64, part[0:half], pltpu.roll(part[half:], 64, 1))
+        for side in range(2):
+            cols = slice(side * 128, (side + 1) * 128)
+            at = half + side * 40
+            for n in range(5):
+                tile = edge[0, frame + n, :, cols] if n < 3 else edge[1, goal_frame + n - 3, :, cols]
+                out[at + 8 * n : at + 8 * n + 8, :] = tile
 
 
 def sweep_kernel(
@@ -245,7 +247,7 @@
     basis,
     coeff,
     shrunk_out,
-    sent,
+    sent_out,
     s_a,
     s_b,
     goal,
@@ -254,11 +256,13 @@
     strip_goal,
     strip_flux,
     flux_f,
+    flux_r,
     own_video,
     own_multiplier,
     own_basis,
     residual,
     out,
+    sent,
     sums,
     sems,
 ):
@@ -275,47 +279,64 @@
         return c
 
     own_at = pl.ds(TOP, rows)
-    strip_chunks = [(c, min(80, all_rows - c)) for c in range(0, all_rows, 80)]
+    strip_chunks = [(c, all_rows // 4) for c in range(0, all_rows, all_rows // 4)]
     first = []
     for half in range(2):
         at = pl.ds(half * 128, 128)
-        for src, at_frame, count in ((before, 0, HALO), (current, HALO, frames), (after, HALO + frames, HALO)):
-            first.append(copy(src.at[pl.ds(0, count), :, at], s_a.at[pl.ds(at_frame, count), half, own_at, :]))
-        for src, at_frame in ((before, 0), (down, 2), (up, 4), (after, 6)):
-            first.append(copy(src.at[pl.ds(HALO, 2), :, at], goal.at[pl.ds(at_frame, 2), half, own_at, :]))
+        for src, start, count, buf, at_frame in (
+            (before, 0, HALO, s_a, 0),
+            (current, 0, frames, s_a, HALO),
+            (after, 0, HALO, s_a, HALO + frames),
+            (before, HALO, 2, goal, 0),
+            (down, HALO, 2, goal, 2),
+            (up, HALO, 2, goal, 4),
+            (after, HALO, 2, goal, 6),
+        ):
+            first.append(copy(src.at[pl.ds(start, count), :, at], buf.at[pl.ds(at_frame, count), half, own_at, :]))
     later = [copy(video, own_video), copy(multiplier, own_multiplier), copy(basis, own_basis)]
 
+    folded = all_rows // 2
     for c, count in strip_chunks:
         at = slice(c, c + count)
+        from_at = slice(c % folded, c % folded + count)
         lanes = lane_of(count)
-        mine, prev, nxt = ring[at, :], ring_before[at, :], ring_after[at, :]
+        mine, prev, nxt = ring[at, :], ring_before[from_at, :], ring_after[from_at, :]
+        turn = 64 if c >= folded else 0
+        prev_own = pltpu.roll(prev, 64, 1) if turn else prev
         strip_a[at, :] = jnp.where(
-            lanes < 36, pltpu.roll(prev, 80, 1), jnp.where(lanes < 84, mine, pltpu.roll(nxt, 48, 1))
+            lanes < 36, prev_own, jnp.where(lanes < 84, mine, pltpu.roll(nxt, (84 + turn) % 128, 1))
         )
         strip_goal[at, :] = jnp.where(
-            lanes < 36, pltpu.roll(prev, 32, 1), jnp.where(lanes < 84, pltpu.roll(mine, 80, 1), nxt)
+            lanes < 36,
+            pltpu.roll(prev, (104 + turn) % 128, 1),
+            jnp.where(lanes < 84, pltpu.roll(mine, 80, 1), pltpu.roll(nxt, 48 + turn, 1)),
         )
     zero8 = jnp.zeros((8, 128), jnp.float32)
     for buf in (strip_a, strip_b):
         buf[pl.ds(all_rows, 8), :] = zero8
     for half in range(2):
         for g in range(2 * HALO + frames):
+            goal_tile = None
+            base = folded + half * 40
             if g < HALO:
-                src, f = ring_before, g + 1
+                tile = ring_before[base + 8 * g : base + 8 * g + 8, :]
+                if g >= 1:
+                    goal_tile = ring_before[base + 8 * (g + 2) : base + 8 * (g + 2) + 8, :]
             elif g < HALO + frames:
-                src, f = ring, g - HALO
+                at = all_rows + half * 2 * frames * 8 + (g - HALO) * 8
+                tile, goal_tile = ring[at : at + 8, :], ring[at + frames * 8 : at + frames * 8 + 8, :]
             else:
-                src, f = ring_after, g - HALO - frames
-            base = all_rows + half * 64
-            tile = src[base + 8 * f : base + 8 * f + 8, :]
+                n = g - HALO - frames
+                tile = ring_after[base + 8 * n : base + 8 * n + 8, :]
+                if n <= 1:
+                    goal_tile = ring_after[base + 8 * (n + 3) : base + 8 * (n + 3) + 8, :]
             s_a[g, half, 0:TOP, :] = tile
             s_a[g, half, pl.ds(TOP + rows, 8), :] = tile
             s_a[g, half, pl.ds(all_rows, 8), :] = zero8
             s_b[g, half, pl.ds(all_rows, 8), :] = zero8
-            if 1 <= g <= 2 * HALO + frames - 2:
-                tile = src[base + 32 + 8 * f : base + 32 + 8 * f + 8, :]
-                goal[g - 1, half, 0:TOP, :] = tile
-                goal[g - 1, half, pl.ds(TOP + rows, 8), :] = tile
+            if goal_tile is not None:
+                goal[g - 1, half, 0:TOP, :] = goal_tile
+                goal[g - 1, half, pl.ds(TOP + rows, 8), :] = goal_tile
 
     def first_row_last(value, count):
         return value[count - 1 : count, :]
@@ -351,7 +372,8 @@
             pc = pltpu.roll(s, 127, 1) - s
             weight = lax.rsqrt(FLOOR + pf * pf + pr * pr + pc * pc)
             ff, fr, fc = pf * weight, pr * weight, pc * weight
-            strip_flux[flux_at, c : c + count, :] = fc
+            k = lane_of(count) % GROUP
+            strip_flux[flux_at, c : c + count, :] = jnp.where(k == 8, s, pltpu.roll(fc, 7, 1))
             spread = (
                 (ff - pltpu.roll(ff, 12, 1)) + (fr - down_one(fr, carry, count)) + (fc - pltpu.roll(fc, 1, 1))
             )
@@ -359,12 +381,14 @@
             new[c : c + count, :] = s + RELAX * (strip_goal[c : c + count, :] - s + SMOOTH * spread)
 
     slots_end, cols_end = slot_count - 1, col_count - 1
+    for half in range(2):
+        flux_r[half, 0:8, :] = zero8
     strip_sweep(strip_a, strip_b, 0)
 
     for c in first:
         c.wait()
 
-    chunks = [(c, min(32, all_rows - c)) for c in range(0, all_rows, 32)]
+    chunks = [(c, min(64, all_rows - c)) for c in range(0, all_rows, 64)]
 
     def edges(old):
         @pl.when(slot == 0)
@@ -390,22 +414,20 @@
 
     last_keep = jnp.where((lane_of(8)[0:1] == 127) & (col == cols_end), 0.0, 1.0)
 
-    def main_sweep(old, new, strip, flux_at, g_first, g_count):
+    def main_sweep(old, new, flux_at, g_first, g_count):
         edges(old)
 
         def body(i, carry0):
             g = g_first + i
-            turn_ahead = (119 + 12 * 128 - 12 * g) % 128
-            turn_flux = (128 * 12 - 2 - 12 * g) % 128
+            turn = (119 + 12 * 128 - 12 * g) % 128
             goal_at = jnp.maximum(g - 1, 0)
-            carry = [jnp.zeros((1, 128), jnp.float32)] * 2
             for c, count in chunks:
                 lanes = lane_of(count)
                 at = pl.ds(c, count)
                 next_at = pl.ds(c + 1, count)
                 s = [old[g, half, at, :] for half in range(2)]
                 turned = [pltpu.roll(x, 127, 1) for x in s]
-                outside = pltpu.roll(strip[at, :], turn_ahead, 1)
+                outside = pltpu.roll(strip_flux[flux_at, at, :], turn, 1)
                 ahead = [
                     jnp.where(lanes == 127, turned[1], turned[0]),
                     jnp.where(lanes == 127, outside, turned[1]),
@@ -421,8 +443,8 @@
                     weight = lax.rsqrt(FLOOR + pf * pf + pr * pr + pc * pc)
                     ff.append(pf * weight)
                     fr.append(pr * weight)
+                    flux_r[half, pl.ds(c + 8, count), :] = fr[half]
                     fc.append(pc * weight)
-                outside = pltpu.roll(strip_flux[flux_at, at, :], turn_flux, 1)
                 turned = [pltpu.roll(x, 1, 1) for x in fc]
                 behind = [
                     jnp.where(lanes == 0, outside, turned[0]),
@@ -432,21 +454,20 @@
                     x = s[half]
                     spread = (
                         (ff[half] - flux_f[half, at, :])
-                        + (fr[half] - down_one(fr[half], carry[half], count))
+                        + (fr[half] - flux_r[half, pl.ds(c + 7, count), :])
                         + (fc[half] - behind[half])
                     )
                     flux_f[half, at, :] = ff[half]
                     new[g, half, at, :] = x + RELAX * (goal[goal_at, half, at, :] - x + SMOOTH * spread)
-                carry = [first_row_last(x, count) for x in fr]
             return carry0
 
         lax.fori_loop(0, g_count, body, 0)
 
-    main_sweep(s_a, s_b, strip_a, 0, 0, 9)
+    main_sweep(s_a, s_b, 0, 0, 9)
     strip_sweep(strip_b, strip_a, 1)
-    main_sweep(s_b, s_a, strip_b, 1, 1, 7)
+    main_sweep(s_b, s_a, 1, 1, 7)
     strip_sweep(strip_a, strip_b, 2)
-    main_sweep(s_a, s_b, strip_a, 2, 2, 5)
+    main_sweep(s_a, s_b, 2, 2, 5)
 
     for c in later:
         c.wait()
@@ -497,8 +518,14 @@
         sent[j, pl.ds(owned * 8, 8), :] = cross
         return carry
 
-    lax.fori_loop(0, slot_count, pack, 0)
-    done.wait()
+    done = [done]
+    group = slot_count // 4
+    for n in range(4):
+        lax.fori_loop(n * group, (n + 1) * group, pack, 0)
+        at = pl.ds(n * group, group)
+        done.append(copy(sent.at[at], sent_out.at[at]))
+    for c in done:
+        c.wait()
 
 
 def gram_kernel(slot, basis, out, old, sums, window):
@@ -548,10 +575,17 @@
     return jax.ShapeDtypeStruct(shape, jnp.float32)
 
 
-LARGE = pltpu.CompilerParams(vmem_limit_bytes=48 * 1024 * 1024)
+LARGE = pltpu.CompilerParams(vmem_limit_bytes=28 * 1024 * 1024)
+SMALL = pltpu.CompilerParams(vmem_limit_bytes=20 * 1024 * 1024)
+
+
+def in_hbm(*shape):
+    return pltpu.HBM(shape, jnp.float32)
 
 
 def local(video, multiplier, foreground, basis, coefficients):
+    plain = (video, multiplier)
+    video, multiplier, basis = (pltpu.with_memory_space_constraint(x, pltpu.HBM) for x in (video, multiplier, basis))
     frames, rows, cols = video.shape
     rank = basis.shape[0]
     frame_count = lax.axis_size("frame")
@@ -578,15 +612,13 @@
     edge = lax.ppermute(edge, "row", [(0, 1), (1, 0)])
     up, down = pl.pallas_call(
         target_kernel,
-        out_shape=(floats(HALO + 2, rows, cols), floats(HALO + 2, rows, cols)),
-        in_specs=[smem()] + anywhere(4),
-        out_specs=anywhere(2),
-        scratch_shapes=[pltpu.VMEM(s, jnp.float32) for s in (video.shape, video.shape, basis.shape)]
-        + [pltpu.VMEM((2, rows, cols), jnp.float32)] * 2
-        + [pltpu.SemaphoreType.DMA((6, 6))],
-        compiler_params=LARGE,
+        out_shape=(pltpu.VMEM((HALO + 2, rows, cols), jnp.float32), pltpu.VMEM((HALO + 2, rows, cols), jnp.float32)),
+        in_specs=[smem()] + vmem(2) + anywhere(1) + vmem(1),
+        out_specs=vmem(2),
+        scratch_shapes=[pltpu.VMEM(basis.shape, jnp.float32), pltpu.SemaphoreType.DMA((6,))],
+        compiler_params=SMALL,
         name="target",
-    )(coefficients, video, multiplier, basis, foreground)
+    )(coefficients, *plain, basis, foreground)
     up, down, edge = lax.optimization_barrier((up, down, edge))
     before = lax.ppermute(up, "frame", to_next)
     after = lax.ppermute(down, "frame", to_previous)
@@ -595,21 +627,22 @@
         out_shape=(floats(all_rows, 128), floats(all_rows, 128)),
         in_specs=vmem(4),
         out_specs=vmem(2),
-        compiler_params=LARGE,
+        compiler_params=SMALL,
         name="strips",
     )(foreground, up, down, edge)
     from_left = lax.ppermute(right, "col", to_right)
     from_right = lax.ppermute(left, "col", to_left)
-    ring = pl.pallas_call(
+    folded = all_rows // 2
+    ring, ring_up, ring_down = pl.pallas_call(
         ring_kernel,
-        out_shape=floats(all_rows + 128, 128),
+        out_shape=(floats(all_rows + 16 * frames * 2, 128), floats(folded + 80, 128), floats(folded + 80, 128)),
         in_specs=vmem(5),
-        out_specs=vmem(1)[0],
-        compiler_params=LARGE,
+        out_specs=vmem(3),
+        compiler_params=SMALL,
         name="ring",
     )(right, left, from_left, from_right, edge)
-    ring_before = lax.ppermute(ring, "frame", to_next)
-    ring_after = lax.ppermute(ring, "frame", to_previous)
+    ring_before = lax.ppermute(ring_up, "frame", to_next)
+    ring_after = lax.ppermute(ring_down, "frame", to_previous)
 
     pixel_ridge = ridge_share * rows * cols * blocks
     owned_rows = rows // frame_count
@@ -624,19 +657,21 @@
         (all_rows, 128),
         (3, all_rows, 128),
         (2, all_rows, 128),
+        (2, all_rows + 8, 128),
         video.shape,
         video.shape,
         basis.shape,
         (2 * frames, rows, 128),
         video.shape,
+        (frame_count, owned_rows * 8 + 8, 128),
         (frames * rank, 8, 128),
     ]
     shrunk, sent = pl.pallas_call(
         functools.partial(sweep_kernel, pixel_ridge / blocks, frame_count, col_count),
-        out_shape=(floats(frames, rows, cols), floats(frame_count, owned_rows * 8 + 8, 128)),
+        out_shape=(in_hbm(frames, rows, cols), in_hbm(frame_count, owned_rows * 8 + 8, 128)),
         in_specs=[smem()] + anywhere(5) + vmem(3) + anywhere(3) + vmem(1),
-        out_specs=anywhere(1) + vmem(1),
-        scratch_shapes=[pltpu.VMEM(s, jnp.float32) for s in scratch] + [pltpu.SemaphoreType.DMA((18,))],
+        out_specs=anywhere(2),
+        scratch_shapes=[pltpu.VMEM(s, jnp.float32) for s in scratch] + [pltpu.SemaphoreType.DMA((22,))],
         compiler_params=LARGE,
         name="sweeps",
     )(
@@ -665,7 +700,7 @@
             pltpu.VMEM((rank * rank, 8, 128), jnp.float32),
             pltpu.VMEM((2 * rank, 16, 128), jnp.float32),
         ],
-        compiler_params=LARGE,
+        compiler_params=SMALL,
         name="gram",
     )(frame_slot.reshape(1), basis)
     parts = jnp.concatenate([got[:, owned_rows * 8, :], gram], axis=0)
@@ -677,7 +712,7 @@
         in_specs=[smem()] + vmem(3),
         out_specs=vmem(2),
         scratch_shapes=[pltpu.VMEM((frame_count, 128), jnp.float32)],
-        compiler_params=LARGE,
+        compiler_params=SMALL,
         name="final",
     )(frame_slot.reshape(1), got, parts, old_owned)
     return shrunk, new_coeff, new_basis.transpose(1, 0, 2)

time: 139 us -> 131 us (0.942)
  starting transfers between devices: 43.4 us -> 38.6 us
  local copies, waits for them, and re-layouts: 4.9 us -> 0.13 us
  waiting for transfers between devices: 34.8 us -> 38.7 us
  Pallas kernels: 41.5 us -> 39.3 us
    unnamed x16 -> x10, local copies, waits for them, and re-layouts: 4.79 us -> 0.02 us
    ppermute x2, waiting for transfers between devices: 0.67 us -> 4.87 us  [the longest x1 4.86 us: local(): ring_after = lax.ppermute(ring_down, 'frame', to_previous)]
    pallas_call x1, Pallas kernels: 3.77 us -> 6.11 us  [local(): pl.pallas_call(gram_kernel, out_shape=(floats(rank, 128), floats(owned_ro...]
    all_to_all x1, starting transfers between devices: 25.4 us -> 23.1 us  [local(): got = lax.all_to_all(sent, 'frame', 0, 0, tiled=True)]
    pallas_call x1, Pallas kernels: 7.05 us -> 4.74 us  [local(): pl.pallas_call(functools.partial(final_kernel, pixel_ridge, frame_ridge),...]
    pallas_call x1, Pallas kernels: 19.4 us -> 17.3 us  [local(): pl.pallas_call(functools.partial(sweep_kernel, pixel_ridge / blocks, fram...]
    ppermute x2, starting transfers between devices: 5 us -> 3.49 us  [the longest x1 2.2 us: local(): ring_before = lax.ppermute(ring_up, 'frame', to_next)]
  transfers between devices with their start and end apart: 8 -> 8, of which waited for: 4 -> 4; matrix products, arithmetic and copies ran while one was open for 0% -> 0% of each run, Pallas kernels for 9% -> 11%
where the time goes in v3:
time: 131 us; the launch traced here: 130 us
  Pallas kernels  39.3 us (30%)
  waiting for transfers between devices  38.7 us (30%)
  starting transfers between devices  38.6 us (29%)
  blocking collectives  12.4 us (9%)
    all_to_all x1, waiting for transfers between devices, local(): got = lax.all_to_all(sent, 'frame', 0, 0, tiled=True)  27.9 us
    all_to_all x1, starting transfers between devices, local(): got = lax.all_to_all(sent, 'frame', 0, 0, tiled=True)  23.1 us
    pallas_call x1, Pallas kernels, local(): pl.pallas_call(functools.partial(sweep_kernel, pixel_ridge / blocks, fram...  17.3 us
    all_to_all x1, blocking collectives, local(): lax.all_to_all(jnp.broadcast_to(parts[None], (blocks, *parts.shape)), ('r...  12.4 us
    pallas_call x1, Pallas kernels, local(): pl.pallas_call(gram_kernel, out_shape=(floats(rank, 128), floats(owned_ro...  6.11 us
    pallas_call x1, Pallas kernels, local(): pl.pallas_call(target_kernel, out_shape=(pltpu.VMEM((HALO + 2, rows, cols...  4.97 us
    ppermute x1, waiting for transfers between devices, local(): ring_after = lax.ppermute(ring_down, 'frame', to_previous)  4.86 us
    pallas_call x1, Pallas kernels, local(): pl.pallas_call(functools.partial(final_kernel, pixel_ridge, frame_ridge),...  4.74 us
  transfers between devices with their start and end apart: 8, of which 4 were waited for; matrix products, arithmetic and copies ran while one was open for 0% of the time, Pallas kernels for 11%

profile of v3, /device:TPU:2, one launch (start us, length us, event | category | flops | bytes accessed | tf_op | source)
XLA Modules:
  0.0 130.4 jit_solution(1504537334260143105)
XLA Ops:
  0.6 0.6 pad_add_fusion.place
  1.2 2.7 %edge.1 = f32[2,4,8,256]{3,2,1,0:T(8,128)} custom-call(s32[3]{0:T(128)} %pad_add_fusion.place, f32[4,16]{1,0:T(4,128)} %coeff.3, f32[4,288,256]{2,1,0:T(8,128)} %video.5, f32[4,288,256]{2,1,0:T(8,128)} %multiplier.5, f32[16,288,256]{2,1,0:T(8,128)} %basis.4, f32[4,288,256]{2,1,0:T(8,128)} %current.7), custom_call_target="tpu_custom_call" | custom-call | tf_op jit(solution)/shard_map/edge/pallas_call | solution.py:603
  4.0 3.3 %collective-permute-start = (f32[2,4,8,256]{3,2,1,0:T(8,128)}, f32[2,4,8,256]{3,2,1,0:T(8,128)S(1)}, u32[]{:S(2)}, u32[]{:S(2)}) collective-permute-start(f32[2,4,8,256]{3,2,1,0:T(8,128)} %edge.1), channel_id=1, source_target_pairs={{0,128},{128,0},{1,129},{129,1},{2,130},{130,2},{3,131},{131,3},{4... | collective-permute-start | bytes 196616 | tf_op jit(solution)/shard_map/ppermute | solution.py:612
  7.3 5.0 %target.1 = (f32[5,288,256]{2,1,0:T(8,128)}, f32[5,288,256]{2,1,0:T(8,128)}) custom-call(f32[4,16]{1,0:T(4,128)S(1)} %copy-done.3, f32[4,288,256]{2,1,0:T(8,128)S(1)} %copy-done.1, f32[4,288,256]{2,1,0:T(8,128)S(1)} %copy-done.2, f32[16,288,256]{2,1,0:T(8,128)} %basis.4, f32[4,288,256]{2,1,0:T(8,128)S(1)} %copy-done), custom_call_target="tpu_custom_call" | custom-call | tf_op jit(solution)/shard_map/target/pallas_call | solution.py:613
  12.2 0.0 collective-permute-done.edge
  12.3 0.0 copy-start.4
  12.3 1.6 %collective-permute-start.1 = (f32[5,288,256]{2,1,0:T(8,128)}, f32[5,288,256]{2,1,0:T(8,128)S(1)}, u32[]{:S(2)}, u32[]{:S(2)}) collective-permute-start(f32[5,288,256]{2,1,0:T(8,128)} %get-tuple-element.22.up), channel_id=1, source_target_pairs={{0,1},{1,2},{2,3},{3,4},{4,5},{5,6},{6,7},{7,8},{8,9},{9,10},{10,1... | collective-permute-start | bytes 4423688 | tf_op jit(solution)/shard_map/ppermute | solution.py:623
  13.8 1.3 collective-permute-start.2
  15.1 3.1 %strips.1 = (f32[304,128]{1,0:T(8,128)S(1)}, f32[304,128]{1,0:T(8,128)S(1)}) custom-call(f32[4,288,256]{2,1,0:T(8,128)S(1)} %copy-done, f32[5,288,256]{2,1,0:T(8,128)} %get-tuple-element.22.up, f32[5,288,256]{2,1,0:T(8,128)} %get-tuple-element.23.down, f32[2,4,8,256]{3,2,1,0:T(8,128)S(1)} %collective-permute-done.edge), custom_call_target="tpu_custom_call" | custom-call | tf_op jit(solution)/shard_map/strips/pallas_call | solution.py:625
  18.2 3.4 %collective-permute-start.3 = (f32[304,128]{1,0:T(8,128)S(1)}, f32[304,128]{1,0:T(8,128)S(1)}, u32[]{:S(2)}, u32[]{:S(2)}) collective-permute-start(f32[304,128]{1,0:T(8,128)S(1)} %get-tuple-element.25.right), channel_id=1, source_target_pairs={{0,32},{32,64},{64,96},{1,33},{33,65},{65,97},{2,34},{34,66},{66,9... | collective-permute-start | bytes 466952 | tf_op jit(solution)/shard_map/ppermute | solution.py:633
  21.6 2.4 %collective-permute-start.4 = (f32[304,128]{1,0:T(8,128)S(1)}, f32[304,128]{1,0:T(8,128)S(1)}, u32[]{:S(2)}, u32[]{:S(2)}) collective-permute-start(f32[304,128]{1,0:T(8,128)S(1)} %get-tuple-element.26.left), channel_id=1, source_target_pairs={{32,0},{64,32},{96,64},{33,1},{65,33},{97,65},{34,2},{66,34},{98,6... | collective-permute-start | bytes 466952 | tf_op jit(solution)/shard_map/ppermute | solution.py:634
  24.1 2.1 %collective-permute-done.3.from_left = f32[304,128]{1,0:T(8,128)S(1)} collective-permute-done((f32[304,128]{1,0:T(8,128)S(1)}, f32[304,128]{1,0:T(8,128)S(1)}, u32[]{:S(2)}, u32[]{:S(2)}) %collective-permute-start.3) | collective-permute-done | bytes 155680 | tf_op jit(solution)/shard_map/ppermute | solution.py:633
  26.2 3.7 %collective-permute-done.4.from_right = f32[304,128]{1,0:T(8,128)S(1)} collective-permute-done((f32[304,128]{1,0:T(8,128)S(1)}, f32[304,128]{1,0:T(8,128)S(1)}, u32[]{:S(2)}, u32[]{:S(2)}) %collective-permute-start.4) | collective-permute-done | bytes 155680 | tf_op jit(solution)/shard_map/ppermute | solution.py:634
  30.0 0.3 ring.1
  30.3 2.2 %collective-permute-start.5 = (f32[232,128]{1,0:T(8,128)S(1)}, f32[232,128]{1,0:T(8,128)S(1)}, u32[]{:S(2)}, u32[]{:S(2)}) collective-permute-start(f32[232,128]{1,0:T(8,128)S(1)} %get-tuple-element.28), channel_id=1, source_target_pairs={{0,1},{1,2},{2,3},{3,4},{4,5},{5,6},{6,7},{7,8},{8,9},{9,10},{10,1... | collective-permute-start | bytes 356360 | tf_op jit(solution)/shard_map/ppermute | solution.py:644
  32.5 1.3 collective-permute-start.6
  33.8 0.1 reshape.12.coeff
  33.9 4.9 %collective-permute-done.6.ring_after = f32[232,128]{1,0:T(8,128)S(1)} collective-permute-done((f32[232,128]{1,0:T(8,128)S(1)}, f32[232,128]{1,0:T(8,128)S(1)}, u32[]{:S(2)}, u32[]{:S(2)}) %collective-permute-start.6) | collective-permute-done | bytes 118816 | tf_op jit(solution)/shard_map/ppermute | solution.py:645
  38.8 17.3 %sweeps.1 = (f32[4,288,256]{2,1,0:T(8,128)}, f32[32,80,128]{2,1,0:T(8,128)}) custom-call(s32[3]{0:T(128)S(1)} %copy-done.4, f32[4,288,256]{2,1,0:T(8,128)S(1)} %copy-done, f32[5,288,256]{2,1,0:T(8,128)S(1)} %collective-permute-done.1.before, f32[5,288,256]{2,1,0:T(8,128)} %collective-permute-done.2.after, f32[5,288,256]{2,1,0:T(8,128)} %get-tuple-element.22.up, ...), custom_call_target="tpu_custom_call" | custom-call | tf_op jit(solution)/shard_map/sweeps/pallas_call | solution.py:669
  56.1 23.1 %all-to-all-start = ((f32[32,80,128]{2,1,0:T(8,128)}), f32[32,80,128]{2,1,0:T(8,128)S(1)}, u32[]{:S(2)}, u32[]{:S(2)}) async-start(f32[32,80,128]{2,1,0:T(8,128)} %get-tuple-element.31), calls=%async_computation | async-start | bytes 2621440 | tf_op jit(solution)/shard_map/all_to_all | solution.py:692
  79.2 6.1 %gram.1 = (f32[16,128]{1,0:T(8,128)S(1)}, f32[9,32,128]{2,1,0:T(8,128)S(1)}) custom-call(s32[1]{0:T(128)} %bitcast.2.slot.slot_ref, f32[16,288,256]{2,1,0:T(8,128)} %basis.4), custom_call_target="tpu_custom_call" | custom-call | tf_op jit(solution)/shard_map/gram/pallas_call | solution.py:694
  85.3 27.9 %all-to-all-done.got_ref = f32[32,80,128]{2,1,0:T(8,128)S(1)} async-done(((f32[32,80,128]{2,1,0:T(8,128)}), f32[32,80,128]{2,1,0:T(8,128)S(1)}, u32[]{:S(2)}, u32[]{:S(2)}) %all-to-all-start) | async-done | bytes 1310752 | tf_op jit(solution)/shard_map/all_to_all | solution.py:692
  113.2 12.4 %all_to_all.10.parts_ref = f32[8,48,128]{2,1,0:T(8,128)S(1)} all-to-all(f32[8,48,128]{2,1,0:T(8,128)S(1)} %broadcast_in_dim.2), channel_id=1, replica_groups=mesh['row'=2,'col'=4,'frame'=32] {'row','col'}, dimensions={0} | all-to-all | bytes 393216 | tf_op jit(solution)/shard_map/all_to_all | solution.py:707
  125.7 4.7 %final.1 = (f32[9,16,256]{2,1,0:T(8,128)}, f32[4,16]{1,0:T(4,128)}) custom-call(s32[1]{0:T(128)} %bitcast.2.slot.slot_ref, f32[32,80,128]{2,1,0:T(8,128)S(1)} %all-to-all-done.got_ref, f32[8,48,128]{2,1,0:T(8,128)S(1)} %all_to_all.10.parts_ref, f32[9,32,128]{2,1,0:T(8,128)S(1)} %get-tuple-element.34.old_ref), custom_call_target="tpu_custom_call" | custom-call | tf_op jit(solution)/shard_map/final/pallas_call | solution.py:709
  (15 shorter events, 0.1 us)
Async XLA Ops:
  1.2 6.0 %copy-start = (f32[4,288,256]{2,1,0:T(8,128)S(1)}, f32[4,288,256]{2,1,0:T(8,128)}, u32[]{:S(2)}) copy-start(f32[4,288,256]{2,1,0:T(8,128)} %current.7) | copy-start | bytes 3538948
  1.2 6.0 %copy-start.1 = (f32[4,288,256]{2,1,0:T(8,128)S(1)}, f32[4,288,256]{2,1,0:T(8,128)}, u32[]{:S(2)}) copy-start(f32[4,288,256]{2,1,0:T(8,128)} %video.5) | copy-start | bytes 3538948
  1.2 6.0 %copy-start.2 = (f32[4,288,256]{2,1,0:T(8,128)S(1)}, f32[4,288,256]{2,1,0:T(8,128)}, u32[]{:S(2)}) copy-start(f32[4,288,256]{2,1,0:T(8,128)} %multiplier.5) | copy-start | bytes 3538948
  1.2 6.0 %copy-start.3 = (f32[4,16]{1,0:T(4,128)S(1)}, f32[4,16]{1,0:T(4,128)}, u32[]{:S(2)}) copy-start(f32[4,16]{1,0:T(4,128)} %coeff.3) | copy-start | bytes 772
  4.0 8.3 %collective-permute-start = (f32[2,4,8,256]{3,2,1,0:T(8,128)}, f32[2,4,8,256]{3,2,1,0:T(8,128)S(1)}, u32[]{:S(2)}, u32[]{:S(2)}) collective-permute-start(f32[2,4,8,256]{3,2,1,0:T(8,128)} %edge.1), channel_id=1, source_target_pairs={{0,128},{128,0},{1,129},{129,1},{2,130},{130,2},{3,131},{131,3},{4... | collective-permute-start | bytes 196616 | tf_op jit(solution)/shard_map/ppermute | solution.py:612
  12.3 26.5 %copy-start.4 = (s32[3]{0:T(128)S(1)}, s32[3]{0:T(128)}, u32[]{:S(2)}) copy-start(s32[3]{0:T(128)} %pad_add_fusion.place) | copy-start | bytes 40
  12.3 26.5 %collective-permute-start.1 = (f32[5,288,256]{2,1,0:T(8,128)}, f32[5,288,256]{2,1,0:T(8,128)S(1)}, u32[]{:S(2)}, u32[]{:S(2)}) collective-permute-start(f32[5,288,256]{2,1,0:T(8,128)} %get-tuple-element.22.up), channel_id=1, source_target_pairs={{0,1},{1,2},{2,3},{3,4},{4,5},{5,6},{6,7},{7,8},{8,9},{9,10},{10,1... | collective-permute-start | bytes 4423688 | tf_op jit(solution)/shard_map/ppermute | solution.py:623
  13.8 24.9 %collective-permute-start.2 = (f32[5,288,256]{2,1,0:T(8,128)}, f32[5,288,256]{2,1,0:T(8,128)}, u32[]{:S(2)}, u32[]{:S(2)}) collective-permute-start(f32[5,288,256]{2,1,0:T(8,128)} %get-tuple-element.23.down), channel_id=1, source_target_pairs={{1,0},{2,1},{3,2},{4,3},{5,4},{6,5},{7,6},{8,7},{9,8},{10,9},{11,1... | collective-permute-start | bytes 4423688 | tf_op jit(solution)/shard_map/ppermute | solution.py:624
  18.2 8.0 %collective-permute-start.3 = (f32[304,128]{1,0:T(8,128)S(1)}, f32[304,128]{1,0:T(8,128)S(1)}, u32[]{:S(2)}, u32[]{:S(2)}) collective-permute-start(f32[304,128]{1,0:T(8,128)S(1)} %get-tuple-element.25.right), channel_id=1, source_target_pairs={{0,32},{32,64},{64,96},{1,33},{33,65},{65,97},{2,34},{34,66},{66,9... | collective-permute-start | bytes 466952 | tf_op jit(solution)/shard_map/ppermute | solution.py:633
  21.6 8.3 %collective-permute-start.4 = (f32[304,128]{1,0:T(8,128)S(1)}, f32[304,128]{1,0:T(8,128)S(1)}, u32[]{:S(2)}, u32[]{:S(2)}) collective-permute-start(f32[304,128]{1,0:T(8,128)S(1)} %get-tuple-element.26.left), channel_id=1, source_target_pairs={{32,0},{64,32},{96,64},{33,1},{65,33},{97,65},{34,2},{66,34},{98,6... | collective-permute-start | bytes 466952 | tf_op jit(solution)/shard_map/ppermute | solution.py:634
  30.3 3.6 %collective-permute-start.5 = (f32[232,128]{1,0:T(8,128)S(1)}, f32[232,128]{1,0:T(8,128)S(1)}, u32[]{:S(2)}, u32[]{:S(2)}) collective-permute-start(f32[232,128]{1,0:T(8,128)S(1)} %get-tuple-element.28), channel_id=1, source_target_pairs={{0,1},{1,2},{2,3},{3,4},{4,5},{5,6},{6,7},{7,8},{8,9},{9,10},{10,1... | collective-permute-start | bytes 356360 | tf_op jit(solution)/shard_map/ppermute | solution.py:644
  32.5 6.2 %collective-permute-start.6 = (f32[232,128]{1,0:T(8,128)S(1)}, f32[232,128]{1,0:T(8,128)S(1)}, u32[]{:S(2)}, u32[]{:S(2)}) collective-permute-start(f32[232,128]{1,0:T(8,128)S(1)} %get-tuple-element.29), channel_id=1, source_target_pairs={{1,0},{2,1},{3,2},{4,3},{5,4},{6,5},{7,6},{8,7},{9,8},{10,9},{11,1... | collective-permute-start | bytes 356360 | tf_op jit(solution)/shard_map/ppermute | solution.py:645
  56.1 57.1 %all-to-all-start = ((f32[32,80,128]{2,1,0:T(8,128)}), f32[32,80,128]{2,1,0:T(8,128)S(1)}, u32[]{:S(2)}, u32[]{:S(2)}) async-start(f32[32,80,128]{2,1,0:T(8,128)} %get-tuple-element.31), calls=%async_computation | async-start | bytes 2621440 | tf_op jit(solution)/shard_map/all_to_all | solution.py:692

commit v4 on v3

--- a/solution.py
+++ b/solution.py
@@ -60,18 +60,19 @@
     return jnp.where((a == b) & (a < count), full, 0.0)
 
 
-def final_kernel(pixel_ridge, ridge, slot_ref, got_ref, parts_ref, old_ref, basis_ref, coeff_ref, coeff_all):
-    slots = got_ref.shape[0]
-    rows_owned = old_ref.shape[0]
+def final_kernel(pixel_ridge, ridge, got_ref, parts_ref, old_ref, basis_ref, coeff_ref, coeff_all):
+    step = 8 * basis_ref.shape[0] + 1
+    slots = got_ref.shape[0] // step
     rank = basis_ref.shape[1]
+    rows_owned = basis_ref.shape[0]
     total = parts_ref[0]
     for peer in range(1, parts_ref.shape[0]):
         total = total + parts_ref[peer]
     eye = jnp.where(iota((rank, rank), 0) == iota((rank, rank), 1), 1.0, 0.0)
     inverse = eliminated(total[slots:, 0:rank] + pixel_ridge * eye)
     coeff = dot(total[0:slots], spread_blocks(inverse, 128, 4))
-    coeff_all[...] = coeff
-    mine = coeff_all[pl.ds(slot_ref[0], 1), :]
+    coeff_all[0:slots] = coeff
+    mine = coeff_all[pl.ds(lax.axis_index("frame"), 1), :]
     for f in range(4):
         coeff_ref[f : f + 1, :] = mine[:, f * rank : (f + 1) * rank]
     width = 128
@@ -93,7 +94,9 @@
     )
     sums = []
     for i in range(0, rows_owned):
-        block = got_ref[:, 8 * i : 8 * (i + 1), :].reshape(lines, 128)
+        block = jnp.concatenate(
+            [got_ref[n * step + 8 * i : n * step + 8 * (i + 1), :] for n in range(slots)], axis=0
+        )
         sums.append(dot(factor, block) + ridge * old_ref[i])
     inverse = spread_blocks(eliminated(gram + ridge * eye), 2 * rank, 2)
     for i in range(rows_owned):
@@ -119,21 +122,20 @@
     return (lanes >= first) | (lanes < first + count - 128)
 
 
-def goal_rows(coeff, video, multiplier, basis, at):
-    frames, rank = video.shape[0], basis.shape[0]
-    sums = [None] * frames
-    for r in range(rank):
+def goal_rows(coeff, video, multiplier, basis, at, which=range(4)):
+    sums = [None] * len(which)
+    for r in range(basis.shape[0]):
         image = basis[r, at, :]
-        for f in range(frames):
+        for k, f in enumerate(which):
             term = coeff[f, r] * image
-            sums[f] = term if r == 0 else sums[f] + term
-    return [video[f, at, :] - sums[f] + dual_scale * multiplier[f, at, :] for f in range(frames)]
-
-
-def edge_kernel(place, coeff, video, multiplier, basis, current, edge, *scratch):
+            sums[k] = term if r == 0 else sums[k] + term
+    return [video[f, at, :] - sums[k] + dual_scale * multiplier[f, at, :] for k, f in enumerate(which)]
+
+
+def edge_kernel(coeff, video, multiplier, basis, current, edge, *scratch):
     buffers, sems = scratch[:-1], scratch[-1]
     frames, rows, _ = video.shape
-    at = pl.ds(pl.multiple_of((1 - place[0]) * (rows - 8), 8), 8)
+    at = pl.ds(pl.multiple_of((1 - lax.axis_index("row")) * (rows - 8), 8), 8)
     near = [
         pltpu.make_async_copy(ref.at[:, at, :], buf, sems.at[k])
         for k, (ref, buf) in enumerate(zip((video, multiplier, basis, current), buffers))
@@ -148,33 +150,42 @@
         edge[1, f] = value
 
 
-def target_kernel(coeff, video, multiplier, basis_in, current, up, down, basis, sems):
+def fill_side(forward, coeff, video, multiplier, basis, current, out, ready):
     frames, rows, _ = video.shape
-    pieces, chunk = sems.shape[0], 16
-    piece = rows // pieces
-    waits = []
+    chunk, piece = 24, rows // len(ready)
+    for k in range(HALO):
+        out[k] = current[frames - HALO + k if forward else k]
+    goals = (frames - 2, frames - 1) if forward else (0, 1)
+    for p, wait in enumerate(ready):
+        wait()
+
+        def body(c, carry):
+            at = pl.ds(pl.multiple_of(p * piece + c * chunk, 8), chunk)
+            for k, value in enumerate(goal_rows(coeff, video, multiplier, basis, at, goals)):
+                out[HALO + k, at, :] = value
+            return carry
+
+        lax.fori_loop(0, piece // chunk, body, 0)
+
+
+def first_side_kernel(coeff, video, multiplier, basis_in, current, out, basis, sems):
+    pieces = sems.shape[0]
+    piece = basis.shape[1] // pieces
+    copies = []
     for p in range(pieces):
         at = pl.ds(p * piece, piece)
-        waits.append(pltpu.make_async_copy(basis_in.at[:, at, :], basis.at[:, at, :], sems.at[p]))
-        waits[p].start()
-    for k in range(HALO):
-        up[k] = current[frames - HALO + k]
-        down[k] = current[k]
-    for p in range(pieces):
-        waits[p].wait()
-
-        def body(c, carry):
-            at = pl.ds(pl.multiple_of(p * piece + c * chunk, chunk), chunk)
-            for f, value in enumerate(goal_rows(coeff, video, multiplier, basis, at)):
-                (down if f < 2 else up)[HALO + f % 2, at, :] = value
-            return carry
-
-        lax.fori_loop(0, piece // chunk, body, 0)
-
-
-def strips_kernel(current, up, down, edge, right, left):
-    frames, rows, _ = current.shape
-    sources = [(current, f, HALO * GROUP + GROUP * f, 0, f) for f in range(frames)]
+        copies.append(pltpu.make_async_copy(basis_in.at[:, at, :], basis.at[:, at, :], sems.at[p]))
+        copies[p].start()
+    fill_side(False, coeff, video, multiplier, basis, current, out, [c.wait for c in copies])
+
+
+def second_side_kernel(coeff, video, multiplier, basis, current, out):
+    fill_side(True, coeff, video, multiplier, basis, current, out, [lambda: None])
+
+
+def strips_kernel(up, down, edge, right, left):
+    frames, rows = edge.shape[1], up.shape[1]
+    sources = [(up if f > 0 else down, max(f - 1, 0), HALO * GROUP + GROUP * f, 0, f) for f in range(frames)]
     sources += [
         (down if f < 2 else up, HALO + f % 2, HALO * GROUP + GROUP * (f + frames), 1, f) for f in range(frames)
     ]
@@ -233,7 +244,6 @@
     ridge_part,
     slot_count,
     col_count,
-    place,
     current,
     before,
     after,
@@ -269,7 +279,7 @@
     frames, rows, _ = current.shape
     all_rows = rows + 2 * TOP
     rank = basis.shape[0]
-    row, col, slot = place[0], place[1], place[2]
+    row, col, slot = lax.axis_index("row"), lax.axis_index("col"), lax.axis_index("frame")
     copies = []
 
     def copy(src, dst):
@@ -279,7 +289,8 @@
         return c
 
     own_at = pl.ds(TOP, rows)
-    strip_chunks = [(c, all_rows // 4) for c in range(0, all_rows, all_rows // 4)]
+    strip_chunks = [(0, 80), (80, all_rows // 2 - 80)]
+    strip_chunks += [(all_rows // 2 + c, count) for c, count in strip_chunks]
     first = []
     for half in range(2):
         at = pl.ds(half * 128, 128)
@@ -504,31 +515,30 @@
         precision=HIGHEST,
         preferred_element_type=jnp.float32,
     )
-    cross = jnp.concatenate([total + ridge_part * coeff[...], jnp.zeros((8, 64), jnp.float32)], axis=1)
-    chunk_rows = sent.shape[1]
+    cross = jnp.concatenate([total[0:1] + ridge_part * coeff[...], jnp.zeros((1, 64), jnp.float32)], axis=1)
     owned = rows // slot_count
-    flat = sent.reshape(sent.shape[0] * chunk_rows, 128)
+    chunk_rows = owned * 8 + 1
 
     def pack(j, carry):
         for f in range(frames):
             for half in range(2):
-                flat[pl.ds(j * chunk_rows + half * frames + f, owned, stride=8), :] = residual[
+                sent[pl.ds(j * chunk_rows + half * frames + f, owned, stride=8), :] = residual[
                     half * frames + f, pl.ds(j * owned, owned), :
                 ]
-        sent[j, pl.ds(owned * 8, 8), :] = cross
+        sent[pl.ds(j * chunk_rows + owned * 8, 1), :] = cross
         return carry
 
     done = [done]
     group = slot_count // 4
     for n in range(4):
         lax.fori_loop(n * group, (n + 1) * group, pack, 0)
-        at = pl.ds(n * group, group)
+        at = pl.ds(n * group * chunk_rows, group * chunk_rows)
         done.append(copy(sent.at[at], sent_out.at[at]))
     for c in done:
         c.wait()
 
 
-def gram_kernel(slot, basis, out, old, sums, window):
+def gram_kernel(slot_count, basis, out, old, sums, window):
     rank, rows, _ = basis.shape
     sums[...] = jnp.zeros_like(sums)
 
@@ -541,13 +551,13 @@
         return carry
 
     lax.fori_loop(0, rows // 8, body, 0)
-    owned = old.shape[0]
-    start = pl.multiple_of(slot[0] * owned // 8 * 8, 8)
-    shift = slot[0] * owned - start
-    flat = old.reshape(owned * 2 * rank, 128)
+    owned = rows // slot_count
+    start = pl.multiple_of(lax.axis_index("frame") * owned // 8 * 8, 8)
+    shift = lax.axis_index("frame") * owned - start
+    flat = old.reshape(old.shape[0] * 2 * rank, 128)
     for half in range(2):
         for r in range(rank):
-            window[half * rank + r] = basis[r, pl.ds(start, 16), half * 128 : (half + 1) * 128]
+            window[half * rank + r, 0:16] = basis[r, pl.ds(start, 16), half * 128 : (half + 1) * 128]
             flat[pl.ds(half * rank + r, owned, stride=2 * rank), :] = window[half * rank + r, pl.ds(shift, owned), :]
     ones = jnp.ones((128, 128), jnp.float32)
     for r in range(rank):
@@ -592,8 +602,6 @@
     row_count = lax.axis_size("row")
     col_count = lax.axis_size("col")
     blocks = row_count * col_count
-    frame_slot = lax.axis_index("frame")
-    place = jnp.stack([lax.axis_index("row"), lax.axis_index("col"), frame_slot])
     all_rows = rows + 2 * TOP
     to_next = [(i, i + 1) for i in range(frame_count - 1)]
     to_previous = [(b, a) for a, b in to_next]
@@ -603,33 +611,41 @@
     edge = pl.pallas_call(
         edge_kernel,
         out_shape=floats(2, frames, 8, cols),
-        in_specs=[smem(), smem()] + anywhere(4),
+        in_specs=[smem()] + anywhere(4),
         out_specs=vmem(1)[0],
         scratch_shapes=[pltpu.VMEM((n, 8, cols), jnp.float32) for n in (frames, frames, rank, frames)]
         + [pltpu.SemaphoreType.DMA((4,))],
         name="edge",
-    )(place, coefficients, video, multiplier, basis, foreground)
+    )(coefficients, video, multiplier, basis, foreground)
     edge = lax.ppermute(edge, "row", [(0, 1), (1, 0)])
-    up, down = pl.pallas_call(
-        target_kernel,
-        out_shape=(pltpu.VMEM((HALO + 2, rows, cols), jnp.float32), pltpu.VMEM((HALO + 2, rows, cols), jnp.float32)),
+    down, images = pl.pallas_call(
+        first_side_kernel,
+        out_shape=(pltpu.VMEM((HALO + 2, rows, cols), jnp.float32), pltpu.VMEM(basis.shape, jnp.float32)),
         in_specs=[smem()] + vmem(2) + anywhere(1) + vmem(1),
         out_specs=vmem(2),
-        scratch_shapes=[pltpu.VMEM(basis.shape, jnp.float32), pltpu.SemaphoreType.DMA((6,))],
+        scratch_shapes=[pltpu.SemaphoreType.DMA((6,))],
         compiler_params=SMALL,
-        name="target",
+        name="first_side",
     )(coefficients, *plain, basis, foreground)
-    up, down, edge = lax.optimization_barrier((up, down, edge))
+    up = pl.pallas_call(
+        second_side_kernel,
+        out_shape=pltpu.VMEM((HALO + 2, rows, cols), jnp.float32),
+        in_specs=[smem()] + vmem(4),
+        out_specs=vmem(1)[0],
+        compiler_params=SMALL,
+        name="second_side",
+    )(coefficients, *plain, images, foreground)
+    up, edge = lax.optimization_barrier((up, edge))
     before = lax.ppermute(up, "frame", to_next)
     after = lax.ppermute(down, "frame", to_previous)
     right, left = pl.pallas_call(
         strips_kernel,
         out_shape=(floats(all_rows, 128), floats(all_rows, 128)),
-        in_specs=vmem(4),
+        in_specs=vmem(3),
         out_specs=vmem(2),
         compiler_params=SMALL,
         name="strips",
-    )(foreground, up, down, edge)
+    )(up, down, edge)
     from_left = lax.ppermute(right, "col", to_right)
     from_right = lax.ppermute(left, "col", to_left)
     folded = all_rows // 2
@@ -661,21 +677,20 @@
         video.shape,
         video.shape,
         basis.shape,
-        (2 * frames, rows, 128),
+        (2 * frames, rows + 16, 128),
         video.shape,
-        (frame_count, owned_rows * 8 + 8, 128),
+        (frame_count * (owned_rows * 8 + 1) + 64, 128),
         (frames * rank, 8, 128),
     ]
     shrunk, sent = pl.pallas_call(
         functools.partial(sweep_kernel, pixel_ridge / blocks, frame_count, col_count),
-        out_shape=(in_hbm(frames, rows, cols), in_hbm(frame_count, owned_rows * 8 + 8, 128)),
-        in_specs=[smem()] + anywhere(5) + vmem(3) + anywhere(3) + vmem(1),
+        out_shape=(in_hbm(frames, rows, cols), in_hbm(frame_count * (owned_rows * 8 + 1), 128)),
+        in_specs=anywhere(5) + vmem(3) + anywhere(3) + vmem(1),
         out_specs=anywhere(2),
         scratch_shapes=[pltpu.VMEM(s, jnp.float32) for s in scratch] + [pltpu.SemaphoreType.DMA((22,))],
         compiler_params=LARGE,
         name="sweeps",
     )(
-        place,
         foreground,
         before,
         after,
@@ -689,32 +704,32 @@
         basis,
         coefficients.reshape(1, frames * rank),
     )
-    got = lax.all_to_all(sent, "frame", 0, 0, tiled=True)
+    got = lax.all_to_all(sent.reshape(frame_count, owned_rows * 8 + 1, 1, 128), "frame", 0, 0, tiled=True)
     basis, _ = lax.optimization_barrier((basis, sent))
     gram, old_owned = pl.pallas_call(
-        gram_kernel,
-        out_shape=(floats(rank, 128), floats(owned_rows, 2 * rank, 128)),
-        in_specs=[smem()] + vmem(1),
+        functools.partial(gram_kernel, frame_count),
+        out_shape=(floats(rank, 128), floats(16, 2 * rank, 128)),
+        in_specs=vmem(1),
         out_specs=vmem(2),
         scratch_shapes=[
             pltpu.VMEM((rank * rank, 8, 128), jnp.float32),
-            pltpu.VMEM((2 * rank, 16, 128), jnp.float32),
+            pltpu.VMEM((2 * rank, 24, 128), jnp.float32),
         ],
         compiler_params=SMALL,
         name="gram",
-    )(frame_slot.reshape(1), basis)
-    parts = jnp.concatenate([got[:, owned_rows * 8, :], gram], axis=0)
+    )(basis)
+    parts = jnp.concatenate([got[:, owned_rows * 8, 0, :], gram], axis=0)
     parts = lax.all_to_all(jnp.broadcast_to(parts[None], (blocks, *parts.shape)), ("row", "col"), 0, 0, tiled=True)
     frame_ridge = ridge_share * frames * frame_count
     new_basis, new_coeff = pl.pallas_call(
         functools.partial(final_kernel, pixel_ridge, frame_ridge),
         out_shape=(floats(owned_rows, rank, cols), floats(frames, rank)),
-        in_specs=[smem()] + vmem(3),
+        in_specs=vmem(3),
         out_specs=vmem(2),
-        scratch_shapes=[pltpu.VMEM((frame_count, 128), jnp.float32)],
+        scratch_shapes=[pltpu.VMEM((frame_count + 8, 128), jnp.float32)],
         compiler_params=SMALL,
         name="final",
-    )(frame_slot.reshape(1), got, parts, old_owned)
+    )(got.reshape(-1, 128), parts, old_owned)
     return shrunk, new_coeff, new_basis.transpose(1, 0, 2)
 
 

time: 131 us -> 127 us (0.969)
  waiting for transfers between devices: 38.7 us -> 33.8 us
  Pallas kernels: 39.3 us -> 40.8 us
    ppermute x1, waiting for transfers between devices: 4.86 us -> 1.87 us  [local(): ring_after = lax.ppermute(ring_down, 'frame', to_previous)]
    pallas_call x2 -> x3, Pallas kernels: 11.1 us -> 13 us  [the longest x1 6.15 us: local(): pl.pallas_call(functools.partial(gram_kernel, frame_count), out_shape=(fl...]
    all_to_all x1, waiting for transfers between devices: 27.9 us -> 26.1 us  [local(): lax.all_to_all(sent.reshape(frame_count, owned_rows * 8 + 1, 1, 128), 'fr...]
    ppermute x1, starting transfers between devices: 1.55 us -> 3.11 us  [local(): before = lax.ppermute(up, 'frame', to_next)]
  transfers between devices with their start and end apart: 8 -> 8, of which waited for: 4 -> 4; matrix products, arithmetic and copies ran while one was open for 0% -> 0% of each run, Pallas kernels for 11% -> 13%
where the time goes in v4:
time: 127 us
  Pallas kernels  40.8 us (32%)
  starting transfers between devices  38.2 us (30%)
  waiting for transfers between devices  33.8 us (27%)
  blocking collectives  13.2 us (10%)
    all_to_all x1, waiting for transfers between devices, local(): lax.all_to_all(sent.reshape(frame_count, owned_rows * 8 + 1, 1, 128), 'fr...  26.1 us
    all_to_all x1, starting transfers between devices, local(): lax.all_to_all(sent.reshape(frame_count, owned_rows * 8 + 1, 1, 128), 'fr...  21.8 us
    pallas_call x1, Pallas kernels, local(): pl.pallas_call(functools.partial(sweep_kernel, pixel_ridge / blocks, fram...  16.9 us
    all_to_all x1, blocking collectives, local(): lax.all_to_all(jnp.broadcast_to(parts[None], (blocks, *parts.shape)), ('r...  13.2 us
    pallas_call x1, Pallas kernels, local(): pl.pallas_call(functools.partial(gram_kernel, frame_count), out_shape=(fl...  6.15 us
    pallas_call x1, Pallas kernels, local(): pl.pallas_call(functools.partial(final_kernel, pixel_ridge, frame_ridge),...  4.77 us
    pallas_call x1, Pallas kernels, local(): pl.pallas_call(first_side_kernel, out_shape=(pltpu.VMEM((HALO + 2, rows,...  4.22 us
    ppermute x1, starting transfers between devices, local(): from_left = lax.ppermute(right, 'col', to_right)  3.4 us
  transfers between devices with their start and end apart: 8, of which 4 were waited for; matrix products, arithmetic and copies ran while one was open for 0% of the time, Pallas kernels for 13%

profile of v4, /device:TPU:2, one launch (start us, length us, event | category | flops | bytes accessed | tf_op | source)
XLA Modules:
  0.0 126.9 jit_solution(8764886580274081022)
XLA Ops:
  0.7 0.0 copy-start.2
  0.7 0.0 copy-start.1
  0.7 2.7 %edge.1 = f32[2,4,8,256]{3,2,1,0:T(8,128)} custom-call(f32[4,16]{1,0:T(4,128)} %coeff.5, f32[4,288,256]{2,1,0:T(8,128)} %video.7, f32[4,288,256]{2,1,0:T(8,128)} %multiplier.7, f32[16,288,256]{2,1,0:T(8,128)} %basis.4, f32[4,288,256]{2,1,0:T(8,128)} %current.7), custom_call_target="tpu_custom_call" | custom-call | tf_op jit(solution)/shard_map/edge/pallas_call | solution.py:611
  3.4 3.3 %collective-permute-start = (f32[2,4,8,256]{3,2,1,0:T(8,128)}, f32[2,4,8,256]{3,2,1,0:T(8,128)S(1)}, u32[]{:S(2)}, u32[]{:S(2)}) collective-permute-start(f32[2,4,8,256]{3,2,1,0:T(8,128)} %edge.1), channel_id=1, source_target_pairs={{0,128},{128,0},{1,129},{129,1},{2,130},{130,2},{3,131},{131,3},{4... | collective-permute-start | bytes 196616 | tf_op jit(solution)/shard_map/ppermute | solution.py:620
  6.7 4.2 %first_side.1 = (f32[5,288,256]{2,1,0:T(8,128)}, f32[16,288,256]{2,1,0:T(8,128)S(1)}) custom-call(f32[4,16]{1,0:T(4,128)S(1)} %copy-done.3, f32[4,288,256]{2,1,0:T(8,128)S(1)} %copy-done.1, f32[4,288,256]{2,1,0:T(8,128)S(1)} %copy-done.2, f32[16,288,256]{2,1,0:T(8,128)} %basis.4, f32[4,288,256]{2,1,0:T(8,128)S(1)} %copy-done), custom_call_target="tpu_custom_call" | custom-call | tf_op jit(solution)/shard_map/first_side/pallas_call | solution.py:621
  10.9 1.3 %collective-permute-start.2 = (f32[5,288,256]{2,1,0:T(8,128)}, f32[5,288,256]{2,1,0:T(8,128)}, u32[]{:S(2)}, u32[]{:S(2)}) collective-permute-start(f32[5,288,256]{2,1,0:T(8,128)} %get-tuple-element.21.down), channel_id=1, source_target_pairs={{1,0},{2,1},{3,2},{4,3},{5,4},{6,5},{7,6},{8,7},{9,8},{10,9},{11,1... | collective-permute-start | bytes 4423688 | tf_op jit(solution)/shard_map/ppermute | solution.py:640
  12.2 2.6 %second_side.1.up = f32[5,288,256]{2,1,0:T(8,128)} custom-call(f32[4,16]{1,0:T(4,128)S(1)} %copy-done.3, f32[4,288,256]{2,1,0:T(8,128)S(1)} %copy-done.1, f32[4,288,256]{2,1,0:T(8,128)S(1)} %copy-done.2, f32[16,288,256]{2,1,0:T(8,128)S(1)} %get-tuple-element.19.basis, f32[4,288,256]{2,1,0:T(8,128)S(1)} %copy-done), custom_call_target="tpu_custom_call" | custom-call | tf_op jit(solution)/shard_map/second_side/pallas_call | solution.py:630
  14.8 3.1 %collective-permute-start.1 = (f32[5,288,256]{2,1,0:T(8,128)}, f32[5,288,256]{2,1,0:T(8,128)S(1)}, u32[]{:S(2)}, u32[]{:S(2)}) collective-permute-start(f32[5,288,256]{2,1,0:T(8,128)} %second_side.1.up), channel_id=1, source_target_pairs={{0,1},{1,2},{2,3},{3,4},{4,5},{5,6},{6,7},{7,8},{8,9},{9,10},{10,1... | collective-permute-start | bytes 4423688 | tf_op jit(solution)/shard_map/ppermute | solution.py:639
  18.0 3.1 %strips.1 = (f32[304,128]{1,0:T(8,128)S(1)}, f32[304,128]{1,0:T(8,128)S(1)}) custom-call(f32[5,288,256]{2,1,0:T(8,128)} %second_side.1.up, f32[5,288,256]{2,1,0:T(8,128)} %get-tuple-element.21.down, f32[2,4,8,256]{3,2,1,0:T(8,128)S(1)} %collective-permute-done.edge), custom_call_target="tpu_custom_call" | custom-call | tf_op jit(solution)/shard_map/strips/pallas_call | solution.py:641
  21.1 3.4 %collective-permute-start.3 = (f32[304,128]{1,0:T(8,128)S(1)}, f32[304,128]{1,0:T(8,128)S(1)}, u32[]{:S(2)}, u32[]{:S(2)}) collective-permute-start(f32[304,128]{1,0:T(8,128)S(1)} %get-tuple-element.23.right), channel_id=1, source_target_pairs={{0,32},{32,64},{64,96},{1,33},{33,65},{65,97},{2,34},{34,66},{66,9... | collective-permute-start | bytes 466952 | tf_op jit(solution)/shard_map/ppermute | solution.py:649
  24.5 2.4 %collective-permute-start.4 = (f32[304,128]{1,0:T(8,128)S(1)}, f32[304,128]{1,0:T(8,128)S(1)}, u32[]{:S(2)}, u32[]{:S(2)}) collective-permute-start(f32[304,128]{1,0:T(8,128)S(1)} %get-tuple-element.24.left), channel_id=1, source_target_pairs={{32,0},{64,32},{96,64},{33,1},{65,33},{97,65},{34,2},{66,34},{98,6... | collective-permute-start | bytes 466952 | tf_op jit(solution)/shard_map/ppermute | solution.py:650
  26.9 2.7 %collective-permute-done.3.from_left = f32[304,128]{1,0:T(8,128)S(1)} collective-permute-done((f32[304,128]{1,0:T(8,128)S(1)}, f32[304,128]{1,0:T(8,128)S(1)}, u32[]{:S(2)}, u32[]{:S(2)}) %collective-permute-start.3) | collective-permute-done | bytes 155680 | tf_op jit(solution)/shard_map/ppermute | solution.py:649
  29.6 3.1 %collective-permute-done.4.from_right = f32[304,128]{1,0:T(8,128)S(1)} collective-permute-done((f32[304,128]{1,0:T(8,128)S(1)}, f32[304,128]{1,0:T(8,128)S(1)}, u32[]{:S(2)}, u32[]{:S(2)}) %collective-permute-start.4) | collective-permute-done | bytes 155680 | tf_op jit(solution)/shard_map/ppermute | solution.py:650
  32.7 0.3 ring.1
  33.1 1.6 %collective-permute-start.5 = (f32[232,128]{1,0:T(8,128)S(1)}, f32[232,128]{1,0:T(8,128)S(1)}, u32[]{:S(2)}, u32[]{:S(2)}) collective-permute-start(f32[232,128]{1,0:T(8,128)S(1)} %get-tuple-element.26), channel_id=1, source_target_pairs={{0,1},{1,2},{2,3},{3,4},{4,5},{5,6},{6,7},{7,8},{8,9},{9,10},{10,1... | collective-permute-start | bytes 356360 | tf_op jit(solution)/shard_map/ppermute | solution.py:660
  34.6 1.3 %collective-permute-start.6 = (f32[232,128]{1,0:T(8,128)S(1)}, f32[232,128]{1,0:T(8,128)S(1)}, u32[]{:S(2)}, u32[]{:S(2)}) collective-permute-start(f32[232,128]{1,0:T(8,128)S(1)} %get-tuple-element.27), channel_id=1, source_target_pairs={{1,0},{2,1},{3,2},{4,3},{5,4},{6,5},{7,6},{8,7},{9,8},{10,9},{11,1... | collective-permute-start | bytes 356360 | tf_op jit(solution)/shard_map/ppermute | solution.py:661
  35.9 0.1 reshape.16.coeff
  36.0 1.9 %collective-permute-done.6.ring_after = f32[232,128]{1,0:T(8,128)S(1)} collective-permute-done((f32[232,128]{1,0:T(8,128)S(1)}, f32[232,128]{1,0:T(8,128)S(1)}, u32[]{:S(2)}, u32[]{:S(2)}) %collective-permute-start.6) | collective-permute-done | bytes 118816 | tf_op jit(solution)/shard_map/ppermute | solution.py:661
  37.9 16.9 %sweeps.1 = (f32[4,288,256]{2,1,0:T(8,128)}, f32[2336,128]{1,0:T(8,128)}) custom-call(f32[4,288,256]{2,1,0:T(8,128)S(1)} %copy-done, f32[5,288,256]{2,1,0:T(8,128)S(1)} %collective-permute-done.1.before, f32[5,288,256]{2,1,0:T(8,128)} %collective-permute-done.2.after, f32[5,288,256]{2,1,0:T(8,128)} %second_side.1.up, f32[5,288,256]{2,1,0:T(8,128)} %get-tuple-element.21.down, ...), custom_call_target="tpu_custom_call" | custom-call | tf_op jit(solution)/shard_map/sweeps/pallas_call | solution.py:685
  54.8 21.8 %all-to-all-start = ((f32[32,73,1,128]{3,2,1,0:T(1,128)}), f32[32,73,1,128]{3,2,1,0:T(1,128)S(1)}, u32[]{:S(2)}, u32[]{:S(2)}) async-start(f32[32,73,1,128]{3,2,1,0:T(1,128)} %bitcast.5), calls=%async_computation | async-start | bytes 2392064 | tf_op jit(solution)/shard_map/all_to_all | solution.py:707
  76.7 6.1 %gram.1 = (f32[16,128]{1,0:T(8,128)S(1)}, f32[16,32,128]{2,1,0:T(8,128)S(1)}) custom-call(f32[16,288,256]{2,1,0:T(8,128)} %basis.4), custom_call_target="tpu_custom_call" | custom-call | tf_op jit(solution)/shard_map/gram/pallas_call | solution.py:709
  82.8 26.1 %all-to-all-done = f32[32,73,1,128]{3,2,1,0:T(1,128)S(1)} async-done(((f32[32,73,1,128]{3,2,1,0:T(1,128)}), f32[32,73,1,128]{3,2,1,0:T(1,128)S(1)}, u32[]{:S(2)}, u32[]{:S(2)}) %all-to-all-start) | async-done | bytes 1196064 | tf_op jit(solution)/shard_map/all_to_all | solution.py:707
  108.9 13.2 %all_to_all.10.parts_ref = f32[8,48,128]{2,1,0:T(8,128)S(1)} all-to-all(f32[8,48,128]{2,1,0:T(8,128)S(1)} %broadcast_in_dim.2), channel_id=1, replica_groups=mesh['row'=2,'col'=4,'frame'=32] {'row','col'}, dimensions={0} | all-to-all | bytes 393216 | tf_op jit(solution)/shard_map/all_to_all | solution.py:722
  122.1 4.8 %final.1 = (f32[9,16,256]{2,1,0:T(8,128)}, f32[4,16]{1,0:T(4,128)}) custom-call(f32[2336,128]{1,0:T(8,128)S(1)} %bitcast.4, f32[8,48,128]{2,1,0:T(8,128)S(1)} %all_to_all.10.parts_ref, f32[16,32,128]{2,1,0:T(8,128)S(1)} %get-tuple-element.32.old_ref), custom_call_target="tpu_custom_call" | custom-call | tf_op jit(solution)/shard_map/final/pallas_call | solution.py:724
  (13 shorter events, 0.1 us)
Async XLA Ops:
  0.6 6.0 %copy-start.3 = (f32[4,16]{1,0:T(4,128)S(1)}, f32[4,16]{1,0:T(4,128)}, u32[]{:S(2)}) copy-start(f32[4,16]{1,0:T(4,128)} %coeff.5) | copy-start | bytes 772
  0.6 6.0 %copy-start = (f32[4,288,256]{2,1,0:T(8,128)S(1)}, f32[4,288,256]{2,1,0:T(8,128)}, u32[]{:S(2)}) copy-start(f32[4,288,256]{2,1,0:T(8,128)} %current.7) | copy-start | bytes 3538948
  0.7 6.0 %copy-start.2 = (f32[4,288,256]{2,1,0:T(8,128)S(1)}, f32[4,288,256]{2,1,0:T(8,128)}, u32[]{:S(2)}) copy-start(f32[4,288,256]{2,1,0:T(8,128)} %multiplier.7) | copy-start | bytes 3538948
  0.7 6.0 %copy-start.1 = (f32[4,288,256]{2,1,0:T(8,128)S(1)}, f32[4,288,256]{2,1,0:T(8,128)}, u32[]{:S(2)}) copy-start(f32[4,288,256]{2,1,0:T(8,128)} %video.7) | copy-start | bytes 3538948
  3.4 11.5 %collective-permute-start = (f32[2,4,8,256]{3,2,1,0:T(8,128)}, f32[2,4,8,256]{3,2,1,0:T(8,128)S(1)}, u32[]{:S(2)}, u32[]{:S(2)}) collective-permute-start(f32[2,4,8,256]{3,2,1,0:T(8,128)} %edge.1), channel_id=1, source_target_pairs={{0,128},{128,0},{1,129},{129,1},{2,130},{130,2},{3,131},{131,3},{4... | collective-permute-start | bytes 196616 | tf_op jit(solution)/shard_map/ppermute | solution.py:620
  10.9 27.0 %collective-permute-start.2 = (f32[5,288,256]{2,1,0:T(8,128)}, f32[5,288,256]{2,1,0:T(8,128)}, u32[]{:S(2)}, u32[]{:S(2)}) collective-permute-start(f32[5,288,256]{2,1,0:T(8,128)} %get-tuple-element.21.down), channel_id=1, source_target_pairs={{1,0},{2,1},{3,2},{4,3},{5,4},{6,5},{7,6},{8,7},{9,8},{10,9},{11,1... | collective-permute-start | bytes 4423688 | tf_op jit(solution)/shard_map/ppermute | solution.py:640
  14.8 23.1 %collective-permute-start.1 = (f32[5,288,256]{2,1,0:T(8,128)}, f32[5,288,256]{2,1,0:T(8,128)S(1)}, u32[]{:S(2)}, u32[]{:S(2)}) collective-permute-start(f32[5,288,256]{2,1,0:T(8,128)} %second_side.1.up), channel_id=1, source_target_pairs={{0,1},{1,2},{2,3},{3,4},{4,5},{5,6},{6,7},{7,8},{8,9},{9,10},{10,1... | collective-permute-start | bytes 4423688 | tf_op jit(solution)/shard_map/ppermute | solution.py:639
  21.1 8.5 %collective-permute-start.3 = (f32[304,128]{1,0:T(8,128)S(1)}, f32[304,128]{1,0:T(8,128)S(1)}, u32[]{:S(2)}, u32[]{:S(2)}) collective-permute-start(f32[304,128]{1,0:T(8,128)S(1)} %get-tuple-element.23.right), channel_id=1, source_target_pairs={{0,32},{32,64},{64,96},{1,33},{33,65},{65,97},{2,34},{34,66},{66,9... | collective-permute-start | bytes 466952 | tf_op jit(solution)/shard_map/ppermute | solution.py:649
  24.5 8.3 %collective-permute-start.4 = (f32[304,128]{1,0:T(8,128)S(1)}, f32[304,128]{1,0:T(8,128)S(1)}, u32[]{:S(2)}, u32[]{:S(2)}) collective-permute-start(f32[304,128]{1,0:T(8,128)S(1)} %get-tuple-element.24.left), channel_id=1, source_target_pairs={{32,0},{64,32},{96,64},{33,1},{65,33},{97,65},{34,2},{66,34},{98,6... | collective-permute-start | bytes 466952 | tf_op jit(solution)/shard_map/ppermute | solution.py:650
  33.1 2.9 %collective-permute-start.5 = (f32[232,128]{1,0:T(8,128)S(1)}, f32[232,128]{1,0:T(8,128)S(1)}, u32[]{:S(2)}, u32[]{:S(2)}) collective-permute-start(f32[232,128]{1,0:T(8,128)S(1)} %get-tuple-element.26), channel_id=1, source_target_pairs={{0,1},{1,2},{2,3},{3,4},{4,5},{5,6},{6,7},{7,8},{8,9},{9,10},{10,1... | collective-permute-start | bytes 356360 | tf_op jit(solution)/shard_map/ppermute | solution.py:660
  34.6 3.3 %collective-permute-start.6 = (f32[232,128]{1,0:T(8,128)S(1)}, f32[232,128]{1,0:T(8,128)S(1)}, u32[]{:S(2)}, u32[]{:S(2)}) collective-permute-start(f32[232,128]{1,0:T(8,128)S(1)} %get-tuple-element.27), channel_id=1, source_target_pairs={{1,0},{2,1},{3,2},{4,3},{5,4},{6,5},{7,6},{8,7},{9,8},{10,9},{11,1... | collective-permute-start | bytes 356360 | tf_op jit(solution)/shard_map/ppermute | solution.py:661
  54.8 54.1 %all-to-all-start = ((f32[32,73,1,128]{3,2,1,0:T(1,128)}), f32[32,73,1,128]{3,2,1,0:T(1,128)S(1)}, u32[]{:S(2)}, u32[]{:S(2)}) async-start(f32[32,73,1,128]{3,2,1,0:T(1,128)} %bitcast.5), calls=%async_computation | async-start | bytes 2392064 | tf_op jit(solution)/shard_map/all_to_all | solution.py:707

commit v5 on v4

--- a/solution.py
+++ b/solution.py
@@ -304,7 +304,6 @@
             (after, HALO, 2, goal, 6),
         ):
             first.append(copy(src.at[pl.ds(start, count), :, at], buf.at[pl.ds(at_frame, count), half, own_at, :]))
-    later = [copy(video, own_video), copy(multiplier, own_multiplier), copy(basis, own_basis)]
 
     folded = all_rows // 2
     for c, count in strip_chunks:
@@ -395,9 +394,12 @@
     for half in range(2):
         flux_r[half, 0:8, :] = zero8
     strip_sweep(strip_a, strip_b, 0)
+    strip_sweep(strip_b, strip_a, 1)
+    strip_sweep(strip_a, strip_b, 2)
 
     for c in first:
         c.wait()
+    later = [copy(video, own_video), copy(multiplier, own_multiplier), copy(basis, own_basis)]
 
     chunks = [(c, min(64, all_rows - c)) for c in range(0, all_rows, 64)]
 
@@ -475,9 +477,7 @@
         lax.fori_loop(0, g_count, body, 0)
 
     main_sweep(s_a, s_b, 0, 0, 9)
-    strip_sweep(strip_b, strip_a, 1)
     main_sweep(s_b, s_a, 1, 1, 7)
-    strip_sweep(strip_a, strip_b, 2)
     main_sweep(s_a, s_b, 2, 2, 5)
 
     for c in later:

time: 127 us -> 127 us (level)
  no operation moved by 1% of the time
where the time goes in v5:
time: 127 us; the launch traced here: 126 us
  Pallas kernels  40.3 us (32%)
  starting transfers between devices  38.2 us (30%)
  waiting for transfers between devices  33.8 us (27%)
  blocking collectives  13.2 us (10%)
    all_to_all x1, waiting for transfers between devices, local(): lax.all_to_all(sent.reshape(frame_count, owned_rows * 8 + 1, 1, 128), 'fr...  26.1 us
    all_to_all x1, starting transfers between devices, local(): lax.all_to_all(sent.reshape(frame_count, owned_rows * 8 + 1, 1, 128), 'fr...  21.8 us
    pallas_call x1, Pallas kernels, local(): pl.pallas_call(functools.partial(sweep_kernel, pixel_ridge / blocks, fram...  16.4 us
    all_to_all x1, blocking collectives, local(): lax.all_to_all(jnp.broadcast_to(parts[None], (blocks, *parts.shape)), ('r...  13.2 us
    pallas_call x1, Pallas kernels, local(): pl.pallas_call(functools.partial(gram_kernel, frame_count), out_shape=(fl...  6.15 us
    pallas_call x1, Pallas kernels, local(): pl.pallas_call(functools.partial(final_kernel, pixel_ridge, frame_ridge),...  4.77 us
    pallas_call x1, Pallas kernels, local(): pl.pallas_call(first_side_kernel, out_shape=(pltpu.VMEM((HALO + 2, rows,...  4.22 us
    ppermute x1, starting transfers between devices, local(): from_left = lax.ppermute(right, 'col', to_right)  3.4 us
  transfers between devices with their start and end apart: 8, of which 4 were waited for; matrix products, arithmetic and copies ran while one was open for 0% of the time, Pallas kernels for 13%

profile of v5, /device:TPU:2, one launch (start us, length us, event | category | flops | bytes accessed | tf_op | source)
XLA Modules:
  0.0 126.4 jit_solution(17262817885082354528)
XLA Ops:
  0.7 0.0 copy-start.2
  0.7 0.0 copy-start.1
  0.7 2.7 %edge.1 = f32[2,4,8,256]{3,2,1,0:T(8,128)} custom-call(f32[4,16]{1,0:T(4,128)} %coeff.5, f32[4,288,256]{2,1,0:T(8,128)} %video.7, f32[4,288,256]{2,1,0:T(8,128)} %multiplier.7, f32[16,288,256]{2,1,0:T(8,128)} %basis.4, f32[4,288,256]{2,1,0:T(8,128)} %current.7), custom_call_target="tpu_custom_call" | custom-call | tf_op jit(solution)/shard_map/edge/pallas_call | solution.py:611
  3.4 3.3 %collective-permute-start = (f32[2,4,8,256]{3,2,1,0:T(8,128)}, f32[2,4,8,256]{3,2,1,0:T(8,128)S(1)}, u32[]{:S(2)}, u32[]{:S(2)}) collective-permute-start(f32[2,4,8,256]{3,2,1,0:T(8,128)} %edge.1), channel_id=1, source_target_pairs={{0,128},{128,0},{1,129},{129,1},{2,130},{130,2},{3,131},{131,3},{4... | collective-permute-start | bytes 196616 | tf_op jit(solution)/shard_map/ppermute | solution.py:620
  6.7 4.2 %first_side.1 = (f32[5,288,256]{2,1,0:T(8,128)}, f32[16,288,256]{2,1,0:T(8,128)S(1)}) custom-call(f32[4,16]{1,0:T(4,128)S(1)} %copy-done.3, f32[4,288,256]{2,1,0:T(8,128)S(1)} %copy-done.1, f32[4,288,256]{2,1,0:T(8,128)S(1)} %copy-done.2, f32[16,288,256]{2,1,0:T(8,128)} %basis.4, f32[4,288,256]{2,1,0:T(8,128)S(1)} %copy-done), custom_call_target="tpu_custom_call" | custom-call | tf_op jit(solution)/shard_map/first_side/pallas_call | solution.py:621
  10.9 1.3 %collective-permute-start.2 = (f32[5,288,256]{2,1,0:T(8,128)}, f32[5,288,256]{2,1,0:T(8,128)}, u32[]{:S(2)}, u32[]{:S(2)}) collective-permute-start(f32[5,288,256]{2,1,0:T(8,128)} %get-tuple-element.21.down), channel_id=1, source_target_pairs={{1,0},{2,1},{3,2},{4,3},{5,4},{6,5},{7,6},{8,7},{9,8},{10,9},{11,1... | collective-permute-start | bytes 4423688 | tf_op jit(solution)/shard_map/ppermute | solution.py:640
  12.2 2.6 %second_side.1.up = f32[5,288,256]{2,1,0:T(8,128)} custom-call(f32[4,16]{1,0:T(4,128)S(1)} %copy-done.3, f32[4,288,256]{2,1,0:T(8,128)S(1)} %copy-done.1, f32[4,288,256]{2,1,0:T(8,128)S(1)} %copy-done.2, f32[16,288,256]{2,1,0:T(8,128)S(1)} %get-tuple-element.19.basis, f32[4,288,256]{2,1,0:T(8,128)S(1)} %copy-done), custom_call_target="tpu_custom_call" | custom-call | tf_op jit(solution)/shard_map/second_side/pallas_call | solution.py:630
  14.8 3.1 %collective-permute-start.1 = (f32[5,288,256]{2,1,0:T(8,128)}, f32[5,288,256]{2,1,0:T(8,128)S(1)}, u32[]{:S(2)}, u32[]{:S(2)}) collective-permute-start(f32[5,288,256]{2,1,0:T(8,128)} %second_side.1.up), channel_id=1, source_target_pairs={{0,1},{1,2},{2,3},{3,4},{4,5},{5,6},{6,7},{7,8},{8,9},{9,10},{10,1... | collective-permute-start | bytes 4423688 | tf_op jit(solution)/shard_map/ppermute | solution.py:639
  18.0 3.1 %strips.1 = (f32[304,128]{1,0:T(8,128)S(1)}, f32[304,128]{1,0:T(8,128)S(1)}) custom-call(f32[5,288,256]{2,1,0:T(8,128)} %second_side.1.up, f32[5,288,256]{2,1,0:T(8,128)} %get-tuple-element.21.down, f32[2,4,8,256]{3,2,1,0:T(8,128)S(1)} %collective-permute-done.edge), custom_call_target="tpu_custom_call" | custom-call | tf_op jit(solution)/shard_map/strips/pallas_call | solution.py:641
  21.1 3.4 %collective-permute-start.3 = (f32[304,128]{1,0:T(8,128)S(1)}, f32[304,128]{1,0:T(8,128)S(1)}, u32[]{:S(2)}, u32[]{:S(2)}) collective-permute-start(f32[304,128]{1,0:T(8,128)S(1)} %get-tuple-element.23.right), channel_id=1, source_target_pairs={{0,32},{32,64},{64,96},{1,33},{33,65},{65,97},{2,34},{34,66},{66,9... | collective-permute-start | bytes 466952 | tf_op jit(solution)/shard_map/ppermute | solution.py:649
  24.5 2.4 %collective-permute-start.4 = (f32[304,128]{1,0:T(8,128)S(1)}, f32[304,128]{1,0:T(8,128)S(1)}, u32[]{:S(2)}, u32[]{:S(2)}) collective-permute-start(f32[304,128]{1,0:T(8,128)S(1)} %get-tuple-element.24.left), channel_id=1, source_target_pairs={{32,0},{64,32},{96,64},{33,1},{65,33},{97,65},{34,2},{66,34},{98,6... | collective-permute-start | bytes 466952 | tf_op jit(solution)/shard_map/ppermute | solution.py:650
  26.9 2.7 %collective-permute-done.3.from_left = f32[304,128]{1,0:T(8,128)S(1)} collective-permute-done((f32[304,128]{1,0:T(8,128)S(1)}, f32[304,128]{1,0:T(8,128)S(1)}, u32[]{:S(2)}, u32[]{:S(2)}) %collective-permute-start.3) | collective-permute-done | bytes 155680 | tf_op jit(solution)/shard_map/ppermute | solution.py:649
  29.6 3.1 %collective-permute-done.4.from_right = f32[304,128]{1,0:T(8,128)S(1)} collective-permute-done((f32[304,128]{1,0:T(8,128)S(1)}, f32[304,128]{1,0:T(8,128)S(1)}, u32[]{:S(2)}, u32[]{:S(2)}) %collective-permute-start.4) | collective-permute-done | bytes 155680 | tf_op jit(solution)/shard_map/ppermute | solution.py:650
  32.7 0.3 ring.1
  33.1 1.6 %collective-permute-start.5 = (f32[232,128]{1,0:T(8,128)S(1)}, f32[232,128]{1,0:T(8,128)S(1)}, u32[]{:S(2)}, u32[]{:S(2)}) collective-permute-start(f32[232,128]{1,0:T(8,128)S(1)} %get-tuple-element.26), channel_id=1, source_target_pairs={{0,1},{1,2},{2,3},{3,4},{4,5},{5,6},{6,7},{7,8},{8,9},{9,10},{10,1... | collective-permute-start | bytes 356360 | tf_op jit(solution)/shard_map/ppermute | solution.py:660
  34.6 1.3 %collective-permute-start.6 = (f32[232,128]{1,0:T(8,128)S(1)}, f32[232,128]{1,0:T(8,128)S(1)}, u32[]{:S(2)}, u32[]{:S(2)}) collective-permute-start(f32[232,128]{1,0:T(8,128)S(1)} %get-tuple-element.27), channel_id=1, source_target_pairs={{1,0},{2,1},{3,2},{4,3},{5,4},{6,5},{7,6},{8,7},{9,8},{10,9},{11,1... | collective-permute-start | bytes 356360 | tf_op jit(solution)/shard_map/ppermute | solution.py:661
  35.9 0.1 reshape.16.coeff
  36.0 1.9 %collective-permute-done.6.ring_after = f32[232,128]{1,0:T(8,128)S(1)} collective-permute-done((f32[232,128]{1,0:T(8,128)S(1)}, f32[232,128]{1,0:T(8,128)S(1)}, u32[]{:S(2)}, u32[]{:S(2)}) %collective-permute-start.6) | collective-permute-done | bytes 118816 | tf_op jit(solution)/shard_map/ppermute | solution.py:661
  37.9 16.4 %sweeps.1 = (f32[4,288,256]{2,1,0:T(8,128)}, f32[2336,128]{1,0:T(8,128)}) custom-call(f32[4,288,256]{2,1,0:T(8,128)S(1)} %copy-done, f32[5,288,256]{2,1,0:T(8,128)S(1)} %collective-permute-done.1.before, f32[5,288,256]{2,1,0:T(8,128)} %collective-permute-done.2.after, f32[5,288,256]{2,1,0:T(8,128)} %second_side.1.up, f32[5,288,256]{2,1,0:T(8,128)} %get-tuple-element.21.down, ...), custom_call_target="tpu_custom_call" | custom-call | tf_op jit(solution)/shard_map/sweeps/pallas_call | solution.py:685
  54.3 21.8 %all-to-all-start = ((f32[32,73,1,128]{3,2,1,0:T(1,128)}), f32[32,73,1,128]{3,2,1,0:T(1,128)S(1)}, u32[]{:S(2)}, u32[]{:S(2)}) async-start(f32[32,73,1,128]{3,2,1,0:T(1,128)} %bitcast.5), calls=%async_computation | async-start | bytes 2392064 | tf_op jit(solution)/shard_map/all_to_all | solution.py:707
  76.2 6.1 %gram.1 = (f32[16,128]{1,0:T(8,128)S(1)}, f32[16,32,128]{2,1,0:T(8,128)S(1)}) custom-call(f32[16,288,256]{2,1,0:T(8,128)} %basis.4), custom_call_target="tpu_custom_call" | custom-call | tf_op jit(solution)/shard_map/gram/pallas_call | solution.py:709
  82.3 26.1 %all-to-all-done = f32[32,73,1,128]{3,2,1,0:T(1,128)S(1)} async-done(((f32[32,73,1,128]{3,2,1,0:T(1,128)}), f32[32,73,1,128]{3,2,1,0:T(1,128)S(1)}, u32[]{:S(2)}, u32[]{:S(2)}) %all-to-all-start) | async-done | bytes 1196064 | tf_op jit(solution)/shard_map/all_to_all | solution.py:707
  108.4 13.2 %all_to_all.10.parts_ref = f32[8,48,128]{2,1,0:T(8,128)S(1)} all-to-all(f32[8,48,128]{2,1,0:T(8,128)S(1)} %broadcast_in_dim.2), channel_id=1, replica_groups=mesh['row'=2,'col'=4,'frame'=32] {'row','col'}, dimensions={0} | all-to-all | bytes 393216 | tf_op jit(solution)/shard_map/all_to_all | solution.py:722
  121.6 4.8 %final.1 = (f32[9,16,256]{2,1,0:T(8,128)}, f32[4,16]{1,0:T(4,128)}) custom-call(f32[2336,128]{1,0:T(8,128)S(1)} %bitcast.4, f32[8,48,128]{2,1,0:T(8,128)S(1)} %all_to_all.10.parts_ref, f32[16,32,128]{2,1,0:T(8,128)S(1)} %get-tuple-element.32.old_ref), custom_call_target="tpu_custom_call" | custom-call | tf_op jit(solution)/shard_map/final/pallas_call | solution.py:724
  (13 shorter events, 0.1 us)
Async XLA Ops:
  0.6 6.0 %copy-start.3 = (f32[4,16]{1,0:T(4,128)S(1)}, f32[4,16]{1,0:T(4,128)}, u32[]{:S(2)}) copy-start(f32[4,16]{1,0:T(4,128)} %coeff.5) | copy-start | bytes 772
  0.6 6.0 %copy-start = (f32[4,288,256]{2,1,0:T(8,128)S(1)}, f32[4,288,256]{2,1,0:T(8,128)}, u32[]{:S(2)}) copy-start(f32[4,288,256]{2,1,0:T(8,128)} %current.7) | copy-start | bytes 3538948
  0.7 6.0 %copy-start.2 = (f32[4,288,256]{2,1,0:T(8,128)S(1)}, f32[4,288,256]{2,1,0:T(8,128)}, u32[]{:S(2)}) copy-start(f32[4,288,256]{2,1,0:T(8,128)} %multiplier.7) | copy-start | bytes 3538948
  0.7 6.0 %copy-start.1 = (f32[4,288,256]{2,1,0:T(8,128)S(1)}, f32[4,288,256]{2,1,0:T(8,128)}, u32[]{:S(2)}) copy-start(f32[4,288,256]{2,1,0:T(8,128)} %video.7) | copy-start | bytes 3538948
  3.4 11.5 %collective-permute-start = (f32[2,4,8,256]{3,2,1,0:T(8,128)}, f32[2,4,8,256]{3,2,1,0:T(8,128)S(1)}, u32[]{:S(2)}, u32[]{:S(2)}) collective-permute-start(f32[2,4,8,256]{3,2,1,0:T(8,128)} %edge.1), channel_id=1, source_target_pairs={{0,128},{128,0},{1,129},{129,1},{2,130},{130,2},{3,131},{131,3},{4... | collective-permute-start | bytes 196616 | tf_op jit(solution)/shard_map/ppermute | solution.py:620
  10.9 27.0 %collective-permute-start.2 = (f32[5,288,256]{2,1,0:T(8,128)}, f32[5,288,256]{2,1,0:T(8,128)}, u32[]{:S(2)}, u32[]{:S(2)}) collective-permute-start(f32[5,288,256]{2,1,0:T(8,128)} %get-tuple-element.21.down), channel_id=1, source_target_pairs={{1,0},{2,1},{3,2},{4,3},{5,4},{6,5},{7,6},{8,7},{9,8},{10,9},{11,1... | collective-permute-start | bytes 4423688 | tf_op jit(solution)/shard_map/ppermute | solution.py:640
  14.8 23.1 %collective-permute-start.1 = (f32[5,288,256]{2,1,0:T(8,128)}, f32[5,288,256]{2,1,0:T(8,128)S(1)}, u32[]{:S(2)}, u32[]{:S(2)}) collective-permute-start(f32[5,288,256]{2,1,0:T(8,128)} %second_side.1.up), channel_id=1, source_target_pairs={{0,1},{1,2},{2,3},{3,4},{4,5},{5,6},{6,7},{7,8},{8,9},{9,10},{10,1... | collective-permute-start | bytes 4423688 | tf_op jit(solution)/shard_map/ppermute | solution.py:639
  21.1 8.5 %collective-permute-start.3 = (f32[304,128]{1,0:T(8,128)S(1)}, f32[304,128]{1,0:T(8,128)S(1)}, u32[]{:S(2)}, u32[]{:S(2)}) collective-permute-start(f32[304,128]{1,0:T(8,128)S(1)} %get-tuple-element.23.right), channel_id=1, source_target_pairs={{0,32},{32,64},{64,96},{1,33},{33,65},{65,97},{2,34},{34,66},{66,9... | collective-permute-start | bytes 466952 | tf_op jit(solution)/shard_map/ppermute | solution.py:649
  24.5 8.3 %collective-permute-start.4 = (f32[304,128]{1,0:T(8,128)S(1)}, f32[304,128]{1,0:T(8,128)S(1)}, u32[]{:S(2)}, u32[]{:S(2)}) collective-permute-start(f32[304,128]{1,0:T(8,128)S(1)} %get-tuple-element.24.left), channel_id=1, source_target_pairs={{32,0},{64,32},{96,64},{33,1},{65,33},{97,65},{34,2},{66,34},{98,6... | collective-permute-start | bytes 466952 | tf_op jit(solution)/shard_map/ppermute | solution.py:650
  33.1 2.9 %collective-permute-start.5 = (f32[232,128]{1,0:T(8,128)S(1)}, f32[232,128]{1,0:T(8,128)S(1)}, u32[]{:S(2)}, u32[]{:S(2)}) collective-permute-start(f32[232,128]{1,0:T(8,128)S(1)} %get-tuple-element.26), channel_id=1, source_target_pairs={{0,1},{1,2},{2,3},{3,4},{4,5},{5,6},{6,7},{7,8},{8,9},{9,10},{10,1... | collective-permute-start | bytes 356360 | tf_op jit(solution)/shard_map/ppermute | solution.py:660
  34.6 3.3 %collective-permute-start.6 = (f32[232,128]{1,0:T(8,128)S(1)}, f32[232,128]{1,0:T(8,128)S(1)}, u32[]{:S(2)}, u32[]{:S(2)}) collective-permute-start(f32[232,128]{1,0:T(8,128)S(1)} %get-tuple-element.27), channel_id=1, source_target_pairs={{1,0},{2,1},{3,2},{4,3},{5,4},{6,5},{7,6},{8,7},{9,8},{10,9},{11,1... | collective-permute-start | bytes 356360 | tf_op jit(solution)/shard_map/ppermute | solution.py:661
  54.3 54.1 %all-to-all-start = ((f32[32,73,1,128]{3,2,1,0:T(1,128)}), f32[32,73,1,128]{3,2,1,0:T(1,128)S(1)}, u32[]{:S(2)}, u32[]{:S(2)}) async-start(f32[32,73,1,128]{3,2,1,0:T(1,128)} %bitcast.5), calls=%async_computation | async-start | bytes 2392064 | tf_op jit(solution)/shard_map/all_to_all | solution.py:707

commit v6 on v5

--- a/solution.py
+++ b/solution.py
@@ -505,8 +505,11 @@
                 sums[f * rank + r] += term[0:8] + term[8:16]
         return carry
 
-    lax.fori_loop(0, rows // 16, finish, 0)
-    done = copy(out, shrunk_out)
+    done, parts = [], 3
+    for n in range(parts):
+        lax.fori_loop(n * rows // 16 // parts, (n + 1) * rows // 16 // parts, finish, 0)
+        at = pl.ds(n * rows // parts, rows // parts)
+        done.append(copy(out.at[:, at, :], shrunk_out.at[:, at, :]))
     lines = jnp.sum(sums[...], axis=1)
     total = lax.dot_general(
         jnp.ones((8, 128), jnp.float32),
@@ -528,7 +531,6 @@
         sent[pl.ds(j * chunk_rows + owned * 8, 1), :] = cross
         return carry
 
-    done = [done]
     group = slot_count // 4
     for n in range(4):
         lax.fori_loop(n * group, (n + 1) * group, pack, 0)
@@ -687,7 +689,7 @@
         out_shape=(in_hbm(frames, rows, cols), in_hbm(frame_count * (owned_rows * 8 + 1), 128)),
         in_specs=anywhere(5) + vmem(3) + anywhere(3) + vmem(1),
         out_specs=anywhere(2),
-        scratch_shapes=[pltpu.VMEM(s, jnp.float32) for s in scratch] + [pltpu.SemaphoreType.DMA((22,))],
+        scratch_shapes=[pltpu.VMEM(s, jnp.float32) for s in scratch] + [pltpu.SemaphoreType.DMA((24,))],
         compiler_params=LARGE,
         name="sweeps",
     )(

time: 127 us -> 127 us (level)
  no operation moved by 1% of the time
where the time goes in v6:
time: 127 us; the launch traced here: 126 us
  Pallas kernels  40.3 us (32%)
  starting transfers between devices  38.2 us (30%)
  waiting for transfers between devices  33.8 us (27%)
  blocking collectives  13.2 us (10%)
    all_to_all x1, waiting for transfers between devices, local(): lax.all_to_all(sent.reshape(frame_count, owned_rows * 8 + 1, 1, 128), 'fr...  26.1 us
    all_to_all x1, starting transfers between devices, local(): lax.all_to_all(sent.reshape(frame_count, owned_rows * 8 + 1, 1, 128), 'fr...  21.8 us
    pallas_call x1, Pallas kernels, local(): pl.pallas_call(functools.partial(sweep_kernel, pixel_ridge / blocks, fram...  16.4 us
    all_to_all x1, blocking collectives, local(): lax.all_to_all(jnp.broadcast_to(parts[None], (blocks, *parts.shape)), ('r...  13.2 us
    pallas_call x1, Pallas kernels, local(): pl.pallas_call(functools.partial(gram_kernel, frame_count), out_shape=(fl...  6.15 us
    pallas_call x1, Pallas kernels, local(): pl.pallas_call(functools.partial(final_kernel, pixel_ridge, frame_ridge),...  4.73 us
    pallas_call x1, Pallas kernels, local(): pl.pallas_call(first_side_kernel, out_shape=(pltpu.VMEM((HALO + 2, rows,...  4.22 us
    ppermute x1, starting transfers between devices, local(): from_left = lax.ppermute(right, 'col', to_right)  3.4 us
  transfers between devices with their start and end apart: 8, of which 4 were waited for; matrix products, arithmetic and copies ran while one was open for 0% of the time, Pallas kernels for 13%

profile of v6, /device:TPU:2, one launch (start us, length us, event | category | flops | bytes accessed | tf_op | source)
XLA Modules:
  0.0 126.4 jit_solution(2600190384709460811)
XLA Ops:
  0.7 0.0 copy-start.2
  0.7 0.0 copy-start.1
  0.7 2.7 %edge.1 = f32[2,4,8,256]{3,2,1,0:T(8,128)} custom-call(f32[4,16]{1,0:T(4,128)} %coeff.5, f32[4,288,256]{2,1,0:T(8,128)} %video.7, f32[4,288,256]{2,1,0:T(8,128)} %multiplier.7, f32[16,288,256]{2,1,0:T(8,128)} %basis.4, f32[4,288,256]{2,1,0:T(8,128)} %current.7), custom_call_target="tpu_custom_call" | custom-call | tf_op jit(solution)/shard_map/edge/pallas_call | solution.py:613
  3.4 3.3 %collective-permute-start = (f32[2,4,8,256]{3,2,1,0:T(8,128)}, f32[2,4,8,256]{3,2,1,0:T(8,128)S(1)}, u32[]{:S(2)}, u32[]{:S(2)}) collective-permute-start(f32[2,4,8,256]{3,2,1,0:T(8,128)} %edge.1), channel_id=1, source_target_pairs={{0,128},{128,0},{1,129},{129,1},{2,130},{130,2},{3,131},{131,3},{4... | collective-permute-start | bytes 196616 | tf_op jit(solution)/shard_map/ppermute | solution.py:622
  6.7 4.2 %first_side.1 = (f32[5,288,256]{2,1,0:T(8,128)}, f32[16,288,256]{2,1,0:T(8,128)S(1)}) custom-call(f32[4,16]{1,0:T(4,128)S(1)} %copy-done.3, f32[4,288,256]{2,1,0:T(8,128)S(1)} %copy-done.1, f32[4,288,256]{2,1,0:T(8,128)S(1)} %copy-done.2, f32[16,288,256]{2,1,0:T(8,128)} %basis.4, f32[4,288,256]{2,1,0:T(8,128)S(1)} %copy-done), custom_call_target="tpu_custom_call" | custom-call | tf_op jit(solution)/shard_map/first_side/pallas_call | solution.py:623
  10.9 1.3 %collective-permute-start.2 = (f32[5,288,256]{2,1,0:T(8,128)}, f32[5,288,256]{2,1,0:T(8,128)}, u32[]{:S(2)}, u32[]{:S(2)}) collective-permute-start(f32[5,288,256]{2,1,0:T(8,128)} %get-tuple-element.21.down), channel_id=1, source_target_pairs={{1,0},{2,1},{3,2},{4,3},{5,4},{6,5},{7,6},{8,7},{9,8},{10,9},{11,1... | collective-permute-start | bytes 4423688 | tf_op jit(solution)/shard_map/ppermute | solution.py:642
  12.2 2.6 %second_side.1.up = f32[5,288,256]{2,1,0:T(8,128)} custom-call(f32[4,16]{1,0:T(4,128)S(1)} %copy-done.3, f32[4,288,256]{2,1,0:T(8,128)S(1)} %copy-done.1, f32[4,288,256]{2,1,0:T(8,128)S(1)} %copy-done.2, f32[16,288,256]{2,1,0:T(8,128)S(1)} %get-tuple-element.19.basis, f32[4,288,256]{2,1,0:T(8,128)S(1)} %copy-done), custom_call_target="tpu_custom_call" | custom-call | tf_op jit(solution)/shard_map/second_side/pallas_call | solution.py:632
  14.8 3.1 %collective-permute-start.1 = (f32[5,288,256]{2,1,0:T(8,128)}, f32[5,288,256]{2,1,0:T(8,128)S(1)}, u32[]{:S(2)}, u32[]{:S(2)}) collective-permute-start(f32[5,288,256]{2,1,0:T(8,128)} %second_side.1.up), channel_id=1, source_target_pairs={{0,1},{1,2},{2,3},{3,4},{4,5},{5,6},{6,7},{7,8},{8,9},{9,10},{10,1... | collective-permute-start | bytes 4423688 | tf_op jit(solution)/shard_map/ppermute | solution.py:641
  18.0 3.1 %strips.1 = (f32[304,128]{1,0:T(8,128)S(1)}, f32[304,128]{1,0:T(8,128)S(1)}) custom-call(f32[5,288,256]{2,1,0:T(8,128)} %second_side.1.up, f32[5,288,256]{2,1,0:T(8,128)} %get-tuple-element.21.down, f32[2,4,8,256]{3,2,1,0:T(8,128)S(1)} %collective-permute-done.edge), custom_call_target="tpu_custom_call" | custom-call | tf_op jit(solution)/shard_map/strips/pallas_call | solution.py:643
  21.1 3.4 %collective-permute-start.3 = (f32[304,128]{1,0:T(8,128)S(1)}, f32[304,128]{1,0:T(8,128)S(1)}, u32[]{:S(2)}, u32[]{:S(2)}) collective-permute-start(f32[304,128]{1,0:T(8,128)S(1)} %get-tuple-element.23.right), channel_id=1, source_target_pairs={{0,32},{32,64},{64,96},{1,33},{33,65},{65,97},{2,34},{34,66},{66,9... | collective-permute-start | bytes 466952 | tf_op jit(solution)/shard_map/ppermute | solution.py:651
  24.5 2.4 %collective-permute-start.4 = (f32[304,128]{1,0:T(8,128)S(1)}, f32[304,128]{1,0:T(8,128)S(1)}, u32[]{:S(2)}, u32[]{:S(2)}) collective-permute-start(f32[304,128]{1,0:T(8,128)S(1)} %get-tuple-element.24.left), channel_id=1, source_target_pairs={{32,0},{64,32},{96,64},{33,1},{65,33},{97,65},{34,2},{66,34},{98,6... | collective-permute-start | bytes 466952 | tf_op jit(solution)/shard_map/ppermute | solution.py:652
  26.9 2.7 %collective-permute-done.3.from_left = f32[304,128]{1,0:T(8,128)S(1)} collective-permute-done((f32[304,128]{1,0:T(8,128)S(1)}, f32[304,128]{1,0:T(8,128)S(1)}, u32[]{:S(2)}, u32[]{:S(2)}) %collective-permute-start.3) | collective-permute-done | bytes 155680 | tf_op jit(solution)/shard_map/ppermute | solution.py:651
  29.6 3.1 %collective-permute-done.4.from_right = f32[304,128]{1,0:T(8,128)S(1)} collective-permute-done((f32[304,128]{1,0:T(8,128)S(1)}, f32[304,128]{1,0:T(8,128)S(1)}, u32[]{:S(2)}, u32[]{:S(2)}) %collective-permute-start.4) | collective-permute-done | bytes 155680 | tf_op jit(solution)/shard_map/ppermute | solution.py:652
  32.7 0.3 ring.1
  33.1 1.6 %collective-permute-start.5 = (f32[232,128]{1,0:T(8,128)S(1)}, f32[232,128]{1,0:T(8,128)S(1)}, u32[]{:S(2)}, u32[]{:S(2)}) collective-permute-start(f32[232,128]{1,0:T(8,128)S(1)} %get-tuple-element.26), channel_id=1, source_target_pairs={{0,1},{1,2},{2,3},{3,4},{4,5},{5,6},{6,7},{7,8},{8,9},{9,10},{10,1... | collective-permute-start | bytes 356360 | tf_op jit(solution)/shard_map/ppermute | solution.py:662
  34.6 1.3 %collective-permute-start.6 = (f32[232,128]{1,0:T(8,128)S(1)}, f32[232,128]{1,0:T(8,128)S(1)}, u32[]{:S(2)}, u32[]{:S(2)}) collective-permute-start(f32[232,128]{1,0:T(8,128)S(1)} %get-tuple-element.27), channel_id=1, source_target_pairs={{1,0},{2,1},{3,2},{4,3},{5,4},{6,5},{7,6},{8,7},{9,8},{10,9},{11,1... | collective-permute-start | bytes 356360 | tf_op jit(solution)/shard_map/ppermute | solution.py:663
  35.9 0.1 reshape.16.coeff
  36.0 1.9 %collective-permute-done.6.ring_after = f32[232,128]{1,0:T(8,128)S(1)} collective-permute-done((f32[232,128]{1,0:T(8,128)S(1)}, f32[232,128]{1,0:T(8,128)S(1)}, u32[]{:S(2)}, u32[]{:S(2)}) %collective-permute-start.6) | collective-permute-done | bytes 118816 | tf_op jit(solution)/shard_map/ppermute | solution.py:663
  37.9 16.4 %sweeps.1 = (f32[4,288,256]{2,1,0:T(8,128)}, f32[2336,128]{1,0:T(8,128)}) custom-call(f32[4,288,256]{2,1,0:T(8,128)S(1)} %copy-done, f32[5,288,256]{2,1,0:T(8,128)S(1)} %collective-permute-done.1.before, f32[5,288,256]{2,1,0:T(8,128)} %collective-permute-done.2.after, f32[5,288,256]{2,1,0:T(8,128)} %second_side.1.up, f32[5,288,256]{2,1,0:T(8,128)} %get-tuple-element.21.down, ...), custom_call_target="tpu_custom_call" | custom-call | tf_op jit(solution)/shard_map/sweeps/pallas_call | solution.py:687
  54.3 21.8 %all-to-all-start = ((f32[32,73,1,128]{3,2,1,0:T(1,128)}), f32[32,73,1,128]{3,2,1,0:T(1,128)S(1)}, u32[]{:S(2)}, u32[]{:S(2)}) async-start(f32[32,73,1,128]{3,2,1,0:T(1,128)} %bitcast.5), calls=%async_computation | async-start | bytes 2392064 | tf_op jit(solution)/shard_map/all_to_all | solution.py:709
  76.2 6.1 %gram.1 = (f32[16,128]{1,0:T(8,128)S(1)}, f32[16,32,128]{2,1,0:T(8,128)S(1)}) custom-call(f32[16,288,256]{2,1,0:T(8,128)} %basis.4), custom_call_target="tpu_custom_call" | custom-call | tf_op jit(solution)/shard_map/gram/pallas_call | solution.py:711
  82.3 26.1 %all-to-all-done = f32[32,73,1,128]{3,2,1,0:T(1,128)S(1)} async-done(((f32[32,73,1,128]{3,2,1,0:T(1,128)}), f32[32,73,1,128]{3,2,1,0:T(1,128)S(1)}, u32[]{:S(2)}, u32[]{:S(2)}) %all-to-all-start) | async-done | bytes 1196064 | tf_op jit(solution)/shard_map/all_to_all | solution.py:709
  108.4 13.2 %all_to_all.10.parts_ref = f32[8,48,128]{2,1,0:T(8,128)S(1)} all-to-all(f32[8,48,128]{2,1,0:T(8,128)S(1)} %broadcast_in_dim.2), channel_id=1, replica_groups=mesh['row'=2,'col'=4,'frame'=32] {'row','col'}, dimensions={0} | all-to-all | bytes 393216 | tf_op jit(solution)/shard_map/all_to_all | solution.py:724
  121.6 4.7 %final.1 = (f32[9,16,256]{2,1,0:T(8,128)}, f32[4,16]{1,0:T(4,128)}) custom-call(f32[2336,128]{1,0:T(8,128)S(1)} %bitcast.4, f32[8,48,128]{2,1,0:T(8,128)S(1)} %all_to_all.10.parts_ref, f32[16,32,128]{2,1,0:T(8,128)S(1)} %get-tuple-element.32.old_ref), custom_call_target="tpu_custom_call" | custom-call | tf_op jit(solution)/shard_map/final/pallas_call | solution.py:726
  (13 shorter events, 0.1 us)
Async XLA Ops:
  0.6 6.0 %copy-start.3 = (f32[4,16]{1,0:T(4,128)S(1)}, f32[4,16]{1,0:T(4,128)}, u32[]{:S(2)}) copy-start(f32[4,16]{1,0:T(4,128)} %coeff.5) | copy-start | bytes 772
  0.6 6.0 %copy-start = (f32[4,288,256]{2,1,0:T(8,128)S(1)}, f32[4,288,256]{2,1,0:T(8,128)}, u32[]{:S(2)}) copy-start(f32[4,288,256]{2,1,0:T(8,128)} %current.7) | copy-start | bytes 3538948
  0.7 6.0 %copy-start.2 = (f32[4,288,256]{2,1,0:T(8,128)S(1)}, f32[4,288,256]{2,1,0:T(8,128)}, u32[]{:S(2)}) copy-start(f32[4,288,256]{2,1,0:T(8,128)} %multiplier.7) | copy-start | bytes 3538948
  0.7 6.0 %copy-start.1 = (f32[4,288,256]{2,1,0:T(8,128)S(1)}, f32[4,288,256]{2,1,0:T(8,128)}, u32[]{:S(2)}) copy-start(f32[4,288,256]{2,1,0:T(8,128)} %video.7) | copy-start | bytes 3538948
  3.4 11.5 %collective-permute-start = (f32[2,4,8,256]{3,2,1,0:T(8,128)}, f32[2,4,8,256]{3,2,1,0:T(8,128)S(1)}, u32[]{:S(2)}, u32[]{:S(2)}) collective-permute-start(f32[2,4,8,256]{3,2,1,0:T(8,128)} %edge.1), channel_id=1, source_target_pairs={{0,128},{128,0},{1,129},{129,1},{2,130},{130,2},{3,131},{131,3},{4... | collective-permute-start | bytes 196616 | tf_op jit(solution)/shard_map/ppermute | solution.py:622
  10.9 27.0 %collective-permute-start.2 = (f32[5,288,256]{2,1,0:T(8,128)}, f32[5,288,256]{2,1,0:T(8,128)}, u32[]{:S(2)}, u32[]{:S(2)}) collective-permute-start(f32[5,288,256]{2,1,0:T(8,128)} %get-tuple-element.21.down), channel_id=1, source_target_pairs={{1,0},{2,1},{3,2},{4,3},{5,4},{6,5},{7,6},{8,7},{9,8},{10,9},{11,1... | collective-permute-start | bytes 4423688 | tf_op jit(solution)/shard_map/ppermute | solution.py:642
  14.8 23.1 %collective-permute-start.1 = (f32[5,288,256]{2,1,0:T(8,128)}, f32[5,288,256]{2,1,0:T(8,128)S(1)}, u32[]{:S(2)}, u32[]{:S(2)}) collective-permute-start(f32[5,288,256]{2,1,0:T(8,128)} %second_side.1.up), channel_id=1, source_target_pairs={{0,1},{1,2},{2,3},{3,4},{4,5},{5,6},{6,7},{7,8},{8,9},{9,10},{10,1... | collective-permute-start | bytes 4423688 | tf_op jit(solution)/shard_map/ppermute | solution.py:641
  21.1 8.5 %collective-permute-start.3 = (f32[304,128]{1,0:T(8,128)S(1)}, f32[304,128]{1,0:T(8,128)S(1)}, u32[]{:S(2)}, u32[]{:S(2)}) collective-permute-start(f32[304,128]{1,0:T(8,128)S(1)} %get-tuple-element.23.right), channel_id=1, source_target_pairs={{0,32},{32,64},{64,96},{1,33},{33,65},{65,97},{2,34},{34,66},{66,9... | collective-permute-start | bytes 466952 | tf_op jit(solution)/shard_map/ppermute | solution.py:651
  24.5 8.3 %collective-permute-start.4 = (f32[304,128]{1,0:T(8,128)S(1)}, f32[304,128]{1,0:T(8,128)S(1)}, u32[]{:S(2)}, u32[]{:S(2)}) collective-permute-start(f32[304,128]{1,0:T(8,128)S(1)} %get-tuple-element.24.left), channel_id=1, source_target_pairs={{32,0},{64,32},{96,64},{33,1},{65,33},{97,65},{34,2},{66,34},{98,6... | collective-permute-start | bytes 466952 | tf_op jit(solution)/shard_map/ppermute | solution.py:652
  33.1 2.9 %collective-permute-start.5 = (f32[232,128]{1,0:T(8,128)S(1)}, f32[232,128]{1,0:T(8,128)S(1)}, u32[]{:S(2)}, u32[]{:S(2)}) collective-permute-start(f32[232,128]{1,0:T(8,128)S(1)} %get-tuple-element.26), channel_id=1, source_target_pairs={{0,1},{1,2},{2,3},{3,4},{4,5},{5,6},{6,7},{7,8},{8,9},{9,10},{10,1... | collective-permute-start | bytes 356360 | tf_op jit(solution)/shard_map/ppermute | solution.py:662
  34.6 3.3 %collective-permute-start.6 = (f32[232,128]{1,0:T(8,128)S(1)}, f32[232,128]{1,0:T(8,128)S(1)}, u32[]{:S(2)}, u32[]{:S(2)}) collective-permute-start(f32[232,128]{1,0:T(8,128)S(1)} %get-tuple-element.27), channel_id=1, source_target_pairs={{1,0},{2,1},{3,2},{4,3},{5,4},{6,5},{7,6},{8,7},{9,8},{10,9},{11,1... | collective-permute-start | bytes 356360 | tf_op jit(solution)/shard_map/ppermute | solution.py:663
  54.3 54.1 %all-to-all-start = ((f32[32,73,1,128]{3,2,1,0:T(1,128)}), f32[32,73,1,128]{3,2,1,0:T(1,128)S(1)}, u32[]{:S(2)}, u32[]{:S(2)}) async-start(f32[32,73,1,128]{3,2,1,0:T(1,128)} %bitcast.5), calls=%async_computation | async-start | bytes 2392064 | tf_op jit(solution)/shard_map/all_to_all | solution.py:709
